TPU v7x, 32 devices: a whole 2x2x4 slice. The times are simulated.
32 devices in a mesh: fsdp: 4 (over y, x), ctx: 8 (over z, core).
Axes of the slice: x: 2, y: 2, z: 4, core: 2. Of those that a mesh axis runs over, the one named last changes fastest.
Arguments:
- layer_input: bfloat16 [4, 2048, 2048], P('fsdp', 'ctx'), may hold values from -6 to 6
- lengths: int32 [4], P('fsdp'), may hold values from 1024 to 2048, as said below
- order: int32 [4], P('fsdp'), may hold values from 0 to 3, as said below
- offsets: int32 [4, 16], P('fsdp', 'ctx'), may hold values from 0 to 1920, as said below
- attn_gain: bfloat16 [2048], P(('fsdp', 'ctx')), may hold values from 0.25 to 1.75
- w_query: bfloat16 [2048, 2048], P(('fsdp', 'ctx')), may hold values from -0.125 to 0.125
- w_key: bfloat16 [2048, 1024], P(('fsdp', 'ctx')), may hold values from -0.125 to 0.125
- w_value: bfloat16 [2048, 1024], P(('fsdp', 'ctx')), may hold values from -0.125 to 0.125
- q_gain: bfloat16 [128], P(('fsdp', 'ctx')), may hold values from 1 to 1.796875
- k_gain: bfloat16 [128], P(('fsdp', 'ctx')), may hold values from 1 to 1.796875
- w_out: bfloat16 [2048, 2048], P(('fsdp', 'ctx')), may hold values from -0.75 to 0.75
- mlp_gain: bfloat16 [2048], P(('fsdp', 'ctx')), may hold values from 0.25 to 1.75
- w_gate: bfloat16 [2048, 6144], P(('fsdp', 'ctx')), may hold values from -0.125 to 0.125
- w_up: bfloat16 [2048, 6144], P(('fsdp', 'ctx')), may hold values from -0.125 to 0.125
- w_down: bfloat16 [6144, 2048], P(('fsdp', 'ctx')), may hold values from -0.078125 to 0.078125
- grad_out: bfloat16 [4, 2048, 2048], P('fsdp', 'ctx'), may hold values from -6 to 6
Outputs:
- layer_output: bfloat16 [4, 2048, 2048], P('fsdp', 'ctx')
- grad_x: bfloat16 [4, 2048, 2048], P('fsdp', 'ctx')
- grad_attn_gain: float32 [2048], P(('fsdp', 'ctx'))
- grad_w_query: float32 [2048, 2048], P(('fsdp', 'ctx'))
- grad_w_key: float32 [2048, 1024], P(('fsdp', 'ctx'))
- grad_w_value: float32 [2048, 1024], P(('fsdp', 'ctx'))
- grad_q_gain: float32 [128], P(('fsdp', 'ctx'))
- grad_k_gain: float32 [128], P(('fsdp', 'ctx'))
- grad_w_out: float32 [2048, 2048], P(('fsdp', 'ctx'))
- grad_mlp_gain: float32 [2048], P(('fsdp', 'ctx'))
- grad_w_gate: float32 [2048, 6144], P(('fsdp', 'ctx'))
- grad_w_up: float32 [2048, 6144], P(('fsdp', 'ctx'))
- grad_w_down: float32 [6144, 2048], P(('fsdp', 'ctx'))
Inputs may be any that keep to these rules, and one draw needn't show every extreme that they name: `lengths`: rows at or past a sequence's length are padding; some sequence has exactly 2048 positions and some exactly 1024. `order`: a permutation; entries g * 1 to (g + 1) - 1 name the sequences placed in the group of fsdp index g. For every sequence, ctx index d stores blocks 2d and 2d+1 of 128 rows, with offsets p * 128 and (15 - p) * 128 for a p that differs between the devices of ctx, so each position is stored once.
All inputs are finite; a program needn't handle non-finite values.
Results may differ from a plain program's by a relative error of at most 0.02.
Values may be sent and summed in bfloat16 or wider, within the bound.
A program may use at most 384 MiB of HBM per device.

v0:
```python
import jax
import jax.numpy as jnp
from jax import lax
from jax.sharding import PartitionSpec as P

H = 16
KVH = 8
HD = 128


EPS = 1e-06
THETA = 1000000.0
NEG = -1e30


def for_sending(shard):
    return jax.tree.map(lambda a: a.astype(jnp.bfloat16) if a.dtype == jnp.float32 else a, shard)


def rms_scale(values, gain):
    inverse = lax.rsqrt(jnp.mean(values * values, axis=-1, keepdims=True) + EPS)
    return values * inverse * gain


def rope_tables(positions, width):
    half_width = width // 2
    freqs = THETA ** (-(jnp.arange(half_width, dtype=jnp.float32) * 2.0) / width)
    angles = positions.astype(jnp.float32)[..., None] * freqs
    cosine = jnp.cos(angles)
    sine = jnp.sin(angles)
    return (jnp.concatenate([cosine, cosine], axis=-1), jnp.concatenate([sine, sine], axis=-1))


def rotate(vectors, cosine, sine):
    half_width = vectors.shape[-1] // 2
    turned = jnp.concatenate([-vectors[..., half_width:], vectors[..., :half_width]], axis=-1)
    return vectors * cosine + turned * sine


def head_path(projection, gain, cosine, sine):
    seq_count, row_count, width_all = projection.shape
    split = projection.reshape(seq_count, row_count, width_all // gain.shape[0], gain.shape[0])
    return rotate(rms_scale(split, gain), cosine[:, :, None, :], sine[:, :, None, :])


def times_transpose(left, right):
    return lax.dot_general(
        left, right, (((1,), (1,)), ((), ())), preferred_element_type=jnp.float32
    )


def transpose_times(left, right):
    return lax.dot_general(
        left, right, (((0,), (0,)), ((), ())), preferred_element_type=jnp.float32
    )


def masked_scores(query_one, key_one, query_pos, key_pos, length_one, score_scale):
    row_count = query_one.shape[0]
    queries = query_one.reshape(row_count, KVH, H // KVH, HD)
    raw_scores = jnp.einsum("rkgd,tkd->kgrt", queries, key_one, preferred_element_type=jnp.float32)
    allowed = (key_pos[None, :] <= query_pos[:, None]) & (key_pos[None, :] < length_one)
    return (jnp.where(allowed[None, None], raw_scores * score_scale, NEG), queries)


def per_device(
    layer_input,
    lengths,
    order,
    offsets,
    attn_gain,
    w_query,
    w_key,
    w_value,
    q_gain,
    k_gain,
    w_out,
    mlp_gain,
    w_gate,
    w_up,
    w_down,
    grad_out,
):
    seq_count, row_count, width_all = layer_input.shape
    block_rows = row_count // 2
    score_scale = HD ** (-0.5)
    token_count = seq_count * row_count
    length_sum = jnp.zeros((seq_count,), jnp.int32)
    offset_sum = jnp.zeros(offsets.shape, jnp.int32)
    piece_rows = lax.all_gather(layer_input, "fsdp", axis=0, tiled=True)
    piece_lengths = lax.all_gather(lengths, "fsdp", axis=0, tiled=True)
    piece_offsets = lax.all_gather(offsets, "fsdp", axis=0, tiled=True)
    seq_ids = jnp.arange(piece_lengths.shape[0], dtype=jnp.int32)
    matches = order[:, None] == seq_ids[None, :]
    rows_sum = jnp.einsum(
        "sn,nrd->srd", matches.astype(jnp.bfloat16), piece_rows, preferred_element_type=jnp.float32
    )
    length_sum = length_sum + jnp.sum(jnp.where(matches, piece_lengths[None, :], 0), axis=1)
    offset_sum = offset_sum + jnp.sum(
        jnp.where(matches[:, :, None], piece_offsets[None, :, :], 0), axis=1
    )
    row_index = jnp.arange(row_count, dtype=jnp.int32)
    positions = (
        jnp.where((row_index < block_rows)[None, :], offset_sum[:, 0:1], offset_sum[:, 1:2])
        + row_index % block_rows
    )
    valid = positions < length_sum[:, None]
    cosine, sine = rope_tables(positions, HD)
    attn_set = (
        lax.all_gather(attn_gain, ("fsdp", "ctx"), axis=0, tiled=True),
        lax.all_gather(w_query, ("fsdp", "ctx"), axis=0, tiled=True),
        lax.all_gather(w_key, ("fsdp", "ctx"), axis=0, tiled=True),
        lax.all_gather(w_value, ("fsdp", "ctx"), axis=0, tiled=True),
        lax.all_gather(q_gain, ("fsdp", "ctx"), axis=0, tiled=True),
        lax.all_gather(k_gain, ("fsdp", "ctx"), axis=0, tiled=True),
        lax.all_gather(w_out, ("fsdp", "ctx"), axis=0, tiled=True),
    )
    attn_gain_full = attn_set[0].astype(jnp.float32)
    q_gain_full = attn_set[4].astype(jnp.float32)
    k_gain_full = attn_set[5].astype(jnp.float32)
    flat = rows_sum.reshape(token_count, width_all)
    normed_one = rms_scale(flat, attn_gain_full).astype(jnp.bfloat16)
    query_proj = jnp.dot(normed_one, attn_set[1], preferred_element_type=jnp.float32).reshape(
        seq_count, row_count, -1
    )
    key_proj = jnp.dot(normed_one, attn_set[2], preferred_element_type=jnp.float32).reshape(
        seq_count, row_count, -1
    )
    value_b = (
        jnp.dot(normed_one, attn_set[3], preferred_element_type=jnp.float32)
        .astype(jnp.bfloat16)
        .reshape(seq_count, row_count, -1)
    )
    query_rot = head_path(query_proj, q_gain_full, cosine, sine).astype(jnp.bfloat16)
    key_rot = (
        head_path(key_proj, k_gain_full, cosine, sine)
        .astype(jnp.bfloat16)
        .reshape(seq_count, row_count, -1)
    )
    key_whole, value_whole, key_positions = (
        lax.all_gather(key_rot, "ctx", axis=1, tiled=True),
        lax.all_gather(value_b, "ctx", axis=1, tiled=True),
        lax.all_gather(for_sending(positions), "ctx", axis=1, tiled=True).astype(positions.dtype),
    )
    key_heads = key_whole.reshape(seq_count, -1, KVH, HD)
    value_heads = value_whole.reshape(seq_count, -1, KVH, HD)

    def attend(items):
        query_one, key_one, value_one, query_pos, key_pos, length_one = items
        scores, queries = masked_scores(
            query_one, key_one, query_pos, key_pos, length_one, score_scale
        )
        row_top = jnp.max(scores, axis=-1, keepdims=True)
        exponent = jnp.exp(scores - row_top)
        row_total = jnp.sum(exponent, axis=-1, keepdims=True)
        attn_probs = (exponent / row_total).astype(jnp.bfloat16)
        mixture = jnp.einsum(
            "kgrt,tkd->rkgd", attn_probs, value_one, preferred_element_type=jnp.float32
        )
        return (mixture.reshape(mixture.shape[0], -1), (row_top + jnp.log(row_total))[..., 0])

    attn_mix, log_totals = lax.map(
        attend, (query_rot, key_heads, value_heads, positions, key_positions, length_sum)
    )
    mix_b = attn_mix.reshape(token_count, -1).astype(jnp.bfloat16)
    hidden_res = flat + jnp.dot(mix_b, attn_set[6], preferred_element_type=jnp.float32)
    mlp_set = (
        lax.all_gather(mlp_gain, ("fsdp", "ctx"), axis=0, tiled=True),
        lax.all_gather(w_gate, ("fsdp", "ctx"), axis=0, tiled=True),
        lax.all_gather(w_up, ("fsdp", "ctx"), axis=0, tiled=True),
        lax.all_gather(w_down, ("fsdp", "ctx"), axis=0, tiled=True),
    )
    mlp_gain_full = mlp_set[0].astype(jnp.float32)
    normed_two = rms_scale(hidden_res, mlp_gain_full).astype(jnp.bfloat16)
    gate_proj = jnp.dot(normed_two, mlp_set[1], preferred_element_type=jnp.float32)
    up_proj = jnp.dot(normed_two, mlp_set[2], preferred_element_type=jnp.float32)
    hidden_act = (jax.nn.silu(gate_proj) * up_proj).astype(jnp.bfloat16)
    output = hidden_res + jnp.dot(hidden_act, mlp_set[3], preferred_element_type=jnp.float32)
    result = output.reshape(layer_input.shape).astype(jnp.bfloat16)
    dy_rows = (grad_out.astype(jnp.float32) * valid[:, :, None].astype(jnp.float32)).reshape(
        token_count, width_all
    )
    dy_b = dy_rows.astype(jnp.bfloat16)
    mlp_back = (
        lax.all_gather(mlp_gain, ("fsdp", "ctx"), axis=0, tiled=True),
        lax.all_gather(w_gate, ("fsdp", "ctx"), axis=0, tiled=True),
        lax.all_gather(w_up, ("fsdp", "ctx"), axis=0, tiled=True),
        lax.all_gather(w_down, ("fsdp", "ctx"), axis=0, tiled=True),
    )
    dhid = times_transpose(dy_b, mlp_back[3])
    _, swiglu_pull = jax.vjp(
        lambda gate_in, up_in: jax.nn.silu(gate_in) * up_in, gate_proj, up_proj
    )
    dgate_f, dup_f = swiglu_pull(dhid)
    dgate_b = dgate_f.astype(jnp.bfloat16)
    dup_b = dup_f.astype(jnp.bfloat16)
    dn_two = times_transpose(dgate_b, mlp_back[1]) + times_transpose(dup_b, mlp_back[2])
    _, norm_two_pull = jax.vjp(rms_scale, hidden_res, mlp_gain_full)
    dh_norm, dmlp_gain_part = norm_two_pull(dn_two)
    dh_rows = dy_rows + dh_norm
    grad_down_part = transpose_times(hidden_act, dy_b)
    grad_gate_part = transpose_times(normed_two, dgate_b)
    grad_up_part = transpose_times(normed_two, dup_b)
    grad_mlp_gain, grad_w_gate, grad_w_up, grad_w_down = (
        lax.psum_scatter(dmlp_gain_part, ("fsdp", "ctx"), scatter_dimension=0, tiled=True),
        lax.psum_scatter(grad_gate_part, ("fsdp", "ctx"), scatter_dimension=0, tiled=True),
        lax.psum_scatter(grad_up_part, ("fsdp", "ctx"), scatter_dimension=0, tiled=True),
        lax.psum_scatter(grad_down_part, ("fsdp", "ctx"), scatter_dimension=0, tiled=True),
    )
    attn_back = (
        lax.all_gather(attn_gain, ("fsdp", "ctx"), axis=0, tiled=True),
        lax.all_gather(w_query, ("fsdp", "ctx"), axis=0, tiled=True),
        lax.all_gather(w_key, ("fsdp", "ctx"), axis=0, tiled=True),
        lax.all_gather(w_value, ("fsdp", "ctx"), axis=0, tiled=True),
        lax.all_gather(q_gain, ("fsdp", "ctx"), axis=0, tiled=True),
        lax.all_gather(k_gain, ("fsdp", "ctx"), axis=0, tiled=True),
        lax.all_gather(w_out, ("fsdp", "ctx"), axis=0, tiled=True),
    )
    dattn_b = dh_rows.astype(jnp.bfloat16)
    dmix_b = (
        times_transpose(dattn_b, attn_back[6])
        .astype(jnp.bfloat16)
        .reshape(seq_count, row_count, -1)
    )

    def attend_back(items):
        query_one, key_one, value_one, query_pos, key_pos, length_one, log_one, dmix_one = items
        scores, queries = masked_scores(
            query_one, key_one, query_pos, key_pos, length_one, score_scale
        )
        attn_probs = jnp.exp(scores - log_one[..., None])
        probs_b = attn_probs.astype(jnp.bfloat16)
        dmix_heads = dmix_one.reshape(dmix_one.shape[0], KVH, H // KVH, HD)
        dprob = jnp.einsum(
            "rkgd,tkd->kgrt", dmix_heads, value_one, preferred_element_type=jnp.float32
        )
        delta = jnp.sum(attn_probs * dprob, axis=-1, keepdims=True)
        dscore = (attn_probs * (dprob - delta)).astype(jnp.bfloat16)
        dq_part = (
            jnp.einsum("kgrt,tkd->rkgd", dscore, key_one, preferred_element_type=jnp.float32)
            * score_scale
        )
        dk_part = (
            jnp.einsum("kgrt,rkgd->tkd", dscore, queries, preferred_element_type=jnp.float32)
            * score_scale
        )
        dv_part = jnp.einsum(
            "kgrt,rkgd->tkd", probs_b, dmix_heads, preferred_element_type=jnp.float32
        )
        return (
            dq_part.reshape(dq_part.shape[0], -1),
            dk_part.reshape(dk_part.shape[0], -1),
            dv_part.reshape(dv_part.shape[0], -1),
        )

    dq_rot, dk_whole, dv_whole = lax.map(
        attend_back,
        (
            query_rot,
            key_heads,
            value_heads,
            positions,
            key_positions,
            length_sum,
            log_totals,
            dmix_b,
        ),
    )
    dk_rot, dv_local = (
        lax.psum_scatter(dk_whole, "ctx", scatter_dimension=1, tiled=True),
        lax.psum_scatter(dv_whole, "ctx", scatter_dimension=1, tiled=True),
    )
    _, query_pull = jax.vjp(
        lambda projection, gain: head_path(projection, gain, cosine, sine), query_proj, q_gain_full
    )
    dq_proj, dq_gain_part = query_pull(dq_rot.reshape(seq_count, row_count, H, HD))
    _, key_pull = jax.vjp(
        lambda projection, gain: head_path(projection, gain, cosine, sine), key_proj, k_gain_full
    )
    dk_proj, dk_gain_part = key_pull(dk_rot.reshape(seq_count, row_count, KVH, HD))
    dq_b = dq_proj.reshape(token_count, -1).astype(jnp.bfloat16)
    dk_b = dk_proj.reshape(token_count, -1).astype(jnp.bfloat16)
    dv_b = dv_local.reshape(token_count, -1).astype(jnp.bfloat16)
    dn_one = (
        times_transpose(dq_b, attn_back[1])
        + times_transpose(dk_b, attn_back[2])
        + times_transpose(dv_b, attn_back[3])
    )
    _, norm_one_pull = jax.vjp(rms_scale, flat, attn_gain_full)
    dflat_norm, dattn_gain_part = norm_one_pull(dn_one)
    dres_rows = dh_rows + dflat_norm
    grad_out_part = transpose_times(mix_b, dattn_b)
    grad_query_part = transpose_times(normed_one, dq_b)
    grad_key_part = transpose_times(normed_one, dk_b)
    grad_value_part = transpose_times(normed_one, dv_b)
    grad_attn_gain, grad_w_query, grad_w_key, grad_w_value, grad_q_gain, grad_k_gain, grad_w_out = (
        lax.psum_scatter(dattn_gain_part, ("fsdp", "ctx"), scatter_dimension=0, tiled=True),
        lax.psum_scatter(grad_query_part, ("fsdp", "ctx"), scatter_dimension=0, tiled=True),
        lax.psum_scatter(grad_key_part, ("fsdp", "ctx"), scatter_dimension=0, tiled=True),
        lax.psum_scatter(grad_value_part, ("fsdp", "ctx"), scatter_dimension=0, tiled=True),
        lax.psum_scatter(dq_gain_part, ("fsdp", "ctx"), scatter_dimension=0, tiled=True),
        lax.psum_scatter(dk_gain_part, ("fsdp", "ctx"), scatter_dimension=0, tiled=True),
        lax.psum_scatter(grad_out_part, ("fsdp", "ctx"), scatter_dimension=0, tiled=True),
    )
    dres_b = dres_rows.reshape(layer_input.shape).astype(jnp.bfloat16)
    own_ids = lax.axis_index("fsdp") * seq_count + jnp.arange(seq_count, dtype=jnp.int32)
    piece_rows = lax.all_gather(dres_b, "fsdp", axis=0, tiled=True)
    piece_order = lax.all_gather(order, "fsdp", axis=0, tiled=True)
    matches = own_ids[:, None] == piece_order[None, :]
    returned = jnp.einsum(
        "sn,nrd->srd", matches.astype(jnp.bfloat16), piece_rows, preferred_element_type=jnp.float32
    )
    grad_x = returned.astype(jnp.bfloat16)
    return (
        result,
        grad_x,
        grad_attn_gain,
        grad_w_query,
        grad_w_key,
        grad_w_value,
        grad_q_gain,
        grad_k_gain,
        grad_w_out,
        grad_mlp_gain,
        grad_w_gate,
        grad_w_up,
        grad_w_down,
    )


def solution(mesh):
    placed = (
        P("fsdp", "ctx", None),
        P("fsdp"),
        P("fsdp"),
        P("fsdp", "ctx"),
        P(("fsdp", "ctx")),
        P(("fsdp", "ctx"), None),
        P(("fsdp", "ctx"), None),
        P(("fsdp", "ctx"), None),
        P(("fsdp", "ctx")),
        P(("fsdp", "ctx")),
        P(("fsdp", "ctx"), None),
        P(("fsdp", "ctx")),
        P(("fsdp", "ctx"), None),
        P(("fsdp", "ctx"), None),
        P(("fsdp", "ctx"), None),
        P("fsdp", "ctx", None),
    )
    return jax.shard_map(
        per_device,
        mesh=mesh,
        in_specs=placed,
        out_specs=(
            P("fsdp", "ctx", None),
            P("fsdp", "ctx", None),
            P(("fsdp", "ctx")),
            P(("fsdp", "ctx"), None),
            P(("fsdp", "ctx"), None),
            P(("fsdp", "ctx"), None),
            P(("fsdp", "ctx")),
            P(("fsdp", "ctx")),
            P(("fsdp", "ctx"), None),
            P(("fsdp", "ctx")),
            P(("fsdp", "ctx"), None),
            P(("fsdp", "ctx"), None),
            P(("fsdp", "ctx"), None),
        ),
        check_vma=False,
    )
```

profile of v0, /device:TPU:0, one launch (start us, length us, event | category | flops | bytes accessed | tf_op | source)
XLA Modules:
  0.0 3272.2 jit_solution(12367730840271334474)
XLA Ops:
  13.5 43.3 %all-reduce.16 = (bf16[2048]{0:T(1024)(128)(2,1)S(1)}, bf16[128]{0:T(256)(128)(2,1)S(1)}, bf16[128]{0:T(256)(128)(2,1)}, bf16[2048]{0:T(1024)(128)(2,1)}) all-reduce(bf16[2048]{0:T(1024)(128)(2,1)S(1)} %dynamic-update-slice, bf16[128]{0:T(256)(128)(2,1)S(1)} %dynamic-update-slice.2, ...), channel_id=1, replica_groups=mesh['fsdp'=4,'ctx'=8] {'fsdp','ctx'}, use_global_device_ids=true, to_apply=%add.4 | all-reduce | flops 4352 | bytes 17408
  56.8 9.4 all-gather.16.cloned.1.call-done
  66.2 5.5 fusion.15
  74.7 56.1 %all-gather.18.cloned.1.call-done = bf16[2048,1024]{1,0:T(8,128)(2,1)} async-done(((bf16[64,1024]{1,0:T(8,128)(2,1)}), bf16[2048,1024]{1,0:T(8,128)(2,1)}) %all-gather.18.cloned.1.call-update) | async-done | bytes 4194320 | tf_op jit(solution)/shard_map/all_gather | solution.py:113
  130.8 4.2 convolution_convert_fusion.1
  135.1 8.2 all-gather.3
  147.9 46.5 %all-gather.20.cloned.1.call-done = bf16[2048,1024]{1,0:T(8,128)(2,1)} async-done(((bf16[64,1024]{1,0:T(8,128)(2,1)}), bf16[2048,1024]{1,0:T(8,128)(2,1)}) %all-gather.20.cloned.1.call-update) | async-done | bytes 4194320 | tf_op jit(solution)/shard_map/all_gather | solution.py:112
  194.4 3.4 fusion.73
  210.1 7.8 all-reduce.14
  219.3 10.9 all_gather.71
  232.1 1.9 compare_convert_fusion
  234.8 2.3 compare_and_fusion
  237.1 5.1 all-gather.32.cloned.1.call-done
  242.2 5.2 copy.151
  247.5 42.5 %all-gather.34.cloned.1.call-done = bf16[2048,1024]{1,0:T(8,128)(2,1)} async-done(((bf16[256,1024]{1,0:T(8,128)(2,1)}), bf16[2048,1024]{1,0:T(8,128)(2,1)}) %all-gather.34.cloned.1.call-update) | async-done | bytes 4194320 | tf_op jit(solution)/shard_map/all_gather | solution.py:141
  289.9 5.3 copy.157
  295.2 6.9 copy.132
  302.1 66.6 %all-gather.22.cloned.1.call-done = bf16[2048,2048]{1,0:T(8,128)(2,1)} async-done(((bf16[64,2048]{1,0:T(8,128)(2,1)}), bf16[2048,2048]{1,0:T(8,128)(2,1)}) %all-gather.22.cloned.1.call-update) | async-done | bytes 8388624 | tf_op jit(solution)/shard_map/all_gather | solution.py:111
  368.7 6.8 fusion.74
  377.0 2.0 multiply_multiply_fusion
  382.0 13.6 fusion.72
  395.6 13.3 fusion.3
  409.0 24.7 fusion.32
  433.7 13.7 all-gather.24.cloned.1.call-done
  447.4 6.3 multiply_reduce_fusion.5
  455.3 147.8 %all-gather.28.cloned.1.call-done = bf16[2048,6144]{1,0:T(8,128)(2,1)} async-done(((bf16[64,6144]{1,0:T(8,128)(2,1)}), bf16[2048,6144]{1,0:T(8,128)(2,1)}) %all-gather.28.cloned.1.call-update) | async-done | bytes 25165840 | tf_op jit(solution)/shard_map/all_gather | solution.py:170
  603.1 14.2 fusion.76
  617.4 141.1 %all-gather.26.cloned.1.call-done = bf16[2048,6144]{1,0:T(8,128)(2,1)} async-done(((bf16[64,6144]{1,0:T(8,128)(2,1)}), bf16[2048,6144]{1,0:T(8,128)(2,1)}) %all-gather.26.cloned.1.call-update) | async-done | bytes 25165840 | tf_op jit(solution)/shard_map/all_gather | solution.py:169
  758.4 14.2 fusion.75
  772.7 140.9 %all-gather.30.cloned.1.call-done = bf16[6144,2048]{1,0:T(8,128)(2,1)} async-done(((bf16[192,2048]{1,0:T(8,128)(2,1)}), bf16[6144,2048]{1,0:T(8,128)(2,1)}) %all-gather.30.cloned.1.call-update) | async-done | bytes 25165840 | tf_op jit(solution)/shard_map/all_gather | solution.py:171
  913.6 19.8 multiply_convert_fusion
  933.4 13.7 fusion.77
  947.1 15.3 multiply_reduce_fusion
  962.4 2.2 fusion.22
  966.0 5.7 convolution_convert_fusion
  972.3 23.6 fusion
  995.9 27.7 fusion.2
  1023.7 14.6 bitcast_multiply_fusion.1
  1038.3 17.9 fusion.5
  1056.4 9.6 convolution_multiply_fusion
  1071.0 7.2 fusion.78
  1078.3 47.9 %reduce-scatter.10.cloned.1.call-done = f32[1,256,1024]{1,2,0:T(8,128)} async-done(((f32[1,2048,1024]{1,2,0:T(8,128)}), f32[1,256,1024]{1,2,0:T(8,128)}) %reduce-scatter.10.cloned.1.call-update) | async-done | bytes 1048592 | tf_op jit(solution)/shard_map/reduce_scatter | solution.py:270
  1132.3 5.3 convolution_add_fusion.3
  1137.6 78.7 %reduce-scatter.12.cloned.1.call-done = f32[1,256,1024]{1,2,0:T(8,128)} async-done(((f32[1,2048,1024]{1,2,0:T(8,128)}), f32[1,256,1024]{1,2,0:T(8,128)}) %reduce-scatter.12.cloned.1.call-update) | async-done | bytes 1048592 | tf_op jit(solution)/shard_map/reduce_scatter | solution.py:271
  1216.3 5.6 multiply_reduce_fusion.2
  1222.0 2.6 fusion.25
  1224.7 5.9 fusion.46
  1232.4 9.5 fusion.49
  1242.9 4.6 fusion.43
  1248.7 8.2 fusion.79
  1257.0 1.8 copy-done.25
  1258.8 20.6 fusion.54
  1280.7 21.5 fusion.81
  1302.5 21.7 fusion.80
  1325.8 13.5 fusion.21
  1339.3 40.3 %all-reduce.15 = (f32[2048]{0:T(1024)S(1)}, f32[128]{0:T(128)S(1)}, f32[128]{0:T(128)S(1)}, f32[2048]{0:T(1024)S(1)}) all-reduce(f32[2048]{0:T(1024)S(1)} %get-tuple-element.68, f32[128]{0:T(128)S(1)} %copy-done.61, f32[128]{0:T(128)S(1)} %copy-done.62, f32[2048]{0:T(1024)S(1)} %copy-done.57), channel_id=7, replica_groups=mesh['fsdp'=4,'ctx'=8] {'fsdp','ctx'}, use_global_device_ids=true, to_apply=%region_16.17.clone | all-reduce | flops 4352 | bytes 34816
  1381.9 5.5 fusion.13
  1389.0 43.2 %reduce-scatter.18.cloned.1.call-done = f32[64,1024]{1,0:T(8,128)} async-done(((f32[2048,1024]{1,0:T(8,128)}), f32[64,1024]{1,0:T(8,128)}) %reduce-scatter.18.cloned.1.call-update) | async-done | bytes 262160 | tf_op jit(solution)/shard_map/reduce_scatter | solution.py:300
  1432.2 187.7 %reduce-scatter.20.cloned.1.call-done = f32[64,2048]{1,0:T(8,128)} async-done(((f32[2048,2048]{1,0:T(8,128)}), f32[64,2048]{1,0:T(8,128)}) %reduce-scatter.20.cloned.1.call-update) | async-done | bytes 524304 | tf_op jit(solution)/shard_map/reduce_scatter | solution.py:303
  1619.9 153.9 %reduce-scatter.16.cloned.1.call-done = f32[64,1024]{1,0:T(8,128)} async-done(((f32[2048,1024]{1,0:T(8,128)}), f32[64,1024]{1,0:T(8,128)}) %reduce-scatter.16.cloned.1.call-update) | async-done | bytes 262160 | tf_op jit(solution)/shard_map/reduce_scatter | solution.py:299
  1773.8 187.3 %reduce-scatter.14.cloned.1.call-done = f32[64,2048]{1,0:T(8,128)} async-done(((f32[2048,2048]{1,0:T(8,128)}), f32[64,2048]{1,0:T(8,128)}) %reduce-scatter.14.cloned.1.call-update) | async-done | bytes 524304 | tf_op jit(solution)/shard_map/reduce_scatter | solution.py:298
  1961.1 433.7 %reduce-scatter.26.cloned.1.call-done = f32[192,2048]{1,0:T(8,128)} async-done(((f32[6144,2048]{1,0:T(8,128)}), f32[192,2048]{1,0:T(8,128)}) %reduce-scatter.26.cloned.1.call-update) | async-done | bytes 1572880 | tf_op jit(solution)/shard_map/reduce_scatter | solution.py:208
  2394.8 435.2 %reduce-scatter.24.cloned.1.call-done = f32[64,6144]{1,0:T(8,128)} async-done(((f32[2048,6144]{1,0:T(8,128)}), f32[64,6144]{1,0:T(8,128)}) %reduce-scatter.24.cloned.1.call-update) | async-done | bytes 1572880 | tf_op jit(solution)/shard_map/reduce_scatter | solution.py:207
  2830.0 435.2 %reduce-scatter.22.cloned.1.call-done = f32[64,6144]{1,0:T(8,128)} async-done(((f32[2048,6144]{1,0:T(8,128)}), f32[64,6144]{1,0:T(8,128)}) %reduce-scatter.22.cloned.1.call-update) | async-done | bytes 1572880 | tf_op jit(solution)/shard_map/reduce_scatter | solution.py:206
  (251 shorter events, 58.8 us)
Async XLA Ops:
  7.2 59.0 %all-gather.16.cloned.1.call-start = ((), (), s32[]{:S(2)}) async-start(), calls=%async_computation.9 | async-start | bytes 5242880 | tf_op jit(solution)/shard_map/all_gather | solution.py:90
  7.9 122.9 %all-gather.18.cloned.1.call-start = ((), (), s32[]{:S(2)}) async-start(), calls=%async_computation.10 | async-start | bytes 4325376 | tf_op jit(solution)/shard_map/all_gather | solution.py:113
  8.7 185.7 %all-gather.20.cloned.1.call-start = ((), (), s32[]{:S(2)}) async-start(), calls=%async_computation.11 | async-start | bytes 4325376 | tf_op jit(solution)/shard_map/all_gather | solution.py:112
  9.4 232.8 %all-gather.32.cloned.1.call-start = ((), (), s32[]{:S(2)}) async-start(), calls=%async_computation.26 | async-start | bytes 4718592 | tf_op jit(solution)/shard_map/all_gather | solution.py:142
  56.8 16.3 copy-start.46
  71.7 375.7 %copy-start = (f32[1,256,2048]{2,0,1:T(1,128)}, f32[1,256,2048]{2,0,1:T(1,128)S(1)}, u32[]{:S(2)}) copy-start(f32[1,256,2048]{2,0,1:T(1,128)S(1)} %fusion.15) | copy-start | bytes 6291460
  74.6 119.7 %copy-start.8 = (bf16[256,2048]{1,0:T(8,128)(2,1)}, bf16[256,2048]{1,0:T(8,128)(2,1)S(1)}, u32[]{:S(2)}) copy-start(bf16[256,2048]{1,0:T(8,128)(2,1)S(1)} %multiply_convert_fusion.3) | copy-start | bytes 3145732
  74.7 60.5 %copy-start.63 = (s32[1,2]{1,0:T(1,128)S(1)}, s32[1,2]{1,0:T(1,128)}, u32[]{:S(2)}) copy-start(s32[1,2]{1,0:T(1,128)} %param.19) | copy-start | bytes 28
  135.1 154.9 %all-gather.34.cloned.1.call-start = ((), (), s32[]{:S(2)}) async-start(), calls=%async_computation.27 | async-start | bytes 4718592 | tf_op jit(solution)/shard_map/all_gather | solution.py:141
  143.4 54.4 %copy-start.55 = (f32[128]{0:T(128)}, f32[128]{0:T(128)S(1)}, u32[]{:S(2)}) copy-start(f32[128]{0:T(128)S(1)} %convert_element_type.136) | copy-start | bytes 1540
  145.8 233.6 %copy-start.36 = (f32[256,128]{0,1:T(8,128)}, f32[256,128]{0,1:T(8,128)S(1)}, u32[]{:S(2)}) copy-start(f32[256,128]{0,1:T(8,128)S(1)} %maximum_bitcast_fusion.1) | copy-start | bytes 393220
  146.5 232.8 %copy-start.33 = (f32[256,128]{0,1:T(8,128)}, f32[256,128]{0,1:T(8,128)S(1)}, u32[]{:S(2)}) copy-start(f32[256,128]{0,1:T(8,128)S(1)} %maximum_bitcast_fusion) | copy-start | bytes 393220
  199.0 1.9 copy-start.6
  199.6 1.7 copy-start.31
  203.9 4.1 copy-start.65
  203.9 14.1 copy-start.64
  203.9 14.1 copy-start.60
  203.9 164.8 %all-gather.22.cloned.1.call-start = ((), (), s32[]{:S(2)}) async-start(), calls=%async_computation.12 | async-start | bytes 8650752 | tf_op jit(solution)/shard_map/all_gather | solution.py:111
  204.5 242.9 %all-gather.24.cloned.1.call-start = ((), (), s32[]{:S(2)}) async-start(), calls=%async_computation.13 | async-start | bytes 8650752 | tf_op jit(solution)/shard_map/all_gather | solution.py:116
  205.2 397.9 %all-gather.28.cloned.1.call-start = ((), (), s32[]{:S(2)}) async-start(), calls=%async_computation.15 | async-start | bytes 25952256 | tf_op jit(solution)/shard_map/all_gather | solution.py:170
  206.0 552.4 %all-gather.26.cloned.1.call-start = ((), (), s32[]{:S(2)}) async-start(), calls=%async_computation.14 | async-start | bytes 25952256 | tf_op jit(solution)/shard_map/all_gather | solution.py:169
  206.7 706.8 %all-gather.30.cloned.1.call-start = ((), (), s32[]{:S(2)}) async-start(), calls=%async_computation.16 | async-start | bytes 25952256 | tf_op jit(solution)/shard_map/all_gather | solution.py:171
  207.3 918.8 %reduce-scatter.10.cloned.1.call-start = ((), (), s32[]{:S(2)}) async-start(), calls=%async_computation.17 | async-start | bytes 9437184 | tf_op jit(solution)/shard_map/reduce_scatter | solution.py:270
  217.9 161.4 %copy-start.58 = (f32[128]{0:T(128)}, f32[128]{0:T(128)S(1)}, u32[]{:S(2)}) copy-start(f32[128]{0:T(128)S(1)} %convert_element_type.140) | copy-start | bytes 1540
  295.2 73.5 %copy-start.9 = (bf16[256,2048]{1,0:T(8,128)(2,1)S(1)}, bf16[256,2048]{1,0:T(8,128)(2,1)}, u32[]{:S(2)}) copy-start(bf16[256,2048]{1,0:T(8,128)(2,1)} %copy-done.8) | copy-start | bytes 3145732
  377.0 2.3 copy-start.44
  377.0 2.3 copy-start.42
  379.0 1.7 copy-start.3
  379.3 2.7 copy-start.5
  379.3 2.7 copy-start.22
  382.0 13.6 copy-start.19
  433.6 20.0 copy-start.21
  455.3 303.1 %copy-start.17 = (bf16[256,2048]{1,0:T(8,128)(2,1)}, bf16[256,2048]{1,0:T(8,128)(2,1)S(1)}, u32[]{:S(2)}) copy-start(bf16[256,2048]{1,0:T(8,128)(2,1)S(1)} %multiply_convert_fusion.2) | copy-start | bytes 3145732
  617.4 296.2 %copy-start.26 = (bf16[1,256,2048]{2,1,0:T(8,128)(2,1)S(1)}, bf16[1,256,2048]{2,1,0:T(8,128)(2,1)}, u32[]{:S(2)}) copy-start(bf16[1,256,2048]{2,1,0:T(8,128)(2,1)} %param.31) | copy-start | bytes 3145732
  933.4 13.7 copy-start.15
  995.9 27.7 copy-start.20
  1038.3 178.0 %reduce-scatter.12.cloned.1.call-start = ((), (), s32[]{:S(2)}) async-start(), calls=%async_computation.18 | async-start | bytes 9437184 | tf_op jit(solution)/shard_map/reduce_scatter | solution.py:271
  1056.2 9.8 copy-start.37
  1056.2 325.7 %all-gather.36.cloned.1.call-start = ((), (), s32[]{:S(2)}) async-start(), calls=%async_computation.28 | async-start | bytes 5242880 | tf_op jit(solution)/shard_map/all_gather | solution.py:307
  1066.3 1.7 copy-start.4
  1066.3 1.7 copy-start.34
  1066.3 1.6 copy-start.43
  1071.0 56.8 %copy-start.41 = (f32[256,128]{1,0:T(8,128)S(1)}, f32[256,128]{1,0:T(8,128)}, u32[]{:S(2)}) copy-start(f32[256,128]{1,0:T(8,128)} %copy.106) | copy-start | bytes 393220
  1128.3 2.1 copy-start.49
  1130.5 1.7 copy-start.35
  1132.3 84.0 %copy-start.1 = (f32[1,256,2048]{2,0,1:T(1,128)S(1)}, f32[1,256,2048]{2,0,1:T(1,128)}, u32[]{:S(2)}) copy-start(f32[1,256,2048]{2,0,1:T(1,128)} %copy-done) | copy-start | bytes 6291460
  1132.3 84.0 %copy-start.47 = (f32[2048]{0:T(1024)S(1)}, f32[2048]{0:T(1024)}, u32[]{:S(2)}) copy-start(f32[2048]{0:T(1024)} %copy-done.46) | copy-start | bytes 24580
  1132.3 84.0 %copy-start.51 = (f32[256]{0:T(256)S(1)}, f32[256]{0:T(256)}, u32[]{:S(2)}) copy-start(f32[256]{0:T(256)} %copy-done.50) | copy-start | bytes 3076
  1137.6 84.3 %copy-start.54 = (f32[256]{0:T(256)S(1)}, f32[256]{0:T(256)}, u32[]{:S(2)}) copy-start(f32[256]{0:T(256)} %copy-done.53) | copy-start | bytes 3076
  1216.3 5.6 copy-start.12
  1222.0 2.7 copy-start.10
  1224.6 207.6 %reduce-scatter.18.cloned.1.call-start = ((), (), s32[]{:S(2)}) async-start(), calls=%async_computation.21 | async-start | bytes 8650752 | tf_op jit(solution)/shard_map/reduce_scatter | solution.py:300
  1230.6 1.8 copy-start.13
  1230.6 389.3 %reduce-scatter.20.cloned.1.call-start = ((), (), s32[]{:S(2)}) async-start(), calls=%async_computation.22 | async-start | bytes 17301504 | tf_op jit(solution)/shard_map/reduce_scatter | solution.py:303
  1241.9 531.9 %reduce-scatter.16.cloned.1.call-start = ((), (), s32[]{:S(2)}) async-start(), calls=%async_computation.20 | async-start | bytes 8650752 | tf_op jit(solution)/shard_map/reduce_scatter | solution.py:299
  1247.5 713.5 %reduce-scatter.14.cloned.1.call-start = ((), (), s32[]{:S(2)}) async-start(), calls=%async_computation.19 | async-start | bytes 17301504 | tf_op jit(solution)/shard_map/reduce_scatter | solution.py:298
  1256.9 1.9 copy-start.25
  1257.0 1137.8 %reduce-scatter.26.cloned.1.call-start = ((), (), s32[]{:S(2)}) async-start(), calls=%async_computation.25 | async-start | bytes 51904512 | tf_op jit(solution)/shard_map/reduce_scatter | solution.py:208
  1279.5 1550.5 %reduce-scatter.24.cloned.1.call-start = ((), (), s32[]{:S(2)}) async-start(), calls=%async_computation.24 | async-start | bytes 51904512 | tf_op jit(solution)/shard_map/reduce_scatter | solution.py:207
  1302.3 1962.9 %reduce-scatter.22.cloned.1.call-start = ((), (), s32[]{:S(2)}) async-start(), calls=%async_computation.23 | async-start | bytes 51904512 | tf_op jit(solution)/shard_map/reduce_scatter | solution.py:206
  1325.8 13.5 copy-start.57
  1325.8 13.5 copy-start.61
  1325.8 13.5 copy-start.62
  1325.8 56.1 %copy-start.66 = (s32[4]{0:T(128)S(1)}, s32[4]{0:T(128)}, u32[]{:S(2)}) copy-start(s32[4]{0:T(128)} %get-tuple-element.85) | copy-start | bytes 52
  (23 other events, 27.5 us)
Sparse Core Ops, SparseCore 0:
  9.8 56.3 all-gather.15
  69.2 61.5 all-gather.17
  133.8 60.5 all-gather.19
  196.4 45.7 all-gather.31
  244.2 45.6 all-gather.33
  292.8 75.8 all-gather.21
  371.7 75.6 all-gather.23
  450.4 152.6 all-gather.27
  606.1 152.2 all-gather.25
  761.3 152.2 all-gather.29
  1038.4 87.6 reduce-scatter.9
  1128.3 87.9 reduce-scatter.11
  1224.8 51.0 all-gather.35
  1278.6 153.5 reduce-scatter.17
  1434.9 184.9 reduce-scatter.19
  1622.7 151.0 reduce-scatter.15
  1776.5 184.5 reduce-scatter.13
  1967.9 426.8 reduce-scatter.25
  2401.8 428.1 reduce-scatter.23
  2836.8 428.2 reduce-scatter.21
where the time goes:
time: 3280 us; the launch traced here: 3270 us
  waiting for transfers between devices  2680 us (82%)
  matrix products  342 us (10%)
  blocking collectives  110 us (3%)
  other arithmetic  69.5 us (2%)
  local copies, waits for them, and re-layouts  53.7 us (2%)
    reduce_scatter x1, waiting for transfers between devices, per_device(): lax.psum_scatter(grad_up_part, ('fsdp', 'ctx'), scatter_dimension=0, tile...  435 us
    reduce_scatter x1, waiting for transfers between devices, per_device(): lax.psum_scatter(grad_gate_part, ('fsdp', 'ctx'), scatter_dimension=0, ti...  435 us
    reduce_scatter x1, waiting for transfers between devices, per_device(): lax.psum_scatter(grad_down_part, ('fsdp', 'ctx'), scatter_dimension=0, ti...  434 us
    reduce_scatter x1, waiting for transfers between devices, per_device(): lax.psum_scatter(grad_out_part, ('fsdp', 'ctx'), scatter_dimension=0, til...  188 us
    reduce_scatter x1, waiting for transfers between devices, per_device(): lax.psum_scatter(grad_query_part, ('fsdp', 'ctx'), scatter_dimension=0, t...  187 us
    reduce_scatter x1, waiting for transfers between devices, per_device(): lax.psum_scatter(grad_key_part, ('fsdp', 'ctx'), scatter_dimension=0, til...  154 us
    all_gather x1, waiting for transfers between devices, per_device(): lax.all_gather(w_up, ('fsdp', 'ctx'), axis=0, tiled=True)  148 us
    all_gather x1, waiting for transfers between devices, per_device(): lax.all_gather(w_gate, ('fsdp', 'ctx'), axis=0, tiled=True)  141 us
  transfers between devices with their start and end apart: 20, of which 19 were waited for; matrix products, arithmetic and copies ran while one was open for 10% of the time, Pallas kernels for 0%

commit v1 on v0

v1 whole, which is shorter than its diff:
```python
import functools

import jax
import jax.numpy as jnp
from jax import lax
from jax.sharding import PartitionSpec as P

H = 16
KVH = 8
HD = 128

EPS = 1e-06
THETA = 1000000.0
NEG = -1e30
BF = jnp.bfloat16
F32 = jnp.float32


def rms_scale(values, gain):
    inverse = lax.rsqrt(jnp.mean(values * values, axis=-1, keepdims=True) + EPS)
    return values * inverse * gain


def rope_tables(positions, width):
    half_width = width // 2
    freqs = THETA ** (-(jnp.arange(half_width, dtype=F32) * 2.0) / width)
    angles = positions.astype(F32)[..., None] * freqs
    cosine = jnp.cos(angles)
    sine = jnp.sin(angles)
    return (jnp.concatenate([cosine, cosine], axis=-1), jnp.concatenate([sine, sine], axis=-1))


def rotate(vectors, cosine, sine):
    half_width = vectors.shape[-1] // 2
    turned = jnp.concatenate([-vectors[..., half_width:], vectors[..., :half_width]], axis=-1)
    return vectors * cosine + turned * sine


def head_path(projection, gain, cosine, sine):
    seqs, rows, width_all = projection.shape
    split = projection.reshape(seqs, rows, width_all // HD, HD)
    return rotate(rms_scale(split, gain), cosine[:, :, None, :], sine[:, :, None, :])


def dot_nn(left, right):
    return lax.dot_general(left, right, (((1,), (0,)), ((), ())), preferred_element_type=F32)


def dot_nt(left, right):
    return lax.dot_general(left, right, (((1,), (1,)), ((), ())), preferred_element_type=F32)


def dot_tn(left, right):
    return lax.dot_general(left, right, (((0,), (0,)), ((), ())), preferred_element_type=F32)


def swap(block, step, count):
    if step == 0:
        return block
    return lax.ppermute(block, "fsdp", [(i, i ^ step) for i in range(count)])


def pick(stacked, index):
    return lax.dynamic_index_in_dim(stacked, index, 0, keepdims=False)


def per_device(
    layer_input,
    lengths,
    order,
    offsets,
    attn_gain,
    w_query,
    w_key,
    w_value,
    q_gain,
    k_gain,
    w_out,
    mlp_gain,
    w_gate,
    w_up,
    w_down,
    grad_out,
):
    groups, ring = lax.axis_size("fsdp"), lax.axis_size("ctx")
    _, rows, width = layer_input.shape
    block_rows = rows // 2
    heads, kv_heads = H // groups, KVH // groups
    per_key = H // KVH
    q_width, kv_width = heads * HD, kv_heads * HD
    shard_rows = w_query.shape[0]
    hidden = w_gate.shape[1] // groups
    score_scale = HD ** (-0.5)
    own = lax.axis_index("fsdp")
    own_ctx = lax.axis_index("ctx")
    steps = range(groups)
    tokens = groups * rows

    small = jnp.concatenate(
        [
            attn_gain.astype(F32),
            mlp_gain.astype(F32),
            q_gain.astype(F32),
            k_gain.astype(F32),
            lengths.astype(F32),
            order.astype(F32),
            offsets.reshape(-1).astype(F32),
        ]
    )[None, :]
    small_all = lax.all_gather(small, ("fsdp", "ctx"), axis=0, tiled=True)
    gain_rows, head_rows = attn_gain.shape[0], q_gain.shape[0]
    at = 0
    attn_gain_full = small_all[:, at : at + gain_rows].reshape(-1)
    at += gain_rows
    mlp_gain_full = small_all[:, at : at + gain_rows].reshape(-1)
    at += gain_rows
    q_gain_full = small_all[:, at : at + head_rows].reshape(-1)
    at += head_rows
    k_gain_full = small_all[:, at : at + head_rows].reshape(-1)
    at += head_rows
    whole = small_all[:, at:].astype(jnp.int32).reshape(groups, ring, 4)
    lengths_all = whole[:, 0, 0]
    order_all = whole[:, 0, 1]
    offsets_all = whole[:, :, 2:4]
    near = own ^ jnp.arange(groups, dtype=jnp.int32)
    length_of = lengths_all[near]
    row_index = jnp.arange(rows, dtype=jnp.int32)
    key_positions = (
        jnp.where(
            (row_index < block_rows)[None, None, :],
            offsets_all[near][:, :, 0:1],
            offsets_all[near][:, :, 1:2],
        )
        + row_index % block_rows
    )
    positions = lax.dynamic_index_in_dim(key_positions, own_ctx, 1, keepdims=False)
    key_positions = key_positions.reshape(groups, -1)
    valid = positions < length_of[:, None]
    slot_of = jnp.sum(
        jnp.where(order_all[None, :] == near[:, None], jnp.arange(groups, dtype=jnp.int32)[None, :], 0), axis=1
    )
    seq_at = order_all[near]

    def to_columns(parts):
        out = jnp.zeros((groups, shard_rows, sum(p.shape[1] for p in parts) // groups), BF)
        for k in steps:
            piece = jnp.concatenate(
                [
                    lax.dynamic_slice_in_dim(p, (own ^ k) * (p.shape[1] // groups), p.shape[1] // groups, 1)
                    for p in parts
                ],
                axis=1,
            )
            out = lax.dynamic_update_index_in_dim(out, swap(piece, k, groups), own ^ k, 0)
        return out

    def from_columns(grad, widths):
        outs = [jnp.zeros((shard_rows, w * groups), F32) for w in widths]
        for k in steps:
            piece = swap(pick(grad, own ^ k), k, groups).astype(F32)
            at = 0
            for n, w in enumerate(widths):
                outs[n] = lax.dynamic_update_slice_in_dim(outs[n], piece[:, at : at + w], (own ^ k) * w, 1)
                at += w
        return outs

    x_own = layer_input[0]
    qkv_local = to_columns([w_query, w_key, w_value])
    w_qkv = lax.all_gather(qkv_local, "ctx", axis=1, tiled=True).reshape(width, -1)
    x_all = jnp.stack([swap(x_own, k, groups) for k in steps])
    flat = x_all.reshape(tokens, width).astype(F32)
    normed_one = rms_scale(flat, attn_gain_full).astype(BF)
    cosine, sine = rope_tables(positions, HD)
    qkv = dot_nn(normed_one, w_qkv).reshape(groups, rows, -1)
    query_proj = qkv[:, :, :q_width]
    key_proj = qkv[:, :, q_width : q_width + kv_width]
    value_b = qkv[:, :, q_width + kv_width :].astype(BF)
    query_rot = head_path(query_proj, q_gain_full, cosine, sine).astype(BF)
    key_rot = head_path(key_proj, k_gain_full, cosine, sine).astype(BF).reshape(groups, rows, -1)
    kv_all = lax.all_gather(jnp.concatenate([key_rot, value_b], axis=2), "ctx", axis=1, tiled=True)
    w_out_full = lax.all_gather(w_out, "ctx", axis=0, tiled=True)
    gate_up_local = to_columns([w_gate, w_up])
    w_gate_up = lax.all_gather(gate_up_local, "ctx", axis=1, tiled=True).reshape(width, -1)
    w_down_full = lax.all_gather(w_down, "ctx", axis=0, tiled=True)

    queries = query_rot.reshape(groups, rows, kv_heads, per_key, HD)
    keys = kv_all[:, :, :kv_width].reshape(groups, -1, kv_heads, HD)
    values = kv_all[:, :, kv_width:].reshape(groups, -1, kv_heads, HD)
    allowed = (key_positions[:, None, :] <= positions[:, :, None]) & (
        key_positions[:, None, :] < length_of[:, None, None]
    )

    def scores_of():
        raw = jnp.einsum("srkgd,stkd->skgrt", queries, keys, preferred_element_type=F32)
        return jnp.where(allowed[:, None, None], raw * score_scale, NEG)

    scores = scores_of()
    row_top = jnp.max(scores, axis=-1, keepdims=True)
    exponent = jnp.exp(scores - row_top)
    row_total = jnp.sum(exponent, axis=-1, keepdims=True)
    probs = (exponent / row_total).astype(BF)
    mixture = jnp.einsum("skgrt,stkd->srkgd", probs, values, preferred_element_type=F32)
    mix_b = mixture.reshape(tokens, -1).astype(BF)
    log_totals = row_top + jnp.log(row_total)

    attn_part = dot_nn(mix_b, w_out_full).reshape(groups, rows, width)
    hidden_res = x_own.astype(F32) + attn_part[0]
    for k in steps[1:]:
        hidden_res = hidden_res + swap(attn_part[k].astype(BF), k, groups).astype(F32)
    normed_two_own = rms_scale(hidden_res, mlp_gain_full).astype(BF)
    normed_two = jnp.concatenate([swap(normed_two_own, k, groups) for k in steps], axis=0)
    gate_up = dot_nn(normed_two, w_gate_up)
    gate_proj, up_proj = gate_up[:, :hidden], gate_up[:, hidden:]
    hidden_act = (jax.nn.silu(gate_proj) * up_proj).astype(BF)
    out_part = dot_nn(hidden_act, w_down_full).reshape(groups, rows, width)
    out_part = jnp.concatenate([(out_part[:1] + hidden_res[None]).astype(BF), out_part[1:].astype(BF)], axis=0)
    result = pick(out_part, own ^ seq_at[0]).astype(F32)
    for k in steps[1:]:
        result = result + swap(pick(out_part, own ^ seq_at[k]), k, groups).astype(F32)
    result = result.astype(BF)[None]

    dy_slots = jnp.stack([swap(grad_out[0], k, groups) for k in steps])
    dy_b = jnp.concatenate(
        [jnp.where(valid[k][:, None], pick(dy_slots, own ^ slot_of[k]), jnp.zeros((), BF)) for k in steps], axis=0
    )
    dhid = dot_nt(dy_b, w_down_full)
    _, swiglu_pull = jax.vjp(lambda g, u: jax.nn.silu(g) * u, gate_proj, up_proj)
    dgate_f, dup_f = swiglu_pull(dhid)
    dgate_up = jnp.concatenate([dgate_f.astype(BF), dup_f.astype(BF)], axis=1)
    dn_two_part = dot_nt(dgate_up, w_gate_up).reshape(groups, rows, width)
    grad_down = lax.psum_scatter(dot_tn(hidden_act, dy_b).astype(BF), "ctx", scatter_dimension=0, tiled=True)
    dn_two = dn_two_part[0]
    for k in steps[1:]:
        dn_two = dn_two + swap(dn_two_part[k].astype(BF), k, groups).astype(F32)
    _, norm_two_pull = jax.vjp(rms_scale, hidden_res, mlp_gain_full)
    dh_norm, dmlp_gain_part = norm_two_pull(dn_two)
    dh_rows = dy_b[:rows].astype(F32) + dh_norm
    dattn_own = dh_rows.astype(BF)
    dattn_b = jnp.concatenate([swap(dattn_own, k, groups) for k in steps], axis=0)
    grad_gate_up = lax.psum_scatter(
        dot_tn(normed_two, dgate_up).astype(BF).reshape(groups, -1, 2 * hidden),
        "ctx",
        scatter_dimension=1,
        tiled=True,
    )
    dmix_b = dot_nt(dattn_b, w_out_full).astype(BF)
    grad_out_w = lax.psum_scatter(dot_tn(mix_b, dattn_b).astype(BF), "ctx", scatter_dimension=0, tiled=True)

    dmix_heads = dmix_b.reshape(groups, rows, kv_heads, per_key, HD)
    attn_probs = jnp.exp(scores_of() - log_totals)
    probs_b = attn_probs.astype(BF)
    dprob = jnp.einsum("srkgd,stkd->skgrt", dmix_heads, values, preferred_element_type=F32)
    delta = jnp.sum(attn_probs * dprob, axis=-1, keepdims=True)
    dscore = (attn_probs * (dprob - delta)).astype(BF)
    dq_rot = jnp.einsum("skgrt,stkd->srkgd", dscore, keys, preferred_element_type=F32) * score_scale
    dk_part = jnp.einsum("skgrt,srkgd->stkd", dscore, queries, preferred_element_type=F32) * score_scale
    dv_part = jnp.einsum("skgrt,srkgd->stkd", probs_b, dmix_heads, preferred_element_type=F32)
    dkv_part = jnp.concatenate(
        [dk_part.reshape(groups, -1, kv_width).astype(BF), dv_part.reshape(groups, -1, kv_width).astype(BF)], axis=2
    )
    dkv = lax.psum_scatter(dkv_part, "ctx", scatter_dimension=1, tiled=True)
    _, query_pull = jax.vjp(lambda p, g: head_path(p, g, cosine, sine), query_proj, q_gain_full)
    dq_proj, dq_gain_part = query_pull(dq_rot.reshape(groups, rows, heads, HD))
    _, key_pull = jax.vjp(lambda p, g: head_path(p, g, cosine, sine), key_proj, k_gain_full)
    dk_proj, dk_gain_part = key_pull(dkv[:, :, :kv_width].astype(F32).reshape(groups, rows, kv_heads, HD))
    dqkv = jnp.concatenate([dq_proj.astype(BF), dk_proj.astype(BF), dkv[:, :, kv_width:]], axis=2).reshape(tokens, -1)
    dn_one_part = dot_nt(dqkv, w_qkv).reshape(groups, rows, width)
    dn_one = dn_one_part[0]
    for k in steps[1:]:
        dn_one = dn_one + swap(dn_one_part[k].astype(BF), k, groups).astype(F32)
    grad_qkv = lax.psum_scatter(
        dot_tn(normed_one, dqkv).astype(BF).reshape(groups, -1, dqkv.shape[1]),
        "ctx",
        scatter_dimension=1,
        tiled=True,
    )
    _, norm_one_pull = jax.vjp(rms_scale, x_own.astype(F32), attn_gain_full)
    dflat_norm, dattn_gain_part = norm_one_pull(dn_one)
    grad_x = (dh_rows + dflat_norm).astype(BF)[None]

    devices = groups * ring
    gains = jnp.concatenate(
        [
            dattn_gain_part.reshape(devices, -1),
            dmlp_gain_part.reshape(devices, -1),
            dq_gain_part.reshape(devices, -1),
            dk_gain_part.reshape(devices, -1),
        ],
        axis=1,
    )
    gains = lax.psum_scatter(gains, ("fsdp", "ctx"), scatter_dimension=0, tiled=True)[0]
    grad_attn_gain = gains[:gain_rows]
    grad_mlp_gain = gains[gain_rows : 2 * gain_rows]
    grad_q_gain = gains[2 * gain_rows : 2 * gain_rows + head_rows]
    grad_k_gain = gains[2 * gain_rows + head_rows :]
    grad_w_gate, grad_w_up = from_columns(grad_gate_up, [hidden, hidden])
    grad_w_query, grad_w_key, grad_w_value = from_columns(grad_qkv, [q_width, kv_width, kv_width])
    return (
        result,
        grad_x,
        grad_attn_gain,
        grad_w_query,
        grad_w_key,
        grad_w_value,
        grad_q_gain,
        grad_k_gain,
        grad_out_w.astype(F32),
        grad_mlp_gain,
        grad_w_gate,
        grad_w_up,
        grad_down.astype(F32),
    )


def solution(mesh):
    rows = P(("fsdp", "ctx"), None)
    vector = P(("fsdp", "ctx"))
    tokens = P("fsdp", "ctx", None)
    return jax.shard_map(
        per_device,
        mesh=mesh,
        in_specs=(
            tokens,
            P("fsdp"),
            P("fsdp"),
            P("fsdp", "ctx"),
            vector,
            rows,
            rows,
            rows,
            vector,
            vector,
            rows,
            vector,
            rows,
            rows,
            rows,
            tokens,
        ),
        out_specs=(
            tokens,
            tokens,
            vector,
            rows,
            rows,
            rows,
            vector,
            vector,
            rows,
            vector,
            rows,
            rows,
            rows,
        ),
        check_vma=False,
    )
```

time: 3280 us -> 1120 us (0.34)
  waiting for transfers between devices: 2680 us -> 436 us
  matrix products: 342 us -> 234 us
  local copies, waits for them, and re-layouts: 53.7 us -> 108 us
  other arithmetic: 69.5 us -> 123 us
  starting transfers between devices: 1.55 us -> 46.2 us
    reduce_scatter x9 -> x5, waiting for transfers between devices: 2000 us -> 117 us  [the longest x1 53.3 us: per_device(): lax.psum_scatter(dot_tn(normed_two, dgate_up).astype(BF).reshape(groups,...]
    all_gather x11 -> x5, waiting for transfers between devices: 670 us -> 42.2 us  [the longest x1 42.2 us: per_device(): lax.all_gather(jnp.concatenate([key_rot, value_b], axis=2), 'ctx', axis=1...]
    ppermute x0 -> x36, waiting for transfers between devices: none -> 275 us  [swap(): return lax.ppermute(block, 'fsdp', [(i, i ^ step) for i in range(count)])]
    dot_general x28 -> x18, matrix products: 336 us -> 234 us  [the longest x4 53 us: dot_nt(): lax.dot_general(left, right, (((1,), (1,)), ((), ())), preferred_element_...]
    unnamed x3 -> x2, blocking collectives: 91.4 us -> 142 us
    ppermute x0 -> x36, starting transfers between devices: none -> 45.8 us  [swap(): return lax.ppermute(block, 'fsdp', [(i, i ^ step) for i in range(count)])]
  transfers between devices with their start and end apart: 20 -> 46, of which waited for: 19 -> 26; matrix products, arithmetic and copies ran while one was open for 10% -> 24% of each run, Pallas kernels for 0% -> 0%
where the time goes in v1:
time: 1120 us; the launch traced here: 1110 us
  waiting for transfers between devices  436 us (39%)
  matrix products  234 us (21%)
  blocking collectives  142 us (13%)
  other arithmetic  123 us (11%)
  local copies, waits for them, and re-layouts  108 us (10%)
  starting transfers between devices  46.2 us (4%)
  between operations  22.6 us (2%)
    ppermute x36, waiting for transfers between devices, swap(): return lax.ppermute(block, 'fsdp', [(i, i ^ step) for i in range(count)])  275 us
    unnamed x2, blocking collectives  142 us
    reduce_scatter x1, waiting for transfers between devices, per_device(): lax.psum_scatter(dot_tn(normed_two, dgate_up).astype(BF).reshape(groups,...  53.3 us
    dot_general x4, matrix products, dot_nt(): lax.dot_general(left, right, (((1,), (1,)), ((), ())), preferred_element_...  53 us
    ppermute x36, starting transfers between devices, swap(): return lax.ppermute(block, 'fsdp', [(i, i ^ step) for i in range(count)])  45.8 us
    dot_general x4, matrix products, dot_tn(): lax.dot_general(left, right, (((0,), (0,)), ((), ())), preferred_element_...  44.4 us
    dot_general x4, matrix products, dot_nn(): lax.dot_general(left, right, (((1,), (0,)), ((), ())), preferred_element_...  43.1 us
    all_gather x1, waiting for transfers between devices, per_device(): lax.all_gather(jnp.concatenate([key_rot, value_b], axis=2), 'ctx', axis=1...  42.2 us
  transfers between devices with their start and end apart: 46, of which 26 were waited for; matrix products, arithmetic and copies ran while one was open for 24% of the time, Pallas kernels for 0%

profile of v1, /device:TPU:0, one launch (start us, length us, event | category | flops | bytes accessed | tf_op | source)
XLA Modules:
  0.0 1111.9 jit_solution(1569155623726878532)
XLA Ops:
  9.2 3.0 collective-permute-start.3
  16.1 4.0 collective-permute-done.4
  26.5 2.8 concatenate.75
  29.5 72.7 %all-reduce.4 = f32[4480]{0:T(1024)S(1)} all-reduce(f32[4480]{0:T(1024)S(1)} %dynamic-update-slice), channel_id=2, replica_groups=mesh['fsdp'=4,'ctx'=8] {'fsdp','ctx'}, use_global_device_ids=true, to_apply=%add.4 | all-reduce | flops 4480 | bytes 35840
  107.1 3.0 mul.536
  112.6 7.7 fusion.24
  131.9 3.0 mul.543
  148.9 7.8 collective-permute-done.12
  156.8 8.5 collective-permute-done.13
  168.4 4.8 compare_and_fusion
  173.2 3.2 slice.352
  182.2 42.2 %all-gather.9.cloned.1.call-done = bf16[4,2048,512]{2,1,0:T(8,128)(2,1)} async-done(((bf16[4,256,512]{2,1,0:T(8,128)(2,1)}), bf16[4,2048,512]{2,1,0:T(8,128)(2,1)}) %all-gather.9.cloned.1.call-update) | async-done | bytes 8388624 | tf_op jit(solution)/shard_map/all_gather | solution.py:180
  224.4 5.8 fusion.87
  230.2 7.0 reshape.464
  237.2 11.2 %copy.221 = bf16[4,2048,2,128,1]{1,3,4,2,0:T(8,128)(2,1)} copy(bf16[4,2048,2,128,1]{3,2,1,0,4:T(2,128)(2,1)} %bitcast.202) | data formatting | bytes 8388608 | tf_op jit(solution)/shard_map/reshape | solution.py:187
  248.5 7.0 reshape.463
  255.5 18.2 %fusion.98 = (f32[4,2,2,256]{3,2,1,0:T(2,128)S(1)}, f32[4,2,2,256,2048]{3,4,2,1,0:T(8,128)}) fusion(bf16[4,2048,2,128,1]{1,3,4,2,0:T(8,128)(2,1)} %copy.221, bf16[4,256,2,2,128]{1,4,3,2,0:T(8,128)(2,1)S(1)} %copy-done.19, pred[4,256,2048]{1,2,0:T(8,128)(4,1)} %compare_and_fusion), kind=kOutput, calls=%fused_computation.273 | convolution fusion | flops 2172645376 | bytes 40910848 | tf_op jit(solution)/shard_map/srkgd,stkd->skgrt/dot_general | solution.py:194
  273.7 13.2 %fusion.3 = f32[4,2,2,256]{3,2,1,0:T(2,128)S(1)} fusion(f32[4,2,2,256,2048]{3,4,2,1,0:T(8,128)} %get-tuple-element.133, f32[4,2,2,256]{3,2,1,0:T(2,128)S(1)} %get-tuple-element.132), kind=kLoop, calls=%fused_computation.12 | loop fusion | flops 16773120 | bytes 33587200 | tf_op jit(solution)/shard_map/reduce_sum | solution.py:200
  286.9 15.7 %fusion.50 = bf16[4,256,2,2,128]{1,4,3,2,0:T(8,128)(2,1)S(1)} fusion(f32[4,2,2,256,2048]{3,4,2,1,0:T(8,128)} %get-tuple-element.133, f32[4,2,2,256]{3,2,1,0:T(2,128)S(1)} %fusion.3, f32[4,2,2,256]{3,2,1,0:T(2,128)S(1)} %get-tuple-element.132, bf16[4,2048,2,128,1]{3,2,1,0,4:T(2,128)(2,1)} %bitcast.199), kind=kOutput, calls=%fused_computation.107 | convolution fusion | flops 2173173760 | bytes 38830080 | tf_op jit(solution)/shard_map/skgrt,stkd->srkgd/dot_general | solution.py:202
  304.1 7.6 fusion.99
  320.3 19.4 %collective-permute-done.6 = bf16[256,2048]{1,0:T(8,128)(2,1)S(1)} collective-permute-done((bf16[256,2048]{1,0:T(8,128)(2,1)}, bf16[256,2048]{1,0:T(8,128)(2,1)S(1)}, u32[]{:S(2)}, u32[]{:S(2)}) %collective-permute-start.6) | collective-permute-done | bytes 1048608 | tf_op jit(solution)/shard_map/ppermute | solution.py:60
  342.2 21.6 %collective-permute-done.7 = bf16[256,2048]{1,0:T(8,128)(2,1)S(1)} collective-permute-done((bf16[256,2048]{1,0:T(8,128)(2,1)}, bf16[256,2048]{1,0:T(8,128)(2,1)S(1)}, u32[]{:S(2)}, u32[]{:S(2)}) %collective-permute-start.7) | collective-permute-done | bytes 1048608 | tf_op jit(solution)/shard_map/ppermute | solution.py:60
  364.7 4.0 multiply_reduce_fusion.4
  371.8 13.0 %collective-permute-done.18 = bf16[256,2048]{1,0:T(8,128)(2,1)} collective-permute-done((bf16[256,2048]{1,0:T(8,128)(2,1)}, bf16[256,2048]{1,0:T(8,128)(2,1)}, u32[]{:S(2)}, u32[]{:S(2)}) %collective-permute-start.18) | collective-permute-done | bytes 1048608 | tf_op jit(solution)/shard_map/ppermute | solution.py:60
  389.6 41.7 %collective-permute-done.19 = bf16[256,2048]{1,0:T(8,128)(2,1)} collective-permute-done((bf16[256,2048]{1,0:T(8,128)(2,1)}, bf16[256,2048]{1,0:T(8,128)(2,1)}, u32[]{:S(2)}, u32[]{:S(2)}) %collective-permute-start.19) | collective-permute-done | bytes 1048608 | tf_op jit(solution)/shard_map/ppermute | solution.py:60
  431.3 2.5 pad_maximum_fusion.4
  435.8 16.9 %collective-permute-done.10 = bf16[256,2048]{1,0:T(8,128)(2,1)} collective-permute-done((bf16[256,2048]{1,0:T(8,128)(2,1)}, bf16[256,2048]{1,0:T(8,128)(2,1)}, u32[]{:S(2)}, u32[]{:S(2)}) %collective-permute-start.10) | collective-permute-done | bytes 1048608 | tf_op jit(solution)/shard_map/ppermute | solution.py:60
  452.7 19.0 %fusion.66 = f32[1024,3072]{1,0:T(8,128)} fusion(bf16[2048,3072]{1,0:T(8,128)(2,1)} %bitcast.216, bf16[256,2048]{1,0:T(8,128)(2,1)} %collective-permute-done.11, bf16[256,2048]{1,0:T(8,128)(2,1)} %collective-permute-done.10, bf16[256,2048]{1,0:T(8,128)(2,1)} %collective-permute-done.9, bf16[256,2048]{1,0:T(8,128)(2,1)} %multiply_convert_fusion.2), kind=kOutput, calls=%fused_computation.139 | convolution fusion | flops 12901679104 | bytes 29360128 | tf_op jit(solution)/shard_map/dot_general | solution.py:46
  471.7 17.8 %fusion.15 = (bf16[1024,1536]{1,0:T(8,128)(2,1)}, bf16[1024,1536]{1,0:T(8,128)(2,1)}, bf16[1024,1536]{1,0:T(8,128)(2,1)}) fusion(f32[1024,3072]{1,0:T(8,128)} %fusion.66, bf16[1536,2048]{1,0:T(8,128)(2,1)} %all-gather.15.cloned.1.call-done, bf16[256,2048]{1,0:T(8,128)(2,1)} %get-tuple-element.47, bf16[256,2048]{1,0:T(8,128)(2,1)} %get-tuple-element.48, ...), kind=kOutput, calls=%fused_computation.37 | convolution fusion | flops 6484393984 | bytes 32505856 | tf_op jit(solution)/shard_map/dot_general | solution.py:50
  489.5 20.8 %fusion.100 = (bf16[1024,2048]{1,0:T(8,128)(2,1)}, f32[1024,2048]{1,0:T(8,128)}) fusion(bf16[2048,3072]{1,0:T(8,128)(2,1)} %bitcast.217, bf16[1024,1536]{1,0:T(8,128)(2,1)} %get-tuple-element.36, bf16[1024,1536]{1,0:T(8,128)(2,1)} %get-tuple-element.35), kind=kOutput, calls=%fused_computation.275 | convolution fusion | flops 12899581952 | bytes 31457280 | tf_op jit(solution)/shard_map/dot_general | solution.py:50
  516.2 22.5 %collective-permute-done.21 = bf16[256,2048]{1,0:T(8,128)(2,1)S(1)} collective-permute-done((bf16[256,2048]{1,0:T(8,128)(2,1)S(1)}, bf16[256,2048]{1,0:T(8,128)(2,1)S(1)}, u32[]{:S(2)}, u32[]{:S(2)}) %collective-permute-start.21) | collective-permute-done | bytes 1048608 | tf_op jit(solution)/shard_map/ppermute | solution.py:60
  538.7 20.0 %collective-permute-done.22 = bf16[256,2048]{1,0:T(8,128)(2,1)S(1)} collective-permute-done((bf16[256,2048]{1,0:T(8,128)(2,1)S(1)}, bf16[256,2048]{1,0:T(8,128)(2,1)S(1)}, u32[]{:S(2)}, u32[]{:S(2)}) %collective-permute-start.22) | collective-permute-done | bytes 1048608 | tf_op jit(solution)/shard_map/ppermute | solution.py:60
  560.2 3.4 multiply_reduce_fusion.1
  568.4 22.5 %collective-permute-done.24 = bf16[256,2048]{1,0:T(8,128)(2,1)S(1)} collective-permute-done((bf16[256,2048]{1,0:T(8,128)(2,1)S(1)}, bf16[256,2048]{1,0:T(8,128)(2,1)S(1)}, u32[]{:S(2)}, u32[]{:S(2)}) %collective-permute-start.24) | collective-permute-done | bytes 1048608 | tf_op jit(solution)/shard_map/ppermute | solution.py:60
  590.9 20.2 %collective-permute-done.25 = bf16[256,2048]{1,0:T(8,128)(2,1)S(1)} collective-permute-done((bf16[256,2048]{1,0:T(8,128)(2,1)S(1)}, bf16[256,2048]{1,0:T(8,128)(2,1)S(1)}, u32[]{:S(2)}, u32[]{:S(2)}) %collective-permute-start.25) | collective-permute-done | bytes 1048608 | tf_op jit(solution)/shard_map/ppermute | solution.py:60
  613.0 5.2 convolution_convert_fusion.3
  619.3 23.7 %fusion = (f32[4,2,2,256]{3,2,1,0:T(2,128)S(1)}, f32[4,2,2048,256,2]{3,2,4,1,0:T(8,128)}) fusion(f32[4,2,2,256,2048]{3,4,2,1,0:T(8,128)} %get-tuple-element.133, f32[4,2,2,256]{3,2,1,0:T(2,128)S(1)} %log_add_fusion, bf16[4,256,2,2,128]{1,4,3,2,0:T(8,128)(2,1)S(1)} %copy.208, bf16[4,2048,2,128,1]{3,2,1,0,4:T(2,128)(2,1)} %bitcast.200), kind=kOutput, calls=%fused_computation.5 | convolution fusion | flops 2172645376 | bytes 72384512 | tf_op jit(solution)/shard_map/srkgd,stkd->skgrt/dot_general | solution.py:252
  643.0 15.6 %bitcast_convert_fusion.1 = bf16[4,2,128,2048]{3,2,1,0:T(8,128)(2,1)} fusion(bf16[4,256,2,2,128]{1,4,3,2,0:T(8,128)(2,1)S(1)} %copy.208, f32[4,2,2,256,2048]{3,4,2,1,0:T(8,128)} %get-tuple-element.133, f32[4,2,2,256]{3,2,1,0:T(2,128)S(1)} %log_add_fusion), kind=kOutput, calls=%fused_computation.26 | convolution fusion | flops 2166358016 | bytes 38813696 | tf_op jit(solution)/shard_map/skgrt,srkgd->stkd/dot_general | solution.py:257
  658.6 27.8 %fusion.2 = bf16[4,2,2,256,2048]{3,4,2,1,0:T(8,128)(2,1)} fusion(f32[4,2,2048,256,2]{3,2,4,1,0:T(8,128)} %get-tuple-element.139, f32[4,2,2,256,2048]{3,4,2,1,0:T(8,128)} %get-tuple-element.133, f32[4,2,2,256]{3,2,1,0:T(2,128)S(1)} %get-tuple-element.138, f32[4,2,2,256]{3,2,1,0:T(2,128)S(1)} %log_add_fusion), kind=kLoop, calls=%fused_computation.7 | loop fusion | flops 33554432 | bytes 83918848 | tf_op jit(solution)/shard_map/convert_element_type | solution.py:254
  686.4 10.7 fusion.12
  697.1 6.3 copy.210
  703.3 6.2 copy.211
  709.6 7.3 pad_maximum_fusion
  718.4 5.5 convolution_convert_fusion.2
  724.1 11.1 convolution_convert_fusion.1
  737.0 19.0 %convolution_convert_fusion = bf16[2048,3072]{1,0:T(8,128)(2,1)} fusion(bf16[1024,1536]{1,0:T(8,128)(2,1)} %get-tuple-element.36, bf16[1024,1536]{1,0:T(8,128)(2,1)S(1)} %copy-done.77, bf16[256,2048]{1,0:T(8,128)(2,1)} %collective-permute-done.11, bf16[256,2048]{1,0:T(8,128)(2,1)} %collective-permute-done.10, bf16[256,2048]{1,0:T(8,128)(2,1)} %collective-permute-done.9, ...), kind=kOutput, calls=%fused_computation.17 | convolution fusion | flops 12920553472 | bytes 23068672 | tf_op jit(solution)/shard_map/dot_general | solution.py:54
  760.0 9.6 convolution_multiply_fusion
  774.8 29.8 %reduce-scatter.6.cloned.1.call-done = bf16[4,256,512]{2,1,0:T(8,128)(2,1)} async-done(((bf16[4,2048,512]{2,1,0:T(8,128)(2,1)}), bf16[4,256,512]{2,1,0:T(8,128)(2,1)}) %reduce-scatter.6.cloned.1.call-update) | async-done | bytes 1048592 | tf_op jit(solution)/shard_map/reduce_scatter | solution.py:261
  811.9 4.3 multiply_reduce_fusion.6
  816.7 5.5 fusion.53
  823.7 3.0 pad_maximum_fusion.9
  826.8 8.7 bitcast_convert_fusion
  837.1 9.2 fusion.101
  850.3 8.8 fusion.102
  859.6 13.2 %collective-permute-done.27 = bf16[256,2048]{1,0:T(8,128)(2,1)S(1)} collective-permute-done((bf16[256,2048]{1,0:T(8,128)(2,1)S(1)}, bf16[256,2048]{1,0:T(8,128)(2,1)S(1)}, u32[]{:S(2)}, u32[]{:S(2)}) %collective-permute-start.27) | collective-permute-done | bytes 1048608 | tf_op jit(solution)/shard_map/ppermute | solution.py:60
  872.8 20.7 %collective-permute-done.28 = bf16[256,2048]{1,0:T(8,128)(2,1)S(1)} collective-permute-done((bf16[256,2048]{1,0:T(8,128)(2,1)S(1)}, bf16[256,2048]{1,0:T(8,128)(2,1)S(1)}, u32[]{:S(2)}, u32[]{:S(2)}) %collective-permute-start.28) | collective-permute-done | bytes 1048608 | tf_op jit(solution)/shard_map/ppermute | solution.py:60
  893.6 3.1 fusion.36
  908.6 3.6 reduce-scatter.14.cloned.1.call-done
  914.9 69.6 %all-reduce.5 = f32[32,136]{1,0:T(8,128)S(1)} all-reduce(f32[32,136]{1,0:T(8,128)S(1)} %pad_maximum_fusion.25), channel_id=4, replica_groups=mesh['fsdp'=4,'ctx'=8] {'fsdp','ctx'}, use_global_device_ids=true, to_apply=%region_18.19.clone | all-reduce | flops 4352 | bytes 34816
  985.7 4.2 fusion.54
  989.8 53.3 %reduce-scatter.12.cloned.1.call-done = bf16[4,64,3072]{2,1,0:T(8,128)(2,1)} async-done(((bf16[4,512,3072]{2,1,0:T(8,128)(2,1)}), bf16[4,64,3072]{2,1,0:T(8,128)(2,1)}) %reduce-scatter.12.cloned.1.call-update) | async-done | bytes 1572880 | tf_op jit(solution)/shard_map/reduce_scatter | solution.py:240
  1048.6 8.2 collective-permute-done.33
  1056.8 6.6 collective-permute-done.34
  1063.8 29.9 %reduce-scatter.8.cloned.1.call-done = bf16[4,64,1024]{2,1,0:T(8,128)(2,1)} async-done(((bf16[4,512,1024]{2,1,0:T(8,128)(2,1)}), bf16[4,64,1024]{2,1,0:T(8,128)(2,1)}) %reduce-scatter.8.cloned.1.call-update) | async-done | bytes 524304 | tf_op jit(solution)/shard_map/reduce_scatter | solution.py:271
  (393 shorter events, 145.8 us)
Async XLA Ops:
  7.2 105.4 %all-gather.7.cloned.1.call-start = ((), (), s32[]{:S(2)}) async-start(), calls=%async_computation.5 | async-start | bytes 4718592 | tf_op jit(solution)/shard_map/all_gather | solution.py:169
  9.2 6.9 collective-permute-start.3
  12.2 7.8 collective-permute-start.4
  13.8 6.3 collective-permute-start.5
  20.9 89.2 %copy-start.10 = (bf16[1,256,2048]{2,1,0:T(8,128)(2,1)S(1)}, bf16[1,256,2048]{2,1,0:T(8,128)(2,1)}, u32[]{:S(2)}) copy-start(bf16[1,256,2048]{2,1,0:T(8,128)(2,1)} %param.16) | copy-start | bytes 3145732
  20.9 203.4 %all-gather.9.cloned.1.call-start = ((), (), s32[]{:S(2)}) async-start(), calls=%async_computation.6 | async-start | bytes 9437184 | tf_op jit(solution)/shard_map/all_gather | solution.py:180
  21.0 89.1 %collective-permute-start = (bf16[256,2048]{1,0:T(8,128)(2,1)}, bf16[256,2048]{1,0:T(8,128)(2,1)}, u32[]{:S(2)}, u32[]{:S(2)}) collective-permute-start(bf16[256,2048]{1,0:T(8,128)(2,1)} %bitcast.196), channel_id=1, source_target_pairs={{0,8},{8,0},{16,24},{24,16},{1,9},{9,1},{17,25},{25,17},{2,10},{10... | collective-permute-start | bytes 3145736 | tf_op jit(solution)/shard_map/ppermute | solution.py:60
  22.2 88.0 %collective-permute-start.1 = (bf16[256,2048]{1,0:T(8,128)(2,1)}, bf16[256,2048]{1,0:T(8,128)(2,1)}, u32[]{:S(2)}, u32[]{:S(2)}) collective-permute-start(bf16[256,2048]{1,0:T(8,128)(2,1)} %bitcast.197), channel_id=1, source_target_pairs={{0,16},{8,24},{16,0},{24,8},{1,17},{9,25},{17,1},{25,9},{2,18},{10... | collective-permute-start | bytes 3145736 | tf_op jit(solution)/shard_map/ppermute | solution.py:60
  23.1 87.0 %collective-permute-start.2 = (bf16[256,2048]{1,0:T(8,128)(2,1)}, bf16[256,2048]{1,0:T(8,128)(2,1)}, u32[]{:S(2)}, u32[]{:S(2)}) collective-permute-start(bf16[256,2048]{1,0:T(8,128)(2,1)} %bitcast.198), channel_id=1, source_target_pairs={{0,24},{8,16},{16,8},{24,0},{1,25},{9,17},{17,9},{25,1},{2,26},{10... | collective-permute-start | bytes 3145736 | tf_op jit(solution)/shard_map/ppermute | solution.py:60
  102.7 64.8 %copy-start.70 = (s32[1024]{0:T(1024)}, s32[1024]{0:T(1024)S(1)}, u32[]{:S(2)}) copy-start(s32[1024]{0:T(1024)S(1)} %pad_clamp_fusion) | copy-start | bytes 12292
  103.5 23.4 %copy-start.68 = (f32[128]{0:T(128)}, f32[128]{0:T(128)S(1)}, u32[]{:S(2)}) copy-start(f32[128]{0:T(128)S(1)} %mul.525) | copy-start | bytes 1540
  105.5 24.2 %copy-start.31 = (f32[4,256,128]{2,1,0:T(8,128)}, f32[4,256,128]{2,1,0:T(8,128)S(1)}, u32[]{:S(2)}) copy-start(f32[4,256,128]{2,1,0:T(8,128)S(1)} %copy.195) | copy-start | bytes 1572868
  105.8 14.5 %copy-start.29 = (f32[4,256,128]{2,1,0:T(8,128)}, f32[4,256,128]{2,1,0:T(8,128)S(1)}, u32[]{:S(2)}) copy-start(f32[4,256,128]{2,1,0:T(8,128)S(1)} %copy.194) | copy-start | bytes 1572868
  142.0 162.1 %all-gather.11.cloned.1.call-start = ((), (), s32[]{:S(2)}) async-start(), calls=%async_computation.7 | async-start | bytes 2359296 | tf_op jit(solution)/shard_map/all_gather | solution.py:181
  142.8 293.1 %all-gather.13.cloned.1.call-start = ((), (), s32[]{:S(2)}) async-start(), calls=%async_computation.8 | async-start | bytes 14155776 | tf_op jit(solution)/shard_map/all_gather | solution.py:183
  144.5 12.3 %collective-permute-start.12 = (bf16[64,3072]{1,0:T(8,128)(2,1)S(1)}, bf16[64,3072]{1,0:T(8,128)(2,1)S(1)}, u32[]{:S(2)}, u32[]{:S(2)}) collective-permute-start(bf16[64,3072]{1,0:T(8,128)(2,1)S(1)} %pad_maximum_fusion.19), channel_id=1, source_target_pairs={{0,8},{8,0},{16,24},{24,16},{1,9},{9,1},{17,25},{25,17},{2,10},{10... | collective-permute-start | bytes 1179656 | tf_op jit(solution)/shard_map/ppermute | solution.py:60
  146.8 18.5 %collective-permute-start.13 = (bf16[64,3072]{1,0:T(8,128)(2,1)S(1)}, bf16[64,3072]{1,0:T(8,128)(2,1)S(1)}, u32[]{:S(2)}, u32[]{:S(2)}) collective-permute-start(bf16[64,3072]{1,0:T(8,128)(2,1)S(1)} %pad_maximum_fusion.20), channel_id=1, source_target_pairs={{0,16},{8,24},{16,0},{24,8},{1,17},{9,25},{17,1},{25,9},{2,18},{10... | collective-permute-start | bytes 1179656 | tf_op jit(solution)/shard_map/ppermute | solution.py:60
  148.6 16.7 %collective-permute-start.14 = (bf16[64,3072]{1,0:T(8,128)(2,1)S(1)}, bf16[64,3072]{1,0:T(8,128)(2,1)S(1)}, u32[]{:S(2)}, u32[]{:S(2)}) collective-permute-start(bf16[64,3072]{1,0:T(8,128)(2,1)S(1)} %pad_maximum_fusion.21), channel_id=1, source_target_pairs={{0,24},{8,16},{16,8},{24,0},{1,25},{9,17},{17,9},{25,1},{2,26},{10... | collective-permute-start | bytes 1179656 | tf_op jit(solution)/shard_map/ppermute | solution.py:60
  166.6 305.1 %all-gather.15.cloned.1.call-start = ((), (), s32[]{:S(2)}) async-start(), calls=%async_computation.9 | async-start | bytes 7077888 | tf_op jit(solution)/shard_map/all_gather | solution.py:184
  167.2 637.4 %reduce-scatter.6.cloned.1.call-start = ((), (), s32[]{:S(2)}) async-start(), calls=%async_computation.10 | async-start | bytes 9437184 | tf_op jit(solution)/shard_map/reduce_scatter | solution.py:261
  167.3 152.7 %copy-start = (s32[4]{0:T(128)}, s32[4]{0:T(128)S(1)}, u32[]{:S(2)}) copy-start(s32[4]{0:T(128)S(1)} %get-tuple-element.22) | copy-start | bytes 52
  313.5 26.2 %collective-permute-start.6 = (bf16[256,2048]{1,0:T(8,128)(2,1)}, bf16[256,2048]{1,0:T(8,128)(2,1)S(1)}, u32[]{:S(2)}, u32[]{:S(2)}) collective-permute-start(bf16[256,2048]{1,0:T(8,128)(2,1)} %get-tuple-element.53), channel_id=1, source_target_pairs={{0,8},{8,0},{16,24},{24,16},{1,9},{9,1},{17,25},{25,17},{2,10},{10... | collective-permute-start | bytes 3145736 | tf_op jit(solution)/shard_map/ppermute | solution.py:60
  315.0 48.7 %collective-permute-start.7 = (bf16[256,2048]{1,0:T(8,128)(2,1)}, bf16[256,2048]{1,0:T(8,128)(2,1)S(1)}, u32[]{:S(2)}, u32[]{:S(2)}) collective-permute-start(bf16[256,2048]{1,0:T(8,128)(2,1)} %get-tuple-element.55), channel_id=1, source_target_pairs={{0,16},{8,24},{16,0},{24,8},{1,17},{9,25},{17,1},{25,9},{2,18},{10... | collective-permute-start | bytes 3145736 | tf_op jit(solution)/shard_map/ppermute | solution.py:60
  316.5 47.2 %collective-permute-start.8 = (bf16[256,2048]{1,0:T(8,128)(2,1)}, bf16[256,2048]{1,0:T(8,128)(2,1)}, u32[]{:S(2)}, u32[]{:S(2)}) collective-permute-start(bf16[256,2048]{1,0:T(8,128)(2,1)} %get-tuple-element.54), channel_id=1, source_target_pairs={{0,24},{8,16},{16,8},{24,0},{1,25},{9,17},{17,9},{25,1},{2,26},{10... | collective-permute-start | bytes 3145736 | tf_op jit(solution)/shard_map/ppermute | solution.py:60
  317.0 67.8 %collective-permute-start.18 = (bf16[256,2048]{1,0:T(8,128)(2,1)}, bf16[256,2048]{1,0:T(8,128)(2,1)}, u32[]{:S(2)}, u32[]{:S(2)}) collective-permute-start(bf16[256,2048]{1,0:T(8,128)(2,1)} %bitcast.42), channel_id=1, source_target_pairs={{0,8},{8,0},{16,24},{24,16},{1,9},{9,1},{17,25},{25,17},{2,10},{10... | collective-permute-start | bytes 3145736 | tf_op jit(solution)/shard_map/ppermute | solution.py:60
  318.5 112.7 %collective-permute-start.19 = (bf16[256,2048]{1,0:T(8,128)(2,1)}, bf16[256,2048]{1,0:T(8,128)(2,1)}, u32[]{:S(2)}, u32[]{:S(2)}) collective-permute-start(bf16[256,2048]{1,0:T(8,128)(2,1)} %bitcast.42), channel_id=1, source_target_pairs={{0,16},{8,24},{16,0},{24,8},{1,17},{9,25},{17,1},{25,9},{2,18},{10... | collective-permute-start | bytes 3145736 | tf_op jit(solution)/shard_map/ppermute | solution.py:60
  320.1 243.5 %copy-start.52 = (f32[2048]{0:T(1024)}, f32[2048]{0:T(1024)S(1)}, u32[]{:S(2)}) copy-start(f32[2048]{0:T(1024)S(1)} %mul.563) | copy-start | bytes 24580
  339.7 24.0 %copy-start.43 = (bf16[256,2048]{1,0:T(8,128)(2,1)}, bf16[256,2048]{1,0:T(8,128)(2,1)S(1)}, u32[]{:S(2)}) copy-start(bf16[256,2048]{1,0:T(8,128)(2,1)S(1)} %collective-permute-done.6) | copy-start | bytes 3145732
  339.7 91.5 %collective-permute-start.20 = (bf16[256,2048]{1,0:T(8,128)(2,1)}, bf16[256,2048]{1,0:T(8,128)(2,1)}, u32[]{:S(2)}, u32[]{:S(2)}) collective-permute-start(bf16[256,2048]{1,0:T(8,128)(2,1)} %bitcast.42), channel_id=1, source_target_pairs={{0,24},{8,16},{16,8},{24,0},{1,25},{9,17},{17,9},{25,1},{2,26},{10... | collective-permute-start | bytes 3145736 | tf_op jit(solution)/shard_map/ppermute | solution.py:60
  368.8 194.9 %copy-start.4 = (f32[256,2048]{1,0:T(8,128)}, f32[256,2048]{1,0:T(8,128)S(1)}, u32[]{:S(2)}) copy-start(f32[256,2048]{1,0:T(8,128)S(1)} %get-tuple-element.32) | copy-start | bytes 6291460
  368.8 194.9 %copy-start.61 = (f32[256]{0:T(256)}, f32[256]{0:T(256)S(1)}, u32[]{:S(2)}) copy-start(f32[256]{0:T(256)S(1)} %fusion.73) | copy-start | bytes 3076
  370.2 82.5 %collective-permute-start.10 = (bf16[256,2048]{1,0:T(8,128)(2,1)}, bf16[256,2048]{1,0:T(8,128)(2,1)}, u32[]{:S(2)}, u32[]{:S(2)}) collective-permute-start(bf16[256,2048]{1,0:T(8,128)(2,1)} %multiply_convert_fusion.2), channel_id=1, source_target_pairs={{0,16},{8,24},{16,0},{24,8},{1,17},{9,25},{17,1},{25,9},{2,18},{10... | collective-permute-start | bytes 3145736 | tf_op jit(solution)/shard_map/ppermute | solution.py:60
  371.7 81.0 %collective-permute-start.11 = (bf16[256,2048]{1,0:T(8,128)(2,1)}, bf16[256,2048]{1,0:T(8,128)(2,1)}, u32[]{:S(2)}, u32[]{:S(2)}) collective-permute-start(bf16[256,2048]{1,0:T(8,128)(2,1)} %multiply_convert_fusion.2), channel_id=1, source_target_pairs={{0,24},{8,16},{16,8},{24,0},{1,25},{9,17},{17,9},{25,1},{2,26},{10... | collective-permute-start | bytes 3145736 | tf_op jit(solution)/shard_map/ppermute | solution.py:60
  384.8 67.9 %collective-permute-start.9 = (bf16[256,2048]{1,0:T(8,128)(2,1)}, bf16[256,2048]{1,0:T(8,128)(2,1)}, u32[]{:S(2)}, u32[]{:S(2)}) collective-permute-start(bf16[256,2048]{1,0:T(8,128)(2,1)} %multiply_convert_fusion.2), channel_id=1, source_target_pairs={{0,8},{8,0},{16,24},{24,16},{1,9},{9,1},{17,25},{25,17},{2,10},{10... | collective-permute-start | bytes 3145736 | tf_op jit(solution)/shard_map/ppermute | solution.py:60
  435.8 288.2 %copy-start.17 = (bf16[256,2048]{1,0:T(8,128)(2,1)}, bf16[256,2048]{1,0:T(8,128)(2,1)S(1)}, u32[]{:S(2)}) copy-start(bf16[256,2048]{1,0:T(8,128)(2,1)S(1)} %get-tuple-element.46) | copy-start | bytes 3145732
  512.6 26.1 %collective-permute-start.21 = (bf16[256,2048]{1,0:T(8,128)(2,1)S(1)}, bf16[256,2048]{1,0:T(8,128)(2,1)S(1)}, u32[]{:S(2)}, u32[]{:S(2)}) collective-permute-start(bf16[256,2048]{1,0:T(8,128)(2,1)S(1)} %get-tuple-element.43), channel_id=1, source_target_pairs={{0,8},{8,0},{16,24},{24,16},{1,9},{9,1},{17,25},{25,17},{2,10},{10... | collective-permute-start | bytes 3145736 | tf_op jit(solution)/shard_map/ppermute | solution.py:60
  513.2 45.5 %collective-permute-start.22 = (bf16[256,2048]{1,0:T(8,128)(2,1)S(1)}, bf16[256,2048]{1,0:T(8,128)(2,1)S(1)}, u32[]{:S(2)}, u32[]{:S(2)}) collective-permute-start(bf16[256,2048]{1,0:T(8,128)(2,1)S(1)} %get-tuple-element.45), channel_id=1, source_target_pairs={{0,16},{8,24},{16,0},{24,8},{1,17},{9,25},{17,1},{25,9},{2,18},{10... | collective-permute-start | bytes 3145736 | tf_op jit(solution)/shard_map/ppermute | solution.py:60
  514.7 45.5 %collective-permute-start.23 = (bf16[256,2048]{1,0:T(8,128)(2,1)S(1)}, bf16[256,2048]{1,0:T(8,128)(2,1)S(1)}, u32[]{:S(2)}, u32[]{:S(2)}) collective-permute-start(bf16[256,2048]{1,0:T(8,128)(2,1)S(1)} %get-tuple-element.44), channel_id=1, source_target_pairs={{0,24},{8,16},{16,8},{24,0},{1,25},{9,17},{17,9},{25,1},{2,26},{10... | collective-permute-start | bytes 3145736 | tf_op jit(solution)/shard_map/ppermute | solution.py:60
  563.6 49.5 %copy-start.36 = (bf16[512,2048]{1,0:T(8,128)(2,1)S(1)}, bf16[512,2048]{1,0:T(8,128)(2,1)}, u32[]{:S(2)}) copy-start(bf16[512,2048]{1,0:T(8,128)(2,1)} %all-gather.11.cloned.1.call-done) | copy-start | bytes 6291460
  564.9 46.2 %copy-start.45 = (bf16[256,2048]{1,0:T(8,128)(2,1)}, bf16[256,2048]{1,0:T(8,128)(2,1)S(1)}, u32[]{:S(2)}) copy-start(bf16[256,2048]{1,0:T(8,128)(2,1)S(1)} %fusion.83) | copy-start | bytes 3145732
  564.9 26.0 %collective-permute-start.24 = (bf16[256,2048]{1,0:T(8,128)(2,1)S(1)}, bf16[256,2048]{1,0:T(8,128)(2,1)S(1)}, u32[]{:S(2)}, u32[]{:S(2)}) collective-permute-start(bf16[256,2048]{1,0:T(8,128)(2,1)S(1)} %fusion.83), channel_id=1, source_target_pairs={{0,8},{8,0},{16,24},{24,16},{1,9},{9,1},{17,25},{25,17},{2,10},{10... | collective-permute-start | bytes 3145736 | tf_op jit(solution)/shard_map/ppermute | solution.py:60
  565.7 45.4 %collective-permute-start.25 = (bf16[256,2048]{1,0:T(8,128)(2,1)S(1)}, bf16[256,2048]{1,0:T(8,128)(2,1)S(1)}, u32[]{:S(2)}, u32[]{:S(2)}) collective-permute-start(bf16[256,2048]{1,0:T(8,128)(2,1)S(1)} %fusion.83), channel_id=1, source_target_pairs={{0,16},{8,24},{16,0},{24,8},{1,17},{9,25},{17,1},{25,9},{2,18},{10... | collective-permute-start | bytes 3145736 | tf_op jit(solution)/shard_map/ppermute | solution.py:60
  567.2 43.9 %collective-permute-start.26 = (bf16[256,2048]{1,0:T(8,128)(2,1)S(1)}, bf16[256,2048]{1,0:T(8,128)(2,1)S(1)}, u32[]{:S(2)}, u32[]{:S(2)}) collective-permute-start(bf16[256,2048]{1,0:T(8,128)(2,1)S(1)} %fusion.83), channel_id=1, source_target_pairs={{0,24},{8,16},{16,8},{24,0},{1,25},{9,17},{17,9},{25,1},{2,26},{10... | collective-permute-start | bytes 3145736 | tf_op jit(solution)/shard_map/ppermute | solution.py:60
  590.9 20.2 %copy-start.73 = (bf16[256,2048]{1,0:T(8,128)(2,1)}, bf16[256,2048]{1,0:T(8,128)(2,1)S(1)}, u32[]{:S(2)}) copy-start(bf16[256,2048]{1,0:T(8,128)(2,1)S(1)} %collective-permute-done.24) | copy-start | bytes 3145732
  658.6 27.8 %copy-start.20 = (bf16[4,256,2,2,128]{1,4,3,2,0:T(8,128)(2,1)S(1)}, bf16[4,256,2,2,128]{1,4,3,2,0:T(8,128)(2,1)}, u32[]{:S(2)}) copy-start(bf16[4,256,2,2,128]{1,4,3,2,0:T(8,128)(2,1)} %fusion.43) | copy-start | bytes 3145732
  716.9 189.9 %reduce-scatter.10.cloned.1.call-start = ((), (), s32[]{:S(2)}) async-start(), calls=%async_computation.12 | async-start | bytes 2359296 | tf_op jit(solution)/shard_map/reduce_scatter | solution.py:247
  724.0 188.2 %reduce-scatter.14.cloned.1.call-start = ((), (), s32[]{:S(2)}) async-start(), calls=%async_computation.14 | async-start | bytes 7077888 | tf_op jit(solution)/shard_map/reduce_scatter | solution.py:231
  735.1 308.0 %reduce-scatter.12.cloned.1.call-start = ((), (), s32[]{:S(2)}) async-start(), calls=%async_computation.13 | async-start | bytes 14155776 | tf_op jit(solution)/shard_map/reduce_scatter | solution.py:240
  756.1 337.7 %reduce-scatter.8.cloned.1.call-start = ((), (), s32[]{:S(2)}) async-start(), calls=%async_computation.11 | async-start | bytes 4718592 | tf_op jit(solution)/shard_map/reduce_scatter | solution.py:271
  846.7 26.1 %collective-permute-start.27 = (bf16[256,2048]{1,0:T(8,128)(2,1)S(1)}, bf16[256,2048]{1,0:T(8,128)(2,1)S(1)}, u32[]{:S(2)}, u32[]{:S(2)}) collective-permute-start(bf16[256,2048]{1,0:T(8,128)(2,1)S(1)} %get-tuple-element.40), channel_id=1, source_target_pairs={{0,8},{8,0},{16,24},{24,16},{1,9},{9,1},{17,25},{25,17},{2,10},{10... | collective-permute-start | bytes 3145736 | tf_op jit(solution)/shard_map/ppermute | solution.py:60
  848.3 45.2 %collective-permute-start.28 = (bf16[256,2048]{1,0:T(8,128)(2,1)S(1)}, bf16[256,2048]{1,0:T(8,128)(2,1)S(1)}, u32[]{:S(2)}, u32[]{:S(2)}) collective-permute-start(bf16[256,2048]{1,0:T(8,128)(2,1)S(1)} %get-tuple-element.42), channel_id=1, source_target_pairs={{0,16},{8,24},{16,0},{24,8},{1,17},{9,25},{17,1},{25,9},{2,18},{10... | collective-permute-start | bytes 3145736 | tf_op jit(solution)/shard_map/ppermute | solution.py:60
  849.7 43.8 %collective-permute-start.29 = (bf16[256,2048]{1,0:T(8,128)(2,1)S(1)}, bf16[256,2048]{1,0:T(8,128)(2,1)S(1)}, u32[]{:S(2)}, u32[]{:S(2)}) collective-permute-start(bf16[256,2048]{1,0:T(8,128)(2,1)S(1)} %get-tuple-element.41), channel_id=1, source_target_pairs={{0,24},{8,16},{16,8},{24,0},{1,25},{9,17},{17,9},{25,1},{2,26},{10... | collective-permute-start | bytes 3145736 | tf_op jit(solution)/shard_map/ppermute | solution.py:60
  859.1 34.4 %copy-start.12 = (bf16[1,256,2048]{2,1,0:T(8,128)(2,1)S(1)}, bf16[1,256,2048]{2,1,0:T(8,128)(2,1)}, u32[]{:S(2)}) copy-start(bf16[1,256,2048]{2,1,0:T(8,128)(2,1)} %param.16) | copy-start | bytes 3145732
  902.5 83.2 %collective-permute-start.15 = (bf16[256,2048]{1,0:T(8,128)(2,1)}, bf16[256,2048]{1,0:T(8,128)(2,1)}, u32[]{:S(2)}, u32[]{:S(2)}) collective-permute-start(bf16[256,2048]{1,0:T(8,128)(2,1)} %get-tuple-element.50), channel_id=1, source_target_pairs={{0,8},{8,0},{16,24},{24,16},{1,9},{9,1},{17,25},{25,17},{2,10},{10... | collective-permute-start | bytes 3145736 | tf_op jit(solution)/shard_map/ppermute | solution.py:60
  903.7 82.0 %collective-permute-start.16 = (bf16[256,2048]{1,0:T(8,128)(2,1)}, bf16[256,2048]{1,0:T(8,128)(2,1)}, u32[]{:S(2)}, u32[]{:S(2)}) collective-permute-start(bf16[256,2048]{1,0:T(8,128)(2,1)} %get-tuple-element.51), channel_id=1, source_target_pairs={{0,16},{8,24},{16,0},{24,8},{1,17},{9,25},{17,1},{25,9},{2,18},{10... | collective-permute-start | bytes 3145736 | tf_op jit(solution)/shard_map/ppermute | solution.py:60
  904.5 81.2 %collective-permute-start.17 = (bf16[256,2048]{1,0:T(8,128)(2,1)}, bf16[256,2048]{1,0:T(8,128)(2,1)}, u32[]{:S(2)}, u32[]{:S(2)}) collective-permute-start(bf16[256,2048]{1,0:T(8,128)(2,1)} %get-tuple-element.52), channel_id=1, source_target_pairs={{0,24},{8,16},{16,8},{24,0},{1,25},{9,17},{17,9},{25,1},{2,26},{10... | collective-permute-start | bytes 3145736 | tf_op jit(solution)/shard_map/ppermute | solution.py:60
  1044.7 12.1 %collective-permute-start.33 = (bf16[64,3072]{1,0:T(8,128)(2,1)S(1)}, bf16[64,3072]{1,0:T(8,128)(2,1)S(1)}, u32[]{:S(2)}, u32[]{:S(2)}) collective-permute-start(bf16[64,3072]{1,0:T(8,128)(2,1)S(1)} %get-tuple-element.64), channel_id=1, source_target_pairs={{0,8},{8,0},{16,24},{24,16},{1,9},{9,1},{17,25},{25,17},{2,10},{10... | collective-permute-start | bytes 1179656 | tf_op jit(solution)/shard_map/ppermute | solution.py:60
  1046.3 17.1 %collective-permute-start.34 = (bf16[64,3072]{1,0:T(8,128)(2,1)S(1)}, bf16[64,3072]{1,0:T(8,128)(2,1)S(1)}, u32[]{:S(2)}, u32[]{:S(2)}) collective-permute-start(bf16[64,3072]{1,0:T(8,128)(2,1)S(1)} %get-tuple-element.63), channel_id=1, source_target_pairs={{0,16},{8,24},{16,0},{24,8},{1,17},{9,25},{17,1},{25,9},{2,18},{10... | collective-permute-start | bytes 1179656 | tf_op jit(solution)/shard_map/ppermute | solution.py:60
  1047.7 15.7 %collective-permute-start.35 = (bf16[64,3072]{1,0:T(8,128)(2,1)S(1)}, bf16[64,3072]{1,0:T(8,128)(2,1)S(1)}, u32[]{:S(2)}, u32[]{:S(2)}) collective-permute-start(bf16[64,3072]{1,0:T(8,128)(2,1)S(1)} %get-tuple-element.62), channel_id=1, source_target_pairs={{0,24},{8,16},{16,8},{24,0},{1,25},{9,17},{17,9},{25,1},{2,26},{10... | collective-permute-start | bytes 1179656 | tf_op jit(solution)/shard_map/ppermute | solution.py:60
  1063.8 40.1 %copy-start.41 = (f32[64,6144]{1,0:T(8,128)}, f32[64,6144]{1,0:T(8,128)S(1)}, u32[]{:S(2)}) copy-start(f32[64,6144]{1,0:T(8,128)S(1)} %get-tuple-element.73) | copy-start | bytes 4718596
  1063.8 40.1 %copy-start.42 = (f32[64,6144]{1,0:T(8,128)}, f32[64,6144]{1,0:T(8,128)S(1)}, u32[]{:S(2)}) copy-start(f32[64,6144]{1,0:T(8,128)S(1)} %get-tuple-element.74) | copy-start | bytes 4718596
  1094.9 5.8 collective-permute-start.30
  1096.4 5.5 collective-permute-start.31
  1097.9 5.9 collective-permute-start.32
  (60 other events, 229.5 us)
Sparse Core Ops, SparseCore 0:
  21.0 47.1 all-gather.6
  142.1 82.1 all-gather.8
  226.0 27.6 all-gather.10
  255.7 116.0 all-gather.12
  373.3 62.8 all-gather.14
  717.0 87.4 reduce-scatter.5
  806.9 34.5 reduce-scatter.9
  843.8 68.3 reduce-scatter.13
  914.5 128.6 reduce-scatter.11
  1045.3 48.3 reduce-scatter.7

commit v2 on v1

v2 whole, which is shorter than its diff:
```python
import functools

import jax
import jax.numpy as jnp
from jax import lax
from jax.experimental import pallas as pl
from jax.experimental.pallas import tpu as pltpu
from jax.sharding import PartitionSpec as P

H = 16
KVH = 8
HD = 128

EPS = 1e-06
THETA = 1000000.0
LOG2_E = 1.4426950408889634
BF = jnp.bfloat16
F32 = jnp.float32


def rms_scale(values, gain):
    inverse = lax.rsqrt(jnp.mean(values * values, axis=-1, keepdims=True) + EPS)
    return values * inverse * gain


def rope_tables(positions):
    freqs = THETA ** (-(jnp.arange(HD // 2, dtype=F32) * 2.0) / HD)
    angles = positions.astype(F32)[:, None] * freqs
    cosine = jnp.cos(angles)
    sine = jnp.sin(angles)
    return (jnp.concatenate([cosine, cosine], axis=-1), jnp.concatenate([-sine, sine], axis=-1))


def dot_nn(left, right):
    return lax.dot_general(left, right, (((1,), (0,)), ((), ())), preferred_element_type=F32)


def dot_nt(left, right):
    return lax.dot_general(left, right, (((1,), (1,)), ((), ())), preferred_element_type=F32)


def dot_tn(left, right):
    return lax.dot_general(left, right, (((0,), (0,)), ((), ())), preferred_element_type=F32)


def pick(stacked, index):
    return lax.dynamic_index_in_dim(stacked, index, 0, keepdims=False)


def xor_order(stacked, index):
    count = stacked.shape[0]
    bit = 1
    while bit < count:
        paired = stacked.reshape((count // (2 * bit), 2, bit) + stacked.shape[1:])
        flipped = jnp.concatenate([paired[:, 1:], paired[:, :1]], axis=1).reshape(stacked.shape)
        stacked = jnp.where((index & bit) != 0, flipped, stacked)
        bit *= 2
    return stacked


def key_block(kv_ref, block, blocks, cols):
    kc, kfb, kz = block // (2 * blocks), (block // blocks) % 2, block % blocks
    taken = kv_ref[kc, kfb, :, kz, :, cols]
    return taken.reshape(taken.shape[0] * taken.shape[1], taken.shape[2])


def stack_heads(ref, kv_head, per_key):
    parts = []
    for head in range(kv_head * per_key, (kv_head + 1) * per_key):
        part = ref[0, :, 0, :, head * HD : (head + 1) * HD]
        parts.append(part.reshape(part.shape[0] * part.shape[1], HD))
    return jnp.concatenate(parts, axis=0)


def attn_fwd_kernel(meta, q_ref, kv_ref, o_ref, lse_ref, acc_ref, total_ref, *, kv_heads, per_key, blocks, piece):
    tile_rows = q_ref.shape[1] * piece
    stacked = per_key * tile_rows
    kv_width = kv_heads * HD
    tile = pl.program_id(0)
    length, flip, start = meta[0], meta[1] * piece, meta[2 + tile]
    ids = 2 + 2 * blocks
    row = lax.broadcasted_iota(jnp.int32, (stacked, 1), 0) % tile_rows
    row_limit = jnp.minimum(start + (row ^ flip), length - 1)
    column = lax.broadcasted_iota(jnp.int32, (1, 2 * tile_rows), 1) ^ flip
    last = jnp.minimum(start, length - 1) // tile_rows
    acc_ref[...] = jnp.zeros_like(acc_ref)
    total_ref[...] = jnp.zeros_like(total_ref)
    queries = [stack_heads(q_ref, h, per_key) for h in range(kv_heads)]

    def body(step, carry):
        block_a, block_b = meta[ids + 2 * step], meta[ids + 2 * step + 1]
        allowed = step * (2 * tile_rows) + column <= row_limit
        for h in range(kv_heads):
            k_cols = slice(h * HD, (h + 1) * HD)
            v_cols = slice(kv_width + h * HD, kv_width + (h + 1) * HD)
            keys = jnp.concatenate([key_block(kv_ref, b, blocks, k_cols) for b in (block_a, block_b)], axis=0)
            values = jnp.concatenate([key_block(kv_ref, b, blocks, v_cols) for b in (block_a, block_b)], axis=0)
            scores = dot_nt(queries[h], keys)
            weight = jnp.where(allowed, jnp.exp2(scores * (HD ** (-0.5) * LOG2_E)), 0.0)
            part = weight[:, :HD]
            for at in range(HD, 2 * tile_rows, HD):
                part = part + weight[:, at : at + HD]
            total_ref[h] += part
            acc_ref[h] += dot_nn(weight.astype(BF), values)
        return carry

    lax.fori_loop(0, last // 2 + 1, body, 0)
    for h in range(kv_heads):
        total = jnp.sum(total_ref[h], axis=1, keepdims=True)
        out = (acc_ref[h] / total).astype(BF)
        for g in range(per_key):
            head = h * per_key + g
            o_ref[0, :, 0, :, head * HD : (head + 1) * HD] = out[g * tile_rows : (g + 1) * tile_rows].reshape(
                -1, piece, HD
            )
        lse_ref[0, h] = jnp.log2(jnp.sum(total_ref[h].T, axis=0, keepdims=True))


def attn_bwd_kernel(
    meta, q_ref, kv_ref, do_ref, o_ref, lse_ref, dq_ref, dkv_ref, sum_ref, dq_sum_ref, *, kv_heads, per_key, blocks, piece
):
    tile_rows = q_ref.shape[1] * piece
    stacked = per_key * tile_rows
    kv_width = kv_heads * HD
    tile = pl.program_id(0)
    length, flip, start = meta[0], meta[1] * piece, meta[2 + tile]
    ids = 2 + 2 * blocks
    row = lax.broadcasted_iota(jnp.int32, (1, stacked), 1) % tile_rows
    row_limit = jnp.minimum(start + (row ^ flip), length - 1)
    column = lax.broadcasted_iota(jnp.int32, (2 * tile_rows, 1), 0) ^ flip
    score_scale = HD ** (-0.5)

    @pl.when(tile == 0)
    def _():
        sum_ref[...] = jnp.zeros_like(sum_ref)

    dq_sum_ref[...] = jnp.zeros_like(dq_sum_ref)
    queries = [stack_heads(q_ref, h, per_key) for h in range(kv_heads)]
    grads = [stack_heads(do_ref, h, per_key) for h in range(kv_heads)]
    deltas = [
        jnp.sum((grads[h].astype(F32) * stack_heads(o_ref, h, per_key).astype(F32)).T, axis=0, keepdims=True)
        for h in range(kv_heads)
    ]
    logs = [lse_ref[0, h] for h in range(kv_heads)]

    def body(step, carry):
        pair = (meta[ids + 2 * step], meta[ids + 2 * step + 1])
        allowed = step * (2 * tile_rows) + column <= row_limit
        for h in range(kv_heads):
            k_cols = slice(h * HD, (h + 1) * HD)
            v_cols = slice(kv_width + h * HD, kv_width + (h + 1) * HD)
            keys = jnp.concatenate([key_block(kv_ref, b, blocks, k_cols) for b in pair], axis=0)
            values = jnp.concatenate([key_block(kv_ref, b, blocks, v_cols) for b in pair], axis=0)
            scores = dot_nt(keys, queries[h])
            probs = jnp.where(allowed, jnp.exp2(scores * (score_scale * LOG2_E) - logs[h]), 0.0)
            dprob = dot_nt(values, grads[h])
            dscore = (probs * (dprob - deltas[h])).astype(BF)
            dv = dot_nn(probs.astype(BF), grads[h])
            dk = dot_nn(dscore, queries[h])
            for n, block in enumerate(pair):
                sum_ref[block, :, k_cols] += dk[n * tile_rows : (n + 1) * tile_rows]
                sum_ref[block, :, v_cols] += dv[n * tile_rows : (n + 1) * tile_rows]
            dq_sum_ref[h] += dot_tn(dscore, keys)
        return carry

    lax.fori_loop(0, jnp.where(start < length, start // tile_rows // 2 + 1, 0), body, 0)
    for h in range(kv_heads):
        for g in range(per_key):
            head = h * per_key + g
            dq_ref[0, :, 0, :, head * HD : (head + 1) * HD] = (
                dq_sum_ref[h, g * tile_rows : (g + 1) * tile_rows] * score_scale
            ).reshape(-1, piece, HD)

    @pl.when(tile == pl.num_programs(0) - 1)
    def _():
        for kc in range(dkv_ref.shape[0]):
            for kfb in range(2):
                for kz in range(blocks):
                    block = (kc * 2 + kfb) * blocks + kz
                    dkv_ref[kc, kfb, :, kz, :, :kv_width] = (
                        (sum_ref[block, :, :kv_width] * score_scale).astype(BF).reshape(-1, piece, kv_width)
                    )
                    dkv_ref[kc, kfb, :, kz, :, kv_width:] = (
                        sum_ref[block, :, kv_width:].astype(BF).reshape(-1, piece, kv_width)
                    )


def attention_specs(queries, kv_all):
    halves, per_block, blocks, piece, q_width = queries.shape
    tile_spec = pl.BlockSpec((1, per_block, 1, piece, q_width), lambda t, meta: (t // blocks, 0, t % blocks, 0, 0))
    kv_spec = pl.BlockSpec(kv_all.shape, lambda t, meta: (0,) * 6)
    kv_heads = kv_all.shape[-1] // (2 * HD)
    per_key = q_width // HD // kv_heads
    lse_spec = pl.BlockSpec((1, kv_heads, 1, per_key * per_block * piece), lambda t, meta: (t, 0, 0, 0))
    sizes = dict(kv_heads=kv_heads, per_key=per_key, blocks=blocks, piece=piece)
    return halves * blocks, tile_spec, kv_spec, lse_spec, sizes, per_block * piece


def attention_forward(meta, queries, kv_all):
    tiles, tile_spec, kv_spec, lse_spec, sizes, tile_rows = attention_specs(queries, kv_all)
    kv_heads, per_key = sizes["kv_heads"], sizes["per_key"]
    stacked = per_key * tile_rows
    pairs = tiles * kv_heads * stacked * tiles * 2 * tile_rows // 2
    return pl.pallas_call(
        functools.partial(attn_fwd_kernel, **sizes),
        grid_spec=pltpu.PrefetchScalarGridSpec(
            num_scalar_prefetch=1,
            grid=(tiles,),
            in_specs=[tile_spec, kv_spec],
            out_specs=[tile_spec, lse_spec],
            scratch_shapes=[
                pltpu.VMEM((kv_heads, stacked, HD), F32),
                pltpu.VMEM((kv_heads, stacked, HD), F32),
            ],
        ),
        out_shape=[
            jax.ShapeDtypeStruct(queries.shape, BF),
            jax.ShapeDtypeStruct((tiles, kv_heads, 1, stacked), F32),
        ],
        cost_estimate=pl.CostEstimate(flops=pairs * HD * 4, transcendentals=pairs, bytes_accessed=4 * kv_all.size),
    )(meta, queries, kv_all)


def attention_backward(meta, queries, kv_all, dmix, mixture, logs):
    tiles, tile_spec, kv_spec, lse_spec, sizes, tile_rows = attention_specs(queries, kv_all)
    kv_heads, per_key = sizes["kv_heads"], sizes["per_key"]
    stacked = per_key * tile_rows
    key_blocks = kv_all.shape[0] * tiles
    pairs = tiles * kv_heads * stacked * tiles * 2 * tile_rows // 2
    return pl.pallas_call(
        functools.partial(attn_bwd_kernel, **sizes),
        grid_spec=pltpu.PrefetchScalarGridSpec(
            num_scalar_prefetch=1,
            grid=(tiles,),
            in_specs=[tile_spec, kv_spec, tile_spec, tile_spec, lse_spec],
            out_specs=[tile_spec, kv_spec],
            scratch_shapes=[
                pltpu.VMEM((key_blocks, tile_rows, kv_all.shape[-1]), F32),
                pltpu.VMEM((kv_heads, stacked, HD), F32),
            ],
        ),
        out_shape=[
            jax.ShapeDtypeStruct(queries.shape, F32),
            jax.ShapeDtypeStruct(kv_all.shape, BF),
        ],
        cost_estimate=pl.CostEstimate(flops=pairs * HD * 10, transcendentals=pairs, bytes_accessed=10 * kv_all.size),
    )(meta, queries, kv_all, dmix, mixture, logs)


def turned(values):
    return pltpu.roll(values, HD // 2, axis=1)


def project_kernel(
    x_ref, gain_ref, w_ref, cos_ref, sin_ref, q_gain_ref, k_gain_ref, normed_ref, proj_ref, q_ref, kv_ref, *, kv_width
):
    q_width = q_ref.shape[1]
    normed_ref[...] = rms_scale(x_ref[...].astype(F32), gain_ref[...]).astype(BF)
    proj = dot_nn(normed_ref[...], w_ref[...])
    proj_ref[...] = proj[:, : q_width + kv_width]
    cosine, sine = cos_ref[...], sin_ref[...]
    for at in range(0, q_width + kv_width, HD):
        gain = q_gain_ref[...] if at < q_width else k_gain_ref[...]
        normed = rms_scale(proj[:, at : at + HD], gain)
        rotated = (normed * cosine + turned(normed) * sine).astype(BF)
        if at < q_width:
            q_ref[:, at : at + HD] = rotated
        else:
            kv_ref[:, at - q_width : at - q_width + HD] = rotated
    kv_ref[:, kv_width:] = proj[:, q_width + kv_width :].astype(BF)


def project(x_all, attn_gain, w_qkv, cosine, sine, q_gain, k_gain, kv_width):
    tokens, width = x_all.shape
    columns = w_qkv.shape[1]
    q_width = columns - 2 * kv_width
    tile = min(256, tokens)

    def rows(n):
        return pl.BlockSpec((tile, n), lambda i: (i, 0))

    def whole(*shape):
        return pl.BlockSpec(shape, lambda i: (0, 0))

    return pl.pallas_call(
        functools.partial(project_kernel, kv_width=kv_width),
        grid=(tokens // tile,),
        in_specs=[rows(width), whole(1, width), whole(width, columns), rows(HD), rows(HD), whole(1, HD), whole(1, HD)],
        out_specs=[rows(width), rows(q_width + kv_width), rows(q_width), rows(2 * kv_width)],
        out_shape=[
            jax.ShapeDtypeStruct((tokens, width), BF),
            jax.ShapeDtypeStruct((tokens, q_width + kv_width), F32),
            jax.ShapeDtypeStruct((tokens, q_width), BF),
            jax.ShapeDtypeStruct((tokens, 2 * kv_width), BF),
        ],
        cost_estimate=pl.CostEstimate(
            flops=2 * tokens * width * columns, transcendentals=0, bytes_accessed=8 * tokens * width
        ),
    )(x_all, attn_gain[None], w_qkv, cosine, sine, q_gain[None], k_gain[None])


def unproject_kernel(
    dq_ref, dkv_ref, other_ref, proj_ref, cos_ref, sin_ref, q_gain_ref, k_gain_ref, dqkv_ref, dgain_ref, *, kv_width
):
    q_width = dq_ref.shape[1]

    @pl.when(pl.program_id(0) == 0)
    def _():
        dgain_ref[...] = jnp.zeros_like(dgain_ref)

    cosine, sine = cos_ref[...], sin_ref[...]
    dkv = dkv_ref[...].astype(F32) + other_ref[...].astype(F32)
    for at in range(0, q_width + kv_width, HD):
        is_q = at < q_width
        grad = dq_ref[:, at : at + HD] if is_q else dkv[:, at - q_width : at - q_width + HD]
        gain = q_gain_ref[...] if is_q else k_gain_ref[...]
        values = proj_ref[:, at : at + HD]
        inverse = lax.rsqrt(jnp.mean(values * values, axis=1, keepdims=True) + EPS)
        dnormed = grad * cosine + turned(grad * sine)
        n = 0 if is_q else 1
        dgain_ref[n : n + 1] += jnp.sum(dnormed * values * inverse, axis=0, keepdims=True)
        scaled = dnormed * gain
        inner = jnp.mean(scaled * values, axis=1, keepdims=True)
        dqkv_ref[:, at : at + HD] = (inverse * scaled - values * (inverse * inverse * inverse * inner)).astype(BF)
    dqkv_ref[:, q_width + kv_width :] = dkv[:, kv_width:].astype(BF)


def unproject(dq, dkv, other, proj, cosine, sine, q_gain, k_gain):
    tokens, q_width = dq.shape
    kv_width = dkv.shape[1] // 2
    columns = q_width + 2 * kv_width
    tile = min(256, tokens)

    def rows(n):
        return pl.BlockSpec((tile, n), lambda i: (i, 0))

    def whole(*shape):
        return pl.BlockSpec(shape, lambda i: (0, 0))

    return pl.pallas_call(
        functools.partial(unproject_kernel, kv_width=kv_width),
        grid=(tokens // tile,),
        in_specs=[
            rows(q_width),
            rows(2 * kv_width),
            rows(2 * kv_width),
            rows(q_width + kv_width),
            rows(HD),
            rows(HD),
            whole(1, HD),
            whole(1, HD),
        ],
        out_specs=[rows(columns), whole(2, HD)],
        out_shape=[jax.ShapeDtypeStruct((tokens, columns), BF), jax.ShapeDtypeStruct((2, HD), F32)],
        cost_estimate=pl.CostEstimate(
            flops=30 * tokens * columns, transcendentals=0, bytes_accessed=12 * tokens * columns
        ),
    )(dq, dkv, other, proj, cosine, sine, q_gain[None], k_gain[None])


def together(*values):
    return lax.optimization_barrier(values)


def per_device(
    layer_input,
    lengths,
    order,
    offsets,
    attn_gain,
    w_query,
    w_key,
    w_value,
    q_gain,
    k_gain,
    w_out,
    mlp_gain,
    w_gate,
    w_up,
    w_down,
    grad_out,
):
    groups, ring = lax.axis_size("fsdp"), lax.axis_size("ctx")
    _, rows, width = layer_input.shape
    lanes = ring // groups
    piece, block_rows = rows // groups, rows // 2
    per_block = block_rows // piece
    heads, kv_heads = H // groups, KVH // groups
    q_width, kv_width = heads * HD, kv_heads * HD
    shard_rows = w_query.shape[0]
    hidden = w_gate.shape[1] // groups
    own = lax.axis_index("fsdp")
    own_ctx = lax.axis_index("ctx")
    plane, lane = own_ctx // lanes, own_ctx % lanes
    steps = range(groups)
    tokens = groups * rows

    def swap(block, step):
        if step == 0:
            return block
        return lax.ppermute(block, "fsdp", [(i, i ^ step) for i in range(groups)])

    def swap_plane(block, step):
        if step == 0:
            return block
        return lax.ppermute(block, "ctx", [(i, (i // lanes ^ step) * lanes + i % lanes) for i in range(ring)])

    def swap_lane(block, step):
        if step == 0:
            return block
        return lax.ppermute(block, "ctx", [(i, i // lanes * lanes + (i % lanes ^ step)) for i in range(ring)])

    def gather_all(part):
        for axis, index, count in (("ctx", own_ctx, ring), ("fsdp", own, groups)):
            step = 1
            while step < count:
                other = lax.ppermute(part, axis, [(i, i ^ step) for i in range(count)])
                low = (index & step) == 0
                part = jnp.concatenate([jnp.where(low, part, other), jnp.where(low, other, part)], axis=0)
                step *= 2
        return part

    def scatter_all(part):
        for axis, index, count in (("fsdp", own, groups), ("ctx", own_ctx, ring)):
            step = count // 2
            while step:
                half = part.shape[0] // 2
                low = (index & step) == 0
                kept = jnp.where(low, part[:half], part[half:])
                sent = jnp.where(low, part[half:], part[:half])
                part = kept + lax.ppermute(sent, axis, [(i, i ^ step) for i in range(count)])
                step //= 2
        return part

    def to_pieces(local):
        pieces = local.reshape(groups, piece, width)
        return jnp.stack([swap(pick(pieces, own ^ k), k) for k in steps])

    def to_plane(spread, holder):
        mine = [swap_plane(pick(spread, own ^ holder[plane ^ k]), k) for k in steps]
        return jnp.concatenate(mine, axis=0)

    def leave_plane(mine):
        return jnp.stack([swap_plane(mine[k], k) for k in steps])

    def from_plane(spread, held):
        back = jnp.stack([swap(pick(spread, plane ^ held[own ^ k]), k) for k in steps])
        return xor_order(back, own).reshape(1, rows, width)

    small = jnp.concatenate(
        [
            attn_gain.astype(F32),
            mlp_gain.astype(F32),
            q_gain.astype(F32),
            k_gain.astype(F32),
            lengths.astype(F32),
            order.astype(F32),
            offsets.reshape(-1).astype(F32),
        ]
    )[None, :]
    small_all = gather_all(small)
    spread, w_query, w_key, w_value = together(to_pieces(layer_input[0]), w_query, w_key, w_value)
    x_own = to_plane(spread, jnp.arange(groups, dtype=jnp.int32))
    x_own, small_all = together(x_own, small_all)
    gain_rows, head_rows = attn_gain.shape[0], q_gain.shape[0]
    at = 0
    attn_gain_full = small_all[:, at : at + gain_rows].reshape(-1)
    at += gain_rows
    mlp_gain_full = small_all[:, at : at + gain_rows].reshape(-1)
    at += gain_rows
    q_gain_full = small_all[:, at : at + head_rows].reshape(-1)
    at += head_rows
    k_gain_full = small_all[:, at : at + head_rows].reshape(-1)
    at += head_rows
    whole = small_all[:, at:].astype(jnp.int32).reshape(groups, ring, 4)
    lengths_all = whole[:, 0, 0]
    order_all = whole[:, 0, 1]
    each = jnp.arange(groups, dtype=jnp.int32)
    slot_of = jnp.sum(jnp.where(order_all[None, :] == each[:, None], each[None, :], 0), axis=1)
    length = pick(lengths_all, plane)
    starts = pick(whole[:, :, 2:4], plane).reshape(groups, lanes, 2)
    starts = jnp.transpose(xor_order(starts, plane), (1, 2, 0))
    starts = jnp.transpose(xor_order(starts, lane), (1, 0, 2))
    starts = jnp.transpose(xor_order(starts, own // per_block), (1, 0, 2))
    flip = own % per_block
    tile_starts = starts[0].reshape(-1)
    block_starts = starts.reshape(-1)
    block_ids = jnp.arange(block_starts.shape[0], dtype=jnp.int32)
    block_at = jnp.sum(
        jnp.where(block_starts[None, :] == (block_ids * block_rows)[:, None], block_ids[None, :], 0), axis=1
    )
    meta = jnp.concatenate([length[None], flip[None].astype(jnp.int32), tile_starts, block_at])
    within = jnp.arange(block_rows, dtype=jnp.int32) ^ (flip * piece)
    positions = (
        starts[0][:, None, :, None] + within.reshape(1, per_block, 1, piece)
    ).reshape(groups, rows)
    valid_own = positions[0] < length

    def to_columns(parts):
        out = jnp.zeros((groups, shard_rows, sum(p.shape[1] for p in parts) // groups), BF)
        for k in steps:
            piece_k = jnp.concatenate(
                [
                    lax.dynamic_slice_in_dim(p, (own ^ k) * (p.shape[1] // groups), p.shape[1] // groups, 1)
                    for p in parts
                ],
                axis=1,
            )
            out = lax.dynamic_update_index_in_dim(out, swap(piece_k, k), own ^ k, 0)
        return out

    def from_columns(grad, widths):
        outs = [jnp.zeros((shard_rows, w * groups), F32) for w in widths]
        for k in steps:
            piece_k = swap(pick(grad, own ^ k), k).astype(F32)
            at = 0
            for n, w in enumerate(widths):
                outs[n] = lax.dynamic_update_slice_in_dim(outs[n], piece_k[:, at : at + w], (own ^ k) * w, 1)
                at += w
        return outs

    qkv_local = to_columns([w_query, w_key, w_value])
    qkv_local, x_own = together(qkv_local, x_own)
    w_qkv = lax.all_gather(qkv_local, "ctx", axis=1, tiled=True).reshape(width, -1)
    w_out_full = lax.all_gather(w_out, "ctx", axis=0, tiled=True)
    x_all = jnp.concatenate([swap(x_own, k) for k in steps], axis=0)
    cosine, sine = rope_tables(positions.reshape(-1))
    normed_one, proj, query_rot, kv_rot = project(
        x_all, attn_gain_full, w_qkv, cosine, sine, q_gain_full, k_gain_full, kv_width
    )
    w_gate, w_up, grad_out, normed_one = together(w_gate, w_up, grad_out, normed_one)
    gate_up_local = to_columns([w_gate, w_up])
    w_gate_up = lax.all_gather(gate_up_local, "ctx", axis=1, tiled=True).reshape(width, -1)
    w_down_full = lax.all_gather(w_down, "ctx", axis=0, tiled=True)
    tile_shape = (2, per_block, groups, piece, -1)
    queries = query_rot.reshape(tile_shape)
    kv_own = kv_rot.reshape(tile_shape)
    kv_all = jnp.stack([swap_lane(kv_own, k) for k in range(lanes)])
    mixture, logs = attention_forward(meta, queries, kv_all)
    mix_b = mixture.reshape(tokens, -1)
    attn_part = dot_nn(mix_b, w_out_full).reshape(groups, rows, width)
    hidden_res = x_own.astype(F32) + attn_part[0]
    for k in steps[1:]:
        hidden_res = hidden_res + swap(attn_part[k].astype(BF), k).astype(F32)
    normed_two_own = rms_scale(hidden_res, mlp_gain_full).astype(BF)
    normed_two = jnp.concatenate([swap(normed_two_own, k) for k in steps], axis=0)
    dy_own = to_plane(to_pieces(grad_out[0]), slot_of)
    dy_own = jnp.where(valid_own[:, None], dy_own, jnp.zeros((), BF))
    gate_up, dy_own = together(dot_nn(normed_two, w_gate_up), dy_own)
    gate_proj, up_proj = gate_up[:, :hidden], gate_up[:, hidden:]
    hidden_act = (jax.nn.silu(gate_proj) * up_proj).astype(BF)

    dy_b = jnp.concatenate([swap(dy_own, k) for k in steps], axis=0)
    grad_down_part, dy_after = together(dot_tn(hidden_act, dy_b).astype(BF), dy_b)
    grad_down = lax.psum_scatter(grad_down_part, "ctx", scatter_dimension=0, tiled=True)
    dhid = dot_nt(dy_after, w_down_full)
    _, swiglu_pull = jax.vjp(lambda g, u: jax.nn.silu(g) * u, gate_proj, up_proj)
    dgate_f, dup_f = swiglu_pull(dhid)
    dgate, dup = dgate_f.astype(BF), dup_f.astype(BF)
    dn_two_part = dot_nt(jnp.concatenate([dgate, dup], axis=1), w_gate_up).reshape(groups, rows, width)
    dn_two_part, normed_two = together(dn_two_part, normed_two)
    dn_two = dn_two_part[0]
    for k in steps[1:]:
        dn_two = dn_two + swap(dn_two_part[k].astype(BF), k).astype(F32)
    grad_gate = lax.psum_scatter(
        dot_tn(normed_two, dgate).astype(BF).reshape(groups, -1, hidden), "ctx", scatter_dimension=1, tiled=True
    )
    grad_up = lax.psum_scatter(
        dot_tn(normed_two, dup).astype(BF).reshape(groups, -1, hidden), "ctx", scatter_dimension=1, tiled=True
    )
    dn_two, grad_down = together(dn_two, grad_down)
    _, norm_two_pull = jax.vjp(rms_scale, hidden_res, mlp_gain_full)
    dh_norm, dmlp_gain_part = norm_two_pull(dn_two)
    dh_rows = dy_own.astype(F32) + dh_norm
    dattn_own = dh_rows.astype(BF)
    dattn_b = jnp.concatenate([swap(dattn_own, k) for k in steps], axis=0)
    out_part = dot_nn(hidden_act, w_down_full).reshape(groups, rows, width)
    out_sent = [out_part[k].astype(BF) for k in steps[1:]]
    dattn_b, grad_gate = together(dattn_b, grad_gate)
    dmix_b = dot_nt(dattn_b, w_out_full).astype(BF)
    dmix_b, grad_out_part, *out_sent = together(dmix_b, dot_tn(mix_b, dattn_b).astype(BF), *out_sent)
    grad_out_w = lax.psum_scatter(grad_out_part, "ctx", scatter_dimension=0, tiled=True)

    dq_rot, dkv_parts = attention_backward(meta, queries, kv_all, dmix_b.reshape(queries.shape), mixture, logs)
    result, dq_rot = together(out_part[0] + hidden_res, dq_rot)
    for k in steps[1:]:
        result = result + swap(out_sent[k - 1], k).astype(F32)
    result = result.astype(BF)
    dkv_parts = dkv_parts.reshape(lanes, tokens, -1)
    other = swap_lane(dkv_parts[1], 1)
    for k in range(2, lanes):
        other = other + swap_lane(dkv_parts[k], k)
    dqkv, dhead_gains = unproject(
        dq_rot.reshape(tokens, -1), dkv_parts[0], other, proj, cosine, sine, q_gain_full, k_gain_full
    )

    dqkv, grad_up, result = together(dqkv, grad_up, result)
    grad_qkv_part = dot_tn(normed_one, dqkv).astype(BF).reshape(groups, -1, dqkv.shape[1])
    grad_qkv = lax.psum_scatter(grad_qkv_part, "ctx", scatter_dimension=1, tiled=True)
    dn_one_part = dot_nt(dqkv, w_qkv).reshape(groups, rows, width)
    dn_one = dn_one_part[0]
    for k in steps[1:]:
        dn_one = dn_one + swap(dn_one_part[k].astype(BF), k).astype(F32)
    result = leave_plane(result.reshape(groups, piece, width))
    dn_one, grad_out_w, result = together(dn_one, grad_out_w, result)
    result = from_plane(result, order_all)
    _, norm_one_pull = jax.vjp(rms_scale, x_own.astype(F32), attn_gain_full)
    dflat_norm, dattn_gain_part = norm_one_pull(dn_one)
    spread = leave_plane((dh_rows + dflat_norm).astype(BF).reshape(groups, piece, width))
    grad_w_query, grad_w_key, grad_w_value = from_columns(grad_qkv, [q_width, kv_width, kv_width])
    spread, grad_w_query = together(spread, grad_w_query)
    grad_x = from_plane(spread, each)

    devices = groups * ring
    gains = jnp.concatenate(
        [
            dattn_gain_part.reshape(devices, -1),
            dmlp_gain_part.reshape(devices, -1),
            dhead_gains[0].reshape(devices, -1),
            dhead_gains[1].reshape(devices, -1),
        ],
        axis=1,
    )
    gains = scatter_all(gains)[0]
    grad_attn_gain = gains[:gain_rows]
    grad_mlp_gain = gains[gain_rows : 2 * gain_rows]
    grad_q_gain = gains[2 * gain_rows : 2 * gain_rows + head_rows]
    grad_k_gain = gains[2 * gain_rows + head_rows :]
    (grad_w_gate,) = from_columns(grad_gate, [hidden])
    (grad_w_up,) = from_columns(grad_up, [hidden])
    return (
        result,
        grad_x,
        grad_attn_gain,
        grad_w_query,
        grad_w_key,
        grad_w_value,
        grad_q_gain,
        grad_k_gain,
        grad_out_w.astype(F32),
        grad_mlp_gain,
        grad_w_gate,
        grad_w_up,
        grad_down.astype(F32),
    )


def solution(mesh):
    rows = P(("fsdp", "ctx"), None)
    vector = P(("fsdp", "ctx"))
    tokens = P("fsdp", "ctx", None)
    return jax.shard_map(
        per_device,
        mesh=mesh,
        in_specs=(
            tokens,
            P("fsdp"),
            P("fsdp"),
            P("fsdp", "ctx"),
            vector,
            rows,
            rows,
            rows,
            vector,
            vector,
            rows,
            vector,
            rows,
            rows,
            rows,
            tokens,
        ),
        out_specs=(
            tokens,
            tokens,
            vector,
            rows,
            rows,
            rows,
            vector,
            vector,
            rows,
            vector,
            rows,
            rows,
            rows,
        ),
        check_vma=False,
    )
```

time: 1120 us -> 825 us (0.74)
  blocking collectives: 142 us -> 0 us
  matrix products: 234 us -> 130 us
  waiting for transfers between devices: 436 us -> 342 us
  starting transfers between devices: 46.2 us -> 136 us
  local copies, waits for them, and re-layouts: 108 us -> 40.4 us
  Pallas kernels: 0 us -> 56.8 us
  other arithmetic: 123 us -> 84.7 us
    unnamed x2 -> x0, blocking collectives: 142 us -> none
    reduce_scatter x5, waiting for transfers between devices: 117 us -> 0.03 us  [the longest x1 0.02 us: per_device(): lax.psum_scatter(dot_tn(normed_two, dup).astype(BF).reshape(groups, -1, h...]
    dot_general x6 -> x0, matrix products: 93.6 us -> none  [the longest x1 23.7 us: per_device(): jnp.einsum('srkgd,stkd->skgrt', dmix_heads, values, preferred_element_typ...]
    ppermute x36 -> x75, starting transfers between devices: 45.8 us -> 135 us  [the longest x51 61.6 us: swap(): return lax.ppermute(block, 'fsdp', [(i, i ^ step) for i in range(groups)])]
    ppermute x36 -> x75, waiting for transfers between devices: 275 us -> 337 us  [the longest x51 274 us: swap(): return lax.ppermute(block, 'fsdp', [(i, i ^ step) for i in range(groups)])]
    pallas_call x0 -> x4, Pallas kernels: none -> 56.8 us  [the longest x1 21.2 us: attention_forward(): pl.pallas_call(functools.partial(attn_fwd_kernel, **sizes), grid_spec=plt...]
    all_gather x1 -> x0, waiting for transfers between devices: 42.2 us -> none  [per_device(): lax.all_gather(jnp.concatenate([key_rot, value_b], axis=2), 'ctx', axis=1...]
    reshape x10 -> x5, local copies, waits for them, and re-layouts: 31.6 us -> 0.46 us  [the longest x3 0.26 us: per_device(): starts = pick(whole[:, :, 2:4], plane).reshape(groups, lanes, 2)]
  transfers between devices with their start and end apart: 46 -> 84, of which waited for: 26 -> 41; matrix products, arithmetic and copies ran while one was open for 24% -> 29% of each run, Pallas kernels for 0% -> 7%
where the time goes in v2:
time: 825 us; the launch traced here: 812 us
  waiting for transfers between devices  342 us (41%)
  starting transfers between devices  136 us (16%)
  matrix products  130 us (16%)
  other arithmetic  84.7 us (10%)
  Pallas kernels  56.8 us (7%)
  local copies, waits for them, and re-layouts  40.4 us (5%)
  between operations  22 us (3%)
    ppermute x51, waiting for transfers between devices, swap(): return lax.ppermute(block, 'fsdp', [(i, i ^ step) for i in range(groups)])  274 us
    ppermute x51, starting transfers between devices, swap(): return lax.ppermute(block, 'fsdp', [(i, i ^ step) for i in range(groups)])  61.6 us
    ppermute x12, waiting for transfers between devices, swap_plane(): lax.ppermute(block, 'ctx', [(i, (i // lanes ^ step) * lanes + i % lanes)...  52 us
    ppermute x12, starting transfers between devices, swap_plane(): lax.ppermute(block, 'ctx', [(i, (i // lanes ^ step) * lanes + i % lanes)...  49.5 us
    dot_general x4, matrix products, dot_nt(): lax.dot_general(left, right, (((1,), (1,)), ((), ())), preferred_element_...  48.3 us
    dot_general x5, matrix products, dot_tn(): lax.dot_general(left, right, (((0,), (0,)), ((), ())), preferred_element_...  44.9 us
    dot_general x3, matrix products, dot_nn(): lax.dot_general(left, right, (((1,), (0,)), ((), ())), preferred_element_...  36.9 us
    pallas_call x1, Pallas kernels, attention_forward(): pl.pallas_call(functools.partial(attn_fwd_kernel, **sizes), grid_spec=plt...  21.2 us
  transfers between devices with their start and end apart: 84, of which 41 were waited for; matrix products, arithmetic and copies ran while one was open for 29% of the time, Pallas kernels for 7%

profile of v2, /device:TPU:0, one launch (start us, length us, event | category | flops | bytes accessed | tf_op | source)
XLA Modules:
  0.0 812.2 jit_solution(18275741516403400187)
XLA Ops:
  13.3 3.0 collective-permute-start.10
  17.8 3.1 collective-permute-start.11
  33.1 4.0 collective-permute-done
  37.1 4.1 collective-permute-done.1
  48.3 4.2 collective-permute-done.3
  54.0 3.5 collective-permute-done.4
  57.5 3.6 collective-permute-done.7
  75.9 14.9 %collective-permute-done.14 = bf16[256,2048]{1,0:T(8,128)(2,1)S(1)} collective-permute-done((bf16[256,2048]{1,0:T(8,128)(2,1)S(1)}, bf16[256,2048]{1,0:T(8,128)(2,1)S(1)}, u32[]{:S(2)}, u32[]{:S(2)}) %collective-permute-start.14) | collective-permute-done | bytes 1048608 | tf_op jit(solution)/shard_map/ppermute | solution.py:401
  90.8 13.0 %collective-permute-done.16 = bf16[256,2048]{1,0:T(8,128)(2,1)} collective-permute-done((bf16[256,2048]{1,0:T(8,128)(2,1)S(1)}, bf16[256,2048]{1,0:T(8,128)(2,1)}, u32[]{:S(2)}, u32[]{:S(2)}) %collective-permute-start.16) | collective-permute-done | bytes 1048608 | tf_op jit(solution)/shard_map/ppermute | solution.py:401
  103.7 3.4 pad_maximum_fusion.1.x_ref
  107.1 3.7 all-gather.5.cloned.1.call-done
  110.9 11.2 %shard_map.255 = (bf16[1024,2048]{1,0:T(8,128)(2,1)}, f32[1024,768]{1,0:T(8,128)}, bf16[1024,512]{1,0:T(8,128)(2,1)}, bf16[1024,512]{1,0:T(8,128)(2,1)}) custom-call(bf16[1024,2048]{1,0:T(8,128)(2,1)} %pad_maximum_fusion.1.x_ref, f32[1,2048]{1,0:T(1,128)} %broadcast_in_dim_reshape.6.gain_ref, bf16[2048,1024]{1,0:T(8,128)(2,1)} %bitcast.294, ...), custom_call_target="tpu_custom_call" | custom-call | flops 4294967296 | bytes 16777216 | tf_op jit(solution)/shard_map/pallas_call | solution.py:285
  126.2 8.1 collective-permute-done.24
  134.3 9.0 %collective-permute-done.25 = bf16[64,3072]{1,0:T(8,128)(2,1)S(1)} collective-permute-done((bf16[64,3072]{1,0:T(8,128)(2,1)S(1)}, bf16[64,3072]{1,0:T(8,128)(2,1)S(1)}, u32[]{:S(2)}, u32[]{:S(2)}) %collective-permute-start.25) | collective-permute-done | bytes 393248 | tf_op jit(solution)/shard_map/ppermute | solution.py:401
  150.4 21.2 %shard_map.256 = (bf16[2,2,4,64,512]{4,3,2,1,0:T(8,128)(2,1)}, f32[8,2,1,256]{3,2,1,0:T(1,128)}) custom-call(s32[26]{0:T(128)} %pad_add_fusion.2.meta, bf16[2,2,4,64,512]{4,3,2,1,0:T(8,128)(2,1)} %bitcast.296, bf16[2,2,2,4,64,512]{5,4,3,2,1,0:T(8,128)(2,1)} %pad_maximum_fusion.4.kv_ref), custom_call_target="tpu_custom_call" | custom-call | flops 2147483648 | bytes 4194304 | tf_op jit(solution)/shard_map/pallas_call | solution.py:204
  171.6 7.6 fusion.50
  187.2 46.0 %collective-permute-done.27 = bf16[64,2048]{1,0:T(8,128)(2,1)S(1)} collective-permute-done((bf16[64,2048]{1,0:T(8,128)(2,1)S(1)}, bf16[64,2048]{1,0:T(8,128)(2,1)S(1)}, u32[]{:S(2)}, u32[]{:S(2)}) %collective-permute-start.27) | collective-permute-done | bytes 262176 | tf_op jit(solution)/shard_map/ppermute | solution.py:401
  244.1 3.5 multiply_reduce_fusion.2
  252.4 7.4 collective-permute-start.30
  261.4 9.3 %collective-permute-done.30 = bf16[64,2048]{1,0:T(8,128)(2,1)S(1)} collective-permute-done((bf16[64,2048]{1,0:T(8,128)(2,1)S(1)}, bf16[64,2048]{1,0:T(8,128)(2,1)S(1)}, u32[]{:S(2)}, u32[]{:S(2)}) %collective-permute-start.30) | collective-permute-done | bytes 262176 | tf_op jit(solution)/shard_map/ppermute | solution.py:406
  271.6 14.6 %collective-permute-done.32 = bf16[64,2048]{1,0:T(8,128)(2,1)} collective-permute-done((bf16[64,2048]{1,0:T(8,128)(2,1)S(1)}, bf16[64,2048]{1,0:T(8,128)(2,1)}, u32[]{:S(2)}, u32[]{:S(2)}) %collective-permute-start.32) | collective-permute-done | bytes 262176 | tf_op jit(solution)/shard_map/ppermute | solution.py:406
  287.6 7.2 collective-permute-done.23
  294.9 17.1 %fusion.31 = f32[1024,3072]{1,0:T(8,128)S(1)} fusion(bf16[2048,3072]{1,0:T(8,128)(2,1)} %bitcast.292, bf16[256,2048]{1,0:T(8,128)(2,1)} %collective-permute-done.23, bf16[256,2048]{1,0:T(8,128)(2,1)} %collective-permute-done.22, bf16[256,2048]{1,0:T(8,128)(2,1)} %collective-permute-done.21, bf16[256,2048]{1,0:T(8,128)(2,1)} %multiply_convert_fusion.2), kind=kOutput, calls=%fused_computation.241 | convolution fusion | flops 12901679104 | bytes 29360128 | tf_op jit(solution)/shard_map/dot_general | solution.py:35
  317.6 20.5 %collective-permute-done.33 = bf16[256,2048]{1,0:T(8,128)(2,1)S(1)} collective-permute-done((bf16[256,2048]{1,0:T(8,128)(2,1)S(1)}, bf16[256,2048]{1,0:T(8,128)(2,1)S(1)}, u32[]{:S(2)}, u32[]{:S(2)}) %collective-permute-start.33) | collective-permute-done | bytes 1048608 | tf_op jit(solution)/shard_map/ppermute | solution.py:401
  338.4 17.6 %collective-permute-done.35 = bf16[256,2048]{1,0:T(8,128)(2,1)S(1)} collective-permute-done((bf16[256,2048]{1,0:T(8,128)(2,1)S(1)}, bf16[256,2048]{1,0:T(8,128)(2,1)S(1)}, u32[]{:S(2)}, u32[]{:S(2)}) %collective-permute-start.35) | collective-permute-done | bytes 1048608 | tf_op jit(solution)/shard_map/ppermute | solution.py:401
  358.2 8.8 %convolution_convert_fusion.2 = bf16[1536,2048]{1,0:T(8,128)(2,1)} fusion(bf16[1024,1536]{1,0:T(8,128)(2,1)S(1)} %multiply_convert_fusion.1, bf16[1024,2048]{1,0:T(8,128)(2,1)S(1)} %constant_dynamic-update-slice_fusion), kind=kOutput, calls=%fused_computation.3 | convolution fusion | flops 6445596672 | bytes 13631488 | tf_op jit(solution)/shard_map/dot_general | solution.py:43
  367.1 4.3 pad_maximum_fusion.2
  371.4 15.6 %fusion.2 = (bf16[1024,1536]{1,0:T(8,128)(2,1)}, bf16[1024,1536]{1,0:T(8,128)(2,1)S(1)}) fusion(f32[1024,3072]{1,0:T(8,128)} %copy-done.4, bf16[1024,2048]{1,0:T(8,128)(2,1)} %copy-done.25, bf16[1536,2048]{1,0:T(8,128)(2,1)} %all-gather.11.cloned.1.call-done), kind=kOutput, calls=%fused_computation.6 | convolution fusion | flops 6464471040 | bytes 29360128 | tf_op jit(solution)/shard_map/dot_general | solution.py:39
  387.0 4.0 pad_maximum_fusion
  391.1 17.3 %fusion.53 = f32[4,256,2048]{2,1,0:T(8,128)} fusion(bf16[4,256,3072]{2,1,0:T(8,128)(2,1)S(1)} %bitcast.258, bf16[2048,3072,1]{1,0,2:T(8,128)(2,1)} %bitcast.293), kind=kOutput, calls=%fused_computation.262 | convolution fusion | flops 12884901888 | bytes 27262976 | tf_op jit(solution)/shard_map/dot_general | solution.py:39
  408.3 8.7 %convolution_convert_fusion.1 = bf16[2048,1536]{1,0:T(8,128)(2,1)} fusion(bf16[1024,2048]{1,0:T(8,128)(2,1)S(1)} %copy-done.7, bf16[1024,1536]{1,0:T(8,128)(2,1)S(1)} %copy-done.9), kind=kOutput, calls=%fused_computation.2 | convolution fusion | flops 6445596672 | bytes 13631488 | tf_op jit(solution)/shard_map/dot_general | solution.py:43
  417.1 11.7 %convolution_convert_fusion = bf16[2048,1536]{1,0:T(8,128)(2,1)} fusion(bf16[1024,2048]{1,0:T(8,128)(2,1)} %pad_maximum_fusion.2, bf16[1024,1536]{1,0:T(8,128)(2,1)} %copy-done.8), kind=kOutput, calls=%fused_computation.1 | convolution fusion | flops 6445596672 | bytes 13631488 | tf_op jit(solution)/shard_map/dot_general | solution.py:43
  428.9 4.1 convert.24
  436.9 12.2 %fusion.51 = (bf16[1024,2048]{1,0:T(8,128)(2,1)}, f32[1024,2048]{1,0:T(8,128)}) fusion(bf16[1024,1536]{1,0:T(8,128)(2,1)S(1)} %copy-done.11, bf16[1536,2048]{1,0:T(8,128)(2,1)} %all-gather.11.cloned.1.call-done), kind=kOutput, calls=%fused_computation.260 | convolution fusion | flops 6444548096 | bytes 22020096 | tf_op jit(solution)/shard_map/dot_general | solution.py:35
  449.2 10.3 %collective-permute-done.36 = bf16[256,2048]{1,0:T(8,128)(2,1)S(1)} collective-permute-done((bf16[256,2048]{1,0:T(8,128)(2,1)S(1)}, bf16[256,2048]{1,0:T(8,128)(2,1)S(1)}, u32[]{:S(2)}, u32[]{:S(2)}) %collective-permute-start.36) | collective-permute-done | bytes 1048608 | tf_op jit(solution)/shard_map/ppermute | solution.py:401
  459.5 17.7 %collective-permute-done.38 = bf16[256,2048]{1,0:T(8,128)(2,1)S(1)} collective-permute-done((bf16[256,2048]{1,0:T(8,128)(2,1)S(1)}, bf16[256,2048]{1,0:T(8,128)(2,1)S(1)}, u32[]{:S(2)}, u32[]{:S(2)}) %collective-permute-start.38) | collective-permute-done | bytes 1048608 | tf_op jit(solution)/shard_map/ppermute | solution.py:401
  477.1 3.6 fusion.17
  483.1 4.1 fusion.30
  493.9 3.7 fusion.35
  500.1 13.3 %collective-permute-done.39 = bf16[256,2048]{1,0:T(8,128)(2,1)S(1)} collective-permute-done((bf16[256,2048]{1,0:T(8,128)(2,1)}, bf16[256,2048]{1,0:T(8,128)(2,1)S(1)}, u32[]{:S(2)}, u32[]{:S(2)}) %collective-permute-start.39) | collective-permute-done | bytes 1048608 | tf_op jit(solution)/shard_map/ppermute | solution.py:401
  513.4 16.4 %collective-permute-done.40 = bf16[256,2048]{1,0:T(8,128)(2,1)} collective-permute-done((bf16[256,2048]{1,0:T(8,128)(2,1)}, bf16[256,2048]{1,0:T(8,128)(2,1)}, u32[]{:S(2)}, u32[]{:S(2)}) %collective-permute-start.40) | collective-permute-done | bytes 1048608 | tf_op jit(solution)/shard_map/ppermute | solution.py:401
  529.8 3.6 pad_maximum_fusion.3
  533.4 6.3 convolution_convert_fusion.4
  539.7 6.3 convolution_convert_fusion.5
  546.0 16.8 %shard_map.257 = (f32[2,2,4,64,512]{4,3,2,1,0:T(8,128)}, bf16[2,2,2,4,64,512]{5,4,3,2,1,0:T(8,128)(2,1)}) custom-call(s32[26]{0:T(128)} %pad_add_fusion.2.meta, bf16[2,2,4,64,512]{4,3,2,1,0:T(8,128)(2,1)} %bitcast.297, bf16[2,2,2,4,64,512]{5,4,3,2,1,0:T(8,128)(2,1)} %pad_maximum_fusion.4.kv_ref, bf16[2,2,4,64,512]{4,3,2,1,0:T(8,128)(2,1)} %bitcast.298, ...), custom_call_target="tpu_custom_call" | custom-call | flops 5368709120 | bytes 10485760 | tf_op jit(solution)/shard_map/pallas_call | solution.py:230
  566.4 3.1 fusion.37
  575.0 32.0 %collective-permute-done.69 = bf16[64,1536]{1,0:T(8,128)(2,1)} collective-permute-done((bf16[64,1536]{1,0:T(8,128)(2,1)}, bf16[64,1536]{1,0:T(8,128)(2,1)}, u32[]{:S(2)}, u32[]{:S(2)}) %collective-permute-start.69) | collective-permute-done | bytes 196640 | tf_op jit(solution)/shard_map/ppermute | solution.py:401
  610.6 4.4 collective-permute-done.70
  617.1 4.4 collective-permute-done.71
  623.3 7.6 shard_map.258
  630.8 3.1 add_convert_fusion
  639.0 26.8 %collective-permute-start.49 = (bf16[64,2048]{1,0:T(8,128)(2,1)}, bf16[64,2048]{1,0:T(8,128)(2,1)}, u32[]{:S(2)}, u32[]{:S(2)}) collective-permute-start(bf16[64,2048]{1,0:T(8,128)(2,1)} %get-tuple-element.159), channel_id=1, source_target_pairs={{0,2},{1,3},{2,0},{3,1},{4,6},{5,7},{6,4},{7,5},{8,10},{9,11},{10,... | collective-permute-start | bytes 786440 | tf_op jit(solution)/shard_map/ppermute | solution.py:406
  665.8 9.1 %fusion.52 = (bf16[1024,2048]{1,0:T(8,128)(2,1)S(1)}, f32[1024,2048]{1,0:T(8,128)}) fusion(bf16[1024,1024]{1,0:T(8,128)(2,1)S(1)} %copy-done.37, bf16[2048,1024]{1,0:T(8,128)(2,1)} %bitcast.295), kind=kOutput, calls=%fused_computation.261 | convolution fusion | flops 4297064448 | bytes 18874368 | tf_op jit(solution)/shard_map/dot_general | solution.py:39
  680.2 9.5 %convolution_convert_fusion.3 = bf16[2048,1024]{1,0:T(8,128)(2,1)} fusion(bf16[1024,2048]{1,0:T(8,128)(2,1)} %get-tuple-element.99, bf16[1024,1024]{1,0:T(8,128)(2,1)} %get-tuple-element.94), kind=kOutput, calls=%fused_computation.20 | convolution fusion | flops 4297064448 | bytes 10485760 | tf_op jit(solution)/shard_map/dot_general | solution.py:43
  694.5 4.6 collective-permute-start.50
  700.9 22.2 %collective-permute-done.50 = bf16[64,2048]{1,0:T(8,128)(2,1)S(1)} collective-permute-done((bf16[64,2048]{1,0:T(8,128)(2,1)}, bf16[64,2048]{1,0:T(8,128)(2,1)S(1)}, u32[]{:S(2)}, u32[]{:S(2)}) %collective-permute-start.50) | collective-permute-done | bytes 262176 | tf_op jit(solution)/shard_map/ppermute | solution.py:406
  727.9 4.3 fusion.15
  738.9 3.3 collective-permute-done.65
  742.3 10.7 %collective-permute-start.66 = (f32[4,136]{1,0:T(4,128)S(1)}, f32[4,136]{1,0:T(4,128)S(1)}, u32[]{:S(2)}, u32[]{:S(2)}) collective-permute-start(f32[4,136]{1,0:T(4,128)S(1)} %slice_select_fusion.2), channel_id=1, source_target_pairs={{0,4},{1,5},{2,6},{3,7},{4,0},{5,1},{6,2},{7,3},{8,12},{9,13},{10,... | collective-permute-start | bytes 6536 | tf_op jit(solution)/shard_map/ppermute | solution.py:431
  753.0 3.6 fusion.6
  767.1 3.7 collective-permute-done.52
  773.0 4.1 collective-permute-done.53
  795.3 5.0 collective-permute-done.61
  800.4 2.9 collective-permute-done.62
  (393 shorter events, 176.1 us)
Async XLA Ops:
  7.2 103.7 %all-gather.5.cloned.1.call-start = ((), (), s32[]{:S(2)}) async-start(), calls=%async_computation.5 | async-start | bytes 4718592 | tf_op jit(solution)/shard_map/all_gather | solution.py:524
  31.1 10.2 %collective-permute-start.1 = (bf16[64,2048]{1,0:T(8,128)(2,1)S(1)}, bf16[64,2048]{1,0:T(8,128)(2,1)S(1)}, u32[]{:S(2)}, u32[]{:S(2)}) collective-permute-start(bf16[64,2048]{1,0:T(8,128)(2,1)S(1)} %get-tuple-element.174), channel_id=1, source_target_pairs={{0,16},{8,24},{16,0},{24,8},{1,17},{9,25},{17,1},{25,9},{2,18},{10... | collective-permute-start | bytes 786440 | tf_op jit(solution)/shard_map/ppermute | solution.py:401
  31.6 9.7 %collective-permute-start.2 = (bf16[64,2048]{1,0:T(8,128)(2,1)S(1)}, bf16[64,2048]{1,0:T(8,128)(2,1)S(1)}, u32[]{:S(2)}, u32[]{:S(2)}) collective-permute-start(bf16[64,2048]{1,0:T(8,128)(2,1)S(1)} %get-tuple-element.173), channel_id=1, source_target_pairs={{0,24},{8,16},{16,8},{24,0},{1,25},{9,17},{17,9},{25,1},{2,26},{10... | collective-permute-start | bytes 786440 | tf_op jit(solution)/shard_map/ppermute | solution.py:401
  41.5 16.0 %collective-permute-start.6 = (bf16[64,2048]{1,0:T(8,128)(2,1)S(1)}, bf16[64,2048]{1,0:T(8,128)(2,1)S(1)}, u32[]{:S(2)}, u32[]{:S(2)}) collective-permute-start(bf16[64,2048]{1,0:T(8,128)(2,1)S(1)} %get-tuple-element.171), channel_id=1, source_target_pairs={{0,2},{1,3},{2,0},{3,1},{4,6},{5,7},{6,4},{7,5},{8,10},{9,11},{10,... | collective-permute-start | bytes 786440 | tf_op jit(solution)/shard_map/ppermute | solution.py:406
  43.1 18.0 %collective-permute-start.7 = (bf16[64,2048]{1,0:T(8,128)(2,1)S(1)}, bf16[64,2048]{1,0:T(8,128)(2,1)S(1)}, u32[]{:S(2)}, u32[]{:S(2)}) collective-permute-start(bf16[64,2048]{1,0:T(8,128)(2,1)S(1)} %get-tuple-element.170), channel_id=1, source_target_pairs={{0,4},{1,5},{2,6},{3,7},{4,0},{5,1},{6,2},{7,3},{8,12},{9,13},{10,... | collective-permute-start | bytes 786440 | tf_op jit(solution)/shard_map/ppermute | solution.py:406
  45.7 15.5 %collective-permute-start.8 = (bf16[64,2048]{1,0:T(8,128)(2,1)S(1)}, bf16[64,2048]{1,0:T(8,128)(2,1)S(1)}, u32[]{:S(2)}, u32[]{:S(2)}) collective-permute-start(bf16[64,2048]{1,0:T(8,128)(2,1)S(1)} %get-tuple-element.169), channel_id=1, source_target_pairs={{0,6},{1,7},{2,4},{3,5},{4,2},{5,3},{6,0},{7,1},{8,14},{9,15},{10,... | collective-permute-start | bytes 786440 | tf_op jit(solution)/shard_map/ppermute | solution.py:406
  46.1 11.4 %collective-permute-start.5 = (bf16[64,1024]{1,0:T(8,128)(2,1)S(1)}, bf16[64,1024]{1,0:T(8,128)(2,1)S(1)}, u32[]{:S(2)}, u32[]{:S(2)}) collective-permute-start(bf16[64,1024]{1,0:T(8,128)(2,1)S(1)} %pad_maximum_fusion.23), channel_id=1, source_target_pairs={{0,24},{8,16},{16,8},{24,0},{1,25},{9,17},{17,9},{25,1},{2,26},{10... | collective-permute-start | bytes 393224 | tf_op jit(solution)/shard_map/ppermute | solution.py:401
  63.7 107.8 %all-gather.7.cloned.1.call-start = ((), (), s32[]{:S(2)}) async-start(), calls=%async_computation.6 | async-start | bytes 2359296 | tf_op jit(solution)/shard_map/all_gather | solution.py:525
  64.5 230.4 %all-gather.9.cloned.1.call-start = ((), (), s32[]{:S(2)}) async-start(), calls=%async_computation.7 | async-start | bytes 14155776 | tf_op jit(solution)/shard_map/all_gather | solution.py:533
  64.7 26.1 %collective-permute-start.14 = (bf16[256,2048]{1,0:T(8,128)(2,1)S(1)}, bf16[256,2048]{1,0:T(8,128)(2,1)S(1)}, u32[]{:S(2)}, u32[]{:S(2)}) collective-permute-start(bf16[256,2048]{1,0:T(8,128)(2,1)S(1)} %pad_maximum_fusion.6), channel_id=1, source_target_pairs={{0,8},{8,0},{16,24},{24,16},{1,9},{9,1},{17,25},{25,17},{2,10},{10... | collective-permute-start | bytes 3145736 | tf_op jit(solution)/shard_map/ppermute | solution.py:401
  65.0 25.7 %collective-permute-start.15 = (bf16[256,2048]{1,0:T(8,128)(2,1)S(1)}, bf16[256,2048]{1,0:T(8,128)(2,1)S(1)}, u32[]{:S(2)}, u32[]{:S(2)}) collective-permute-start(bf16[256,2048]{1,0:T(8,128)(2,1)S(1)} %pad_maximum_fusion.6), channel_id=1, source_target_pairs={{0,16},{8,24},{16,0},{24,8},{1,17},{9,25},{17,1},{25,9},{2,18},{10... | collective-permute-start | bytes 3145736 | tf_op jit(solution)/shard_map/ppermute | solution.py:401
  66.5 37.3 %collective-permute-start.16 = (bf16[256,2048]{1,0:T(8,128)(2,1)S(1)}, bf16[256,2048]{1,0:T(8,128)(2,1)}, u32[]{:S(2)}, u32[]{:S(2)}) collective-permute-start(bf16[256,2048]{1,0:T(8,128)(2,1)S(1)} %pad_maximum_fusion.6), channel_id=1, source_target_pairs={{0,24},{8,16},{16,8},{24,0},{1,25},{9,17},{17,9},{25,1},{2,26},{10... | collective-permute-start | bytes 3145736 | tf_op jit(solution)/shard_map/ppermute | solution.py:401
  122.2 12.1 %collective-permute-start.24 = (bf16[64,3072]{1,0:T(8,128)(2,1)S(1)}, bf16[64,3072]{1,0:T(8,128)(2,1)S(1)}, u32[]{:S(2)}, u32[]{:S(2)}) collective-permute-start(bf16[64,3072]{1,0:T(8,128)(2,1)S(1)} %pad_maximum_fusion.18), channel_id=1, source_target_pairs={{0,8},{8,0},{16,24},{24,16},{1,9},{9,1},{17,25},{25,17},{2,10},{10... | collective-permute-start | bytes 1179656 | tf_op jit(solution)/shard_map/ppermute | solution.py:401
  123.8 19.5 %collective-permute-start.25 = (bf16[64,3072]{1,0:T(8,128)(2,1)S(1)}, bf16[64,3072]{1,0:T(8,128)(2,1)S(1)}, u32[]{:S(2)}, u32[]{:S(2)}) collective-permute-start(bf16[64,3072]{1,0:T(8,128)(2,1)S(1)} %pad_maximum_fusion.19), channel_id=1, source_target_pairs={{0,16},{8,24},{16,0},{24,8},{1,17},{9,25},{17,1},{25,9},{2,18},{10... | collective-permute-start | bytes 1179656 | tf_op jit(solution)/shard_map/ppermute | solution.py:401
  125.3 18.0 %collective-permute-start.26 = (bf16[64,3072]{1,0:T(8,128)(2,1)S(1)}, bf16[64,3072]{1,0:T(8,128)(2,1)S(1)}, u32[]{:S(2)}, u32[]{:S(2)}) collective-permute-start(bf16[64,3072]{1,0:T(8,128)(2,1)S(1)} %pad_maximum_fusion.20), channel_id=1, source_target_pairs={{0,24},{8,16},{16,8},{24,0},{1,25},{9,17},{17,9},{25,1},{2,26},{10... | collective-permute-start | bytes 1179656 | tf_op jit(solution)/shard_map/ppermute | solution.py:401
  144.5 226.8 %all-gather.11.cloned.1.call-start = ((), (), s32[]{:S(2)}) async-start(), calls=%async_computation.8 | async-start | bytes 7077888 | tf_op jit(solution)/shard_map/all_gather | solution.py:534
  145.1 335.7 %reduce-scatter.6.cloned.1.call-start = ((), (), s32[]{:S(2)}) async-start(), calls=%async_computation.9 | async-start | bytes 7077888 | tf_op jit(solution)/shard_map/reduce_scatter | solution.py:555
  180.9 61.9 %collective-permute-start.18 = (bf16[256,2048]{1,0:T(8,128)(2,1)}, bf16[256,2048]{1,0:T(8,128)(2,1)S(1)}, u32[]{:S(2)}, u32[]{:S(2)}) collective-permute-start(bf16[256,2048]{1,0:T(8,128)(2,1)} %get-tuple-element.128), channel_id=1, source_target_pairs={{0,8},{8,0},{16,24},{24,16},{1,9},{9,1},{17,25},{25,17},{2,10},{10... | collective-permute-start | bytes 3145736 | tf_op jit(solution)/shard_map/ppermute | solution.py:401
  181.9 60.9 %collective-permute-start.19 = (bf16[256,2048]{1,0:T(8,128)(2,1)}, bf16[256,2048]{1,0:T(8,128)(2,1)S(1)}, u32[]{:S(2)}, u32[]{:S(2)}) collective-permute-start(bf16[256,2048]{1,0:T(8,128)(2,1)} %get-tuple-element.130), channel_id=1, source_target_pairs={{0,16},{8,24},{16,0},{24,8},{1,17},{9,25},{17,1},{25,9},{2,18},{10... | collective-permute-start | bytes 3145736 | tf_op jit(solution)/shard_map/ppermute | solution.py:401
  182.8 60.0 %collective-permute-start.20 = (bf16[256,2048]{1,0:T(8,128)(2,1)}, bf16[256,2048]{1,0:T(8,128)(2,1)}, u32[]{:S(2)}, u32[]{:S(2)}) collective-permute-start(bf16[256,2048]{1,0:T(8,128)(2,1)} %get-tuple-element.129), channel_id=1, source_target_pairs={{0,24},{8,16},{16,8},{24,0},{1,25},{9,17},{17,9},{25,1},{2,26},{10... | collective-permute-start | bytes 3145736 | tf_op jit(solution)/shard_map/ppermute | solution.py:401
  185.3 48.0 %collective-permute-start.27 = (bf16[64,2048]{1,0:T(8,128)(2,1)S(1)}, bf16[64,2048]{1,0:T(8,128)(2,1)S(1)}, u32[]{:S(2)}, u32[]{:S(2)}) collective-permute-start(bf16[64,2048]{1,0:T(8,128)(2,1)S(1)} %get-tuple-element.167), channel_id=1, source_target_pairs={{0,8},{8,0},{16,24},{24,16},{1,9},{9,1},{17,25},{25,17},{2,10},{10... | collective-permute-start | bytes 786440 | tf_op jit(solution)/shard_map/ppermute | solution.py:401
  186.3 52.5 %collective-permute-start.28 = (bf16[64,2048]{1,0:T(8,128)(2,1)}, bf16[64,2048]{1,0:T(8,128)(2,1)}, u32[]{:S(2)}, u32[]{:S(2)}) collective-permute-start(bf16[64,2048]{1,0:T(8,128)(2,1)} %get-tuple-element.166), channel_id=1, source_target_pairs={{0,16},{8,24},{16,0},{24,8},{1,17},{9,25},{17,1},{25,9},{2,18},{10... | collective-permute-start | bytes 786440 | tf_op jit(solution)/shard_map/ppermute | solution.py:401
  248.9 38.8 %collective-permute-start.21 = (bf16[256,2048]{1,0:T(8,128)(2,1)}, bf16[256,2048]{1,0:T(8,128)(2,1)}, u32[]{:S(2)}, u32[]{:S(2)}) collective-permute-start(bf16[256,2048]{1,0:T(8,128)(2,1)} %multiply_convert_fusion.2), channel_id=1, source_target_pairs={{0,8},{8,0},{16,24},{24,16},{1,9},{9,1},{17,25},{25,17},{2,10},{10... | collective-permute-start | bytes 3145736 | tf_op jit(solution)/shard_map/ppermute | solution.py:401
  249.8 37.8 %collective-permute-start.22 = (bf16[256,2048]{1,0:T(8,128)(2,1)}, bf16[256,2048]{1,0:T(8,128)(2,1)}, u32[]{:S(2)}, u32[]{:S(2)}) collective-permute-start(bf16[256,2048]{1,0:T(8,128)(2,1)} %multiply_convert_fusion.2), channel_id=1, source_target_pairs={{0,16},{8,24},{16,0},{24,8},{1,17},{9,25},{17,1},{25,9},{2,18},{10... | collective-permute-start | bytes 3145736 | tf_op jit(solution)/shard_map/ppermute | solution.py:401
  250.7 44.1 %collective-permute-start.23 = (bf16[256,2048]{1,0:T(8,128)(2,1)}, bf16[256,2048]{1,0:T(8,128)(2,1)}, u32[]{:S(2)}, u32[]{:S(2)}) collective-permute-start(bf16[256,2048]{1,0:T(8,128)(2,1)} %multiply_convert_fusion.2), channel_id=1, source_target_pairs={{0,24},{8,16},{16,8},{24,0},{1,25},{9,17},{17,9},{25,1},{2,26},{10... | collective-permute-start | bytes 3145736 | tf_op jit(solution)/shard_map/ppermute | solution.py:401
  252.4 18.2 %collective-permute-start.30 = (bf16[64,2048]{1,0:T(8,128)(2,1)S(1)}, bf16[64,2048]{1,0:T(8,128)(2,1)S(1)}, u32[]{:S(2)}, u32[]{:S(2)}) collective-permute-start(bf16[64,2048]{1,0:T(8,128)(2,1)S(1)} %get-tuple-element.163), channel_id=1, source_target_pairs={{0,2},{1,3},{2,0},{3,1},{4,6},{5,7},{6,4},{7,5},{8,10},{9,11},{10,... | collective-permute-start | bytes 786440 | tf_op jit(solution)/shard_map/ppermute | solution.py:406
  259.9 11.7 %collective-permute-start.31 = (bf16[64,2048]{1,0:T(8,128)(2,1)S(1)}, bf16[64,2048]{1,0:T(8,128)(2,1)S(1)}, u32[]{:S(2)}, u32[]{:S(2)}) collective-permute-start(bf16[64,2048]{1,0:T(8,128)(2,1)S(1)} %get-tuple-element.162), channel_id=1, source_target_pairs={{0,4},{1,5},{2,6},{3,7},{4,0},{5,1},{6,2},{7,3},{8,12},{9,13},{10,... | collective-permute-start | bytes 786440 | tf_op jit(solution)/shard_map/ppermute | solution.py:406
  270.7 15.6 %collective-permute-start.32 = (bf16[64,2048]{1,0:T(8,128)(2,1)S(1)}, bf16[64,2048]{1,0:T(8,128)(2,1)}, u32[]{:S(2)}, u32[]{:S(2)}) collective-permute-start(bf16[64,2048]{1,0:T(8,128)(2,1)S(1)} %get-tuple-element.161), channel_id=1, source_target_pairs={{0,6},{1,7},{2,4},{3,5},{4,2},{5,3},{6,0},{7,1},{8,14},{9,15},{10,... | collective-permute-start | bytes 786440 | tf_op jit(solution)/shard_map/ppermute | solution.py:406
  312.0 26.1 %collective-permute-start.33 = (bf16[256,2048]{1,0:T(8,128)(2,1)S(1)}, bf16[256,2048]{1,0:T(8,128)(2,1)S(1)}, u32[]{:S(2)}, u32[]{:S(2)}) collective-permute-start(bf16[256,2048]{1,0:T(8,128)(2,1)S(1)} %maximum_select_fusion), channel_id=1, source_target_pairs={{0,8},{8,0},{16,24},{24,16},{1,9},{9,1},{17,25},{25,17},{2,10},{10... | collective-permute-start | bytes 3145736 | tf_op jit(solution)/shard_map/ppermute | solution.py:401
  312.9 25.4 %collective-permute-start.34 = (bf16[256,2048]{1,0:T(8,128)(2,1)S(1)}, bf16[256,2048]{1,0:T(8,128)(2,1)S(1)}, u32[]{:S(2)}, u32[]{:S(2)}) collective-permute-start(bf16[256,2048]{1,0:T(8,128)(2,1)S(1)} %maximum_select_fusion), channel_id=1, source_target_pairs={{0,16},{8,24},{16,0},{24,8},{1,17},{9,25},{17,1},{25,9},{2,18},{10... | collective-permute-start | bytes 3145736 | tf_op jit(solution)/shard_map/ppermute | solution.py:401
  314.3 41.7 %collective-permute-start.35 = (bf16[256,2048]{1,0:T(8,128)(2,1)S(1)}, bf16[256,2048]{1,0:T(8,128)(2,1)S(1)}, u32[]{:S(2)}, u32[]{:S(2)}) collective-permute-start(bf16[256,2048]{1,0:T(8,128)(2,1)S(1)} %maximum_select_fusion), channel_id=1, source_target_pairs={{0,24},{8,16},{16,8},{24,0},{1,25},{9,17},{17,9},{25,1},{2,26},{10... | collective-permute-start | bytes 3145736 | tf_op jit(solution)/shard_map/ppermute | solution.py:401
  367.0 166.4 %reduce-scatter.8.cloned.1.call-start = ((), (), s32[]{:S(2)}) async-start(), calls=%async_computation.10 | async-start | bytes 7077888 | tf_op jit(solution)/shard_map/reduce_scatter | solution.py:565
  417.0 217.0 %reduce-scatter.10.cloned.1.call-start = ((), (), s32[]{:S(2)}) async-start(), calls=%async_computation.11 | async-start | bytes 7077888 | tf_op jit(solution)/shard_map/reduce_scatter | solution.py:568
  428.8 303.4 %reduce-scatter.12.cloned.1.call-start = ((), (), s32[]{:S(2)}) async-start(), calls=%async_computation.12 | async-start | bytes 2359296 | tf_op jit(solution)/shard_map/reduce_scatter | solution.py:582
  433.4 26.1 %collective-permute-start.36 = (bf16[256,2048]{1,0:T(8,128)(2,1)S(1)}, bf16[256,2048]{1,0:T(8,128)(2,1)S(1)}, u32[]{:S(2)}, u32[]{:S(2)}) collective-permute-start(bf16[256,2048]{1,0:T(8,128)(2,1)S(1)} %get-tuple-element.125), channel_id=1, source_target_pairs={{0,8},{8,0},{16,24},{24,16},{1,9},{9,1},{17,25},{25,17},{2,10},{10... | collective-permute-start | bytes 3145736 | tf_op jit(solution)/shard_map/ppermute | solution.py:401
  435.1 24.4 %collective-permute-start.37 = (bf16[256,2048]{1,0:T(8,128)(2,1)S(1)}, bf16[256,2048]{1,0:T(8,128)(2,1)S(1)}, u32[]{:S(2)}, u32[]{:S(2)}) collective-permute-start(bf16[256,2048]{1,0:T(8,128)(2,1)S(1)} %get-tuple-element.127), channel_id=1, source_target_pairs={{0,16},{8,24},{16,0},{24,8},{1,17},{9,25},{17,1},{25,9},{2,18},{10... | collective-permute-start | bytes 3145736 | tf_op jit(solution)/shard_map/ppermute | solution.py:401
  435.7 41.4 %collective-permute-start.38 = (bf16[256,2048]{1,0:T(8,128)(2,1)S(1)}, bf16[256,2048]{1,0:T(8,128)(2,1)S(1)}, u32[]{:S(2)}, u32[]{:S(2)}) collective-permute-start(bf16[256,2048]{1,0:T(8,128)(2,1)S(1)} %get-tuple-element.126), channel_id=1, source_target_pairs={{0,24},{8,16},{16,8},{24,0},{1,25},{9,17},{17,9},{25,1},{2,26},{10... | collective-permute-start | bytes 3145736 | tf_op jit(solution)/shard_map/ppermute | solution.py:401
  487.1 26.2 %collective-permute-start.39 = (bf16[256,2048]{1,0:T(8,128)(2,1)}, bf16[256,2048]{1,0:T(8,128)(2,1)S(1)}, u32[]{:S(2)}, u32[]{:S(2)}) collective-permute-start(bf16[256,2048]{1,0:T(8,128)(2,1)} %get-tuple-element.133), channel_id=1, source_target_pairs={{0,8},{8,0},{16,24},{24,16},{1,9},{9,1},{17,25},{25,17},{2,10},{10... | collective-permute-start | bytes 3145736 | tf_op jit(solution)/shard_map/ppermute | solution.py:401
  488.1 41.7 %collective-permute-start.40 = (bf16[256,2048]{1,0:T(8,128)(2,1)}, bf16[256,2048]{1,0:T(8,128)(2,1)}, u32[]{:S(2)}, u32[]{:S(2)}) collective-permute-start(bf16[256,2048]{1,0:T(8,128)(2,1)} %get-tuple-element.133), channel_id=1, source_target_pairs={{0,16},{8,24},{16,0},{24,8},{1,17},{9,25},{17,1},{25,9},{2,18},{10... | collective-permute-start | bytes 3145736 | tf_op jit(solution)/shard_map/ppermute | solution.py:401
  489.5 40.2 %collective-permute-start.41 = (bf16[256,2048]{1,0:T(8,128)(2,1)}, bf16[256,2048]{1,0:T(8,128)(2,1)}, u32[]{:S(2)}, u32[]{:S(2)}) collective-permute-start(bf16[256,2048]{1,0:T(8,128)(2,1)} %get-tuple-element.133), channel_id=1, source_target_pairs={{0,24},{8,16},{16,8},{24,0},{1,25},{9,17},{17,9},{25,1},{2,26},{10... | collective-permute-start | bytes 3145736 | tf_op jit(solution)/shard_map/ppermute | solution.py:401
  562.8 68.0 %collective-permute-start.43 = (bf16[256,2048]{1,0:T(8,128)(2,1)}, bf16[256,2048]{1,0:T(8,128)(2,1)}, u32[]{:S(2)}, u32[]{:S(2)}) collective-permute-start(bf16[256,2048]{1,0:T(8,128)(2,1)} %get-tuple-element.91), channel_id=1, source_target_pairs={{0,8},{8,0},{16,24},{24,16},{1,9},{9,1},{17,25},{25,17},{2,10},{10... | collective-permute-start | bytes 3145736 | tf_op jit(solution)/shard_map/ppermute | solution.py:401
  564.5 66.3 %collective-permute-start.44 = (bf16[256,2048]{1,0:T(8,128)(2,1)}, bf16[256,2048]{1,0:T(8,128)(2,1)}, u32[]{:S(2)}, u32[]{:S(2)}) collective-permute-start(bf16[256,2048]{1,0:T(8,128)(2,1)} %get-tuple-element.92), channel_id=1, source_target_pairs={{0,16},{8,24},{16,0},{24,8},{1,17},{9,25},{17,1},{25,9},{2,18},{10... | collective-permute-start | bytes 3145736 | tf_op jit(solution)/shard_map/ppermute | solution.py:401
  564.9 66.0 %collective-permute-start.45 = (bf16[256,2048]{1,0:T(8,128)(2,1)}, bf16[256,2048]{1,0:T(8,128)(2,1)}, u32[]{:S(2)}, u32[]{:S(2)}) collective-permute-start(bf16[256,2048]{1,0:T(8,128)(2,1)} %get-tuple-element.93), channel_id=1, source_target_pairs={{0,24},{8,16},{16,8},{24,0},{1,25},{9,17},{17,9},{25,1},{2,26},{10... | collective-permute-start | bytes 3145736 | tf_op jit(solution)/shard_map/ppermute | solution.py:401
  569.5 52.8 %collective-permute-start.42 = (bf16[1024,512]{1,0:T(8,128)(2,1)}, bf16[1024,512]{1,0:T(8,128)(2,1)S(1)}, u32[]{:S(2)}, u32[]{:S(2)}) collective-permute-start(bf16[1024,512]{1,0:T(8,128)(2,1)} %bitcast.69), channel_id=1, source_target_pairs={{0,1},{1,0},{2,3},{3,2},{4,5},{5,4},{6,7},{7,6},{8,9},{9,8},{10,11... | collective-permute-start | bytes 3145736 | tf_op jit(solution)/shard_map/ppermute | solution.py:411
  570.2 36.7 %collective-permute-start.69 = (bf16[64,1536]{1,0:T(8,128)(2,1)}, bf16[64,1536]{1,0:T(8,128)(2,1)}, u32[]{:S(2)}, u32[]{:S(2)}) collective-permute-start(bf16[64,1536]{1,0:T(8,128)(2,1)} %get-tuple-element.181), channel_id=1, source_target_pairs={{0,8},{8,0},{16,24},{24,16},{1,9},{9,1},{17,25},{25,17},{2,10},{10... | collective-permute-start | bytes 589832 | tf_op jit(solution)/shard_map/ppermute | solution.py:401
  571.9 209.5 %reduce-scatter.14.cloned.1.call-start = ((), (), s32[]{:S(2)}) async-start(), calls=%async_computation.13 | async-start | bytes 4718592 | tf_op jit(solution)/shard_map/reduce_scatter | solution.py:599
  636.1 56.5 %collective-permute-start.72 = (bf16[64,1536]{1,0:T(8,128)(2,1)}, bf16[64,1536]{1,0:T(8,128)(2,1)}, u32[]{:S(2)}, u32[]{:S(2)}) collective-permute-start(bf16[64,1536]{1,0:T(8,128)(2,1)} %get-tuple-element.178), channel_id=1, source_target_pairs={{0,8},{8,0},{16,24},{24,16},{1,9},{9,1},{17,25},{25,17},{2,10},{10... | collective-permute-start | bytes 589832 | tf_op jit(solution)/shard_map/ppermute | solution.py:401
  636.4 58.2 %collective-permute-start.73 = (bf16[64,1536]{1,0:T(8,128)(2,1)}, bf16[64,1536]{1,0:T(8,128)(2,1)}, u32[]{:S(2)}, u32[]{:S(2)}) collective-permute-start(bf16[64,1536]{1,0:T(8,128)(2,1)} %get-tuple-element.177), channel_id=1, source_target_pairs={{0,16},{8,24},{16,0},{24,8},{1,17},{9,25},{17,1},{25,9},{2,18},{10... | collective-permute-start | bytes 589832 | tf_op jit(solution)/shard_map/ppermute | solution.py:401
  639.0 60.2 %collective-permute-start.49 = (bf16[64,2048]{1,0:T(8,128)(2,1)}, bf16[64,2048]{1,0:T(8,128)(2,1)}, u32[]{:S(2)}, u32[]{:S(2)}) collective-permute-start(bf16[64,2048]{1,0:T(8,128)(2,1)} %get-tuple-element.159), channel_id=1, source_target_pairs={{0,2},{1,3},{2,0},{3,1},{4,6},{5,7},{6,4},{7,5},{8,10},{9,11},{10,... | collective-permute-start | bytes 786440 | tf_op jit(solution)/shard_map/ppermute | solution.py:406
  676.6 50.3 %collective-permute-start.46 = (bf16[256,2048]{1,0:T(8,128)(2,1)}, bf16[256,2048]{1,0:T(8,128)(2,1)S(1)}, u32[]{:S(2)}, u32[]{:S(2)}) collective-permute-start(bf16[256,2048]{1,0:T(8,128)(2,1)} %get-tuple-element.119), channel_id=1, source_target_pairs={{0,8},{8,0},{16,24},{24,16},{1,9},{9,1},{17,25},{25,17},{2,10},{10... | collective-permute-start | bytes 3145736 | tf_op jit(solution)/shard_map/ppermute | solution.py:401
  677.9 49.0 %collective-permute-start.47 = (bf16[256,2048]{1,0:T(8,128)(2,1)}, bf16[256,2048]{1,0:T(8,128)(2,1)}, u32[]{:S(2)}, u32[]{:S(2)}) collective-permute-start(bf16[256,2048]{1,0:T(8,128)(2,1)} %get-tuple-element.121), channel_id=1, source_target_pairs={{0,16},{8,24},{16,0},{24,8},{1,17},{9,25},{17,1},{25,9},{2,18},{10... | collective-permute-start | bytes 3145736 | tf_op jit(solution)/shard_map/ppermute | solution.py:401
  692.7 34.3 %collective-permute-start.48 = (bf16[256,2048]{1,0:T(8,128)(2,1)}, bf16[256,2048]{1,0:T(8,128)(2,1)S(1)}, u32[]{:S(2)}, u32[]{:S(2)}) collective-permute-start(bf16[256,2048]{1,0:T(8,128)(2,1)} %get-tuple-element.120), channel_id=1, source_target_pairs={{0,24},{8,16},{16,8},{24,0},{1,25},{9,17},{17,9},{25,1},{2,26},{10... | collective-permute-start | bytes 3145736 | tf_op jit(solution)/shard_map/ppermute | solution.py:401
  694.5 28.6 %collective-permute-start.50 = (bf16[64,2048]{1,0:T(8,128)(2,1)}, bf16[64,2048]{1,0:T(8,128)(2,1)S(1)}, u32[]{:S(2)}, u32[]{:S(2)}) collective-permute-start(bf16[64,2048]{1,0:T(8,128)(2,1)} %get-tuple-element.158), channel_id=1, source_target_pairs={{0,4},{1,5},{2,6},{3,7},{4,0},{5,1},{6,2},{7,3},{8,12},{9,13},{10,... | collective-permute-start | bytes 786440 | tf_op jit(solution)/shard_map/ppermute | solution.py:406
  699.2 25.7 %collective-permute-start.51 = (bf16[64,2048]{1,0:T(8,128)(2,1)}, bf16[64,2048]{1,0:T(8,128)(2,1)S(1)}, u32[]{:S(2)}, u32[]{:S(2)}) collective-permute-start(bf16[64,2048]{1,0:T(8,128)(2,1)} %get-tuple-element.157), channel_id=1, source_target_pairs={{0,6},{1,7},{2,4},{3,5},{4,2},{5,3},{6,0},{7,1},{8,14},{9,15},{10,... | collective-permute-start | bytes 786440 | tf_op jit(solution)/shard_map/ppermute | solution.py:406
  723.1 12.5 %collective-permute-start.74 = (bf16[64,1536]{1,0:T(8,128)(2,1)}, bf16[64,1536]{1,0:T(8,128)(2,1)}, u32[]{:S(2)}, u32[]{:S(2)}) collective-permute-start(bf16[64,1536]{1,0:T(8,128)(2,1)} %get-tuple-element.176), channel_id=1, source_target_pairs={{0,24},{8,16},{16,8},{24,0},{1,25},{9,17},{17,9},{25,1},{2,26},{10... | collective-permute-start | bytes 589832 | tf_op jit(solution)/shard_map/ppermute | solution.py:401
  742.3 14.4 %collective-permute-start.66 = (f32[4,136]{1,0:T(4,128)S(1)}, f32[4,136]{1,0:T(4,128)S(1)}, u32[]{:S(2)}, u32[]{:S(2)}) collective-permute-start(f32[4,136]{1,0:T(4,128)S(1)} %slice_select_fusion.2), channel_id=1, source_target_pairs={{0,4},{1,5},{2,6},{3,7},{4,0},{5,1},{6,2},{7,3},{8,12},{9,13},{10,... | collective-permute-start | bytes 6536 | tf_op jit(solution)/shard_map/ppermute | solution.py:431
  758.5 19.2 %collective-permute-start.55 = (bf16[64,2048]{1,0:T(8,128)(2,1)S(1)}, bf16[64,2048]{1,0:T(8,128)(2,1)S(1)}, u32[]{:S(2)}, u32[]{:S(2)}) collective-permute-start(bf16[64,2048]{1,0:T(8,128)(2,1)S(1)} %get-tuple-element.146), channel_id=1, source_target_pairs={{0,2},{1,3},{2,0},{3,1},{4,6},{5,7},{6,4},{7,5},{8,10},{9,11},{10,... | collective-permute-start | bytes 786440 | tf_op jit(solution)/shard_map/ppermute | solution.py:406
  759.0 18.8 %collective-permute-start.56 = (bf16[64,2048]{1,0:T(8,128)(2,1)S(1)}, bf16[64,2048]{1,0:T(8,128)(2,1)S(1)}, u32[]{:S(2)}, u32[]{:S(2)}) collective-permute-start(bf16[64,2048]{1,0:T(8,128)(2,1)S(1)} %get-tuple-element.145), channel_id=1, source_target_pairs={{0,4},{1,5},{2,6},{3,7},{4,0},{5,1},{6,2},{7,3},{8,12},{9,13},{10,... | collective-permute-start | bytes 786440 | tf_op jit(solution)/shard_map/ppermute | solution.py:406
  761.6 9.2 %collective-permute-start.52 = (bf16[64,2048]{1,0:T(8,128)(2,1)S(1)}, bf16[64,2048]{1,0:T(8,128)(2,1)S(1)}, u32[]{:S(2)}, u32[]{:S(2)}) collective-permute-start(bf16[64,2048]{1,0:T(8,128)(2,1)S(1)} %get-tuple-element.155), channel_id=1, source_target_pairs={{0,8},{8,0},{16,24},{24,16},{1,9},{9,1},{17,25},{25,17},{2,10},{10... | collective-permute-start | bytes 786440 | tf_op jit(solution)/shard_map/ppermute | solution.py:401
  763.1 14.0 %collective-permute-start.53 = (bf16[64,2048]{1,0:T(8,128)(2,1)S(1)}, bf16[64,2048]{1,0:T(8,128)(2,1)S(1)}, u32[]{:S(2)}, u32[]{:S(2)}) collective-permute-start(bf16[64,2048]{1,0:T(8,128)(2,1)S(1)} %get-tuple-element.154), channel_id=1, source_target_pairs={{0,16},{8,24},{16,0},{24,8},{1,17},{9,25},{17,1},{25,9},{2,18},{10... | collective-permute-start | bytes 786440 | tf_op jit(solution)/shard_map/ppermute | solution.py:401
  765.4 11.7 %collective-permute-start.54 = (bf16[64,2048]{1,0:T(8,128)(2,1)S(1)}, bf16[64,2048]{1,0:T(8,128)(2,1)S(1)}, u32[]{:S(2)}, u32[]{:S(2)}) collective-permute-start(bf16[64,2048]{1,0:T(8,128)(2,1)S(1)} %get-tuple-element.153), channel_id=1, source_target_pairs={{0,24},{8,16},{16,8},{24,0},{1,25},{9,17},{17,9},{25,1},{2,26},{10... | collective-permute-start | bytes 786440 | tf_op jit(solution)/shard_map/ppermute | solution.py:401
  770.8 9.2 %collective-permute-start.57 = (bf16[64,2048]{1,0:T(8,128)(2,1)S(1)}, bf16[64,2048]{1,0:T(8,128)(2,1)S(1)}, u32[]{:S(2)}, u32[]{:S(2)}) collective-permute-start(bf16[64,2048]{1,0:T(8,128)(2,1)S(1)} %get-tuple-element.144), channel_id=1, source_target_pairs={{0,6},{1,7},{2,4},{3,5},{4,2},{5,3},{6,0},{7,1},{8,14},{9,15},{10,... | collective-permute-start | bytes 786440 | tf_op jit(solution)/shard_map/ppermute | solution.py:406
  792.4 10.9 %collective-permute-start.62 = (bf16[64,2048]{1,0:T(8,128)(2,1)S(1)}, bf16[64,2048]{1,0:T(8,128)(2,1)S(1)}, u32[]{:S(2)}, u32[]{:S(2)}) collective-permute-start(bf16[64,2048]{1,0:T(8,128)(2,1)S(1)} %get-tuple-element.141), channel_id=1, source_target_pairs={{0,16},{8,24},{16,0},{24,8},{1,17},{9,25},{17,1},{25,9},{2,18},{10... | collective-permute-start | bytes 786440 | tf_op jit(solution)/shard_map/ppermute | solution.py:401
  792.9 10.4 %collective-permute-start.63 = (bf16[64,2048]{1,0:T(8,128)(2,1)S(1)}, bf16[64,2048]{1,0:T(8,128)(2,1)S(1)}, u32[]{:S(2)}, u32[]{:S(2)}) collective-permute-start(bf16[64,2048]{1,0:T(8,128)(2,1)S(1)} %get-tuple-element.140), channel_id=1, source_target_pairs={{0,24},{8,16},{16,8},{24,0},{1,25},{9,17},{17,9},{25,1},{2,26},{10... | collective-permute-start | bytes 786440 | tf_op jit(solution)/shard_map/ppermute | solution.py:401
  (58 other events, 846.1 us)
Sparse Core Ops, SparseCore 0:
  63.9 46.9 all-gather.4
  112.5 27.9 all-gather.6
  144.6 116.5 all-gather.8
  262.8 72.9 all-gather.10
  367.1 79.0 reduce-scatter.5
  448.4 68.1 reduce-scatter.7
  518.9 68.1 reduce-scatter.9
  589.4 45.0 reduce-scatter.11
  689.8 62.2 reduce-scatter.13

commit v3 on v2

--- a/solution.py
+++ b/solution.py
@@ -14,6 +14,7 @@
 EPS = 1e-06
 THETA = 1000000.0
 LOG2_E = 1.4426950408889634
+STEP = 4
 BF = jnp.bfloat16
 F32 = jnp.float32
 
@@ -81,30 +82,31 @@
     ids = 2 + 2 * blocks
     row = lax.broadcasted_iota(jnp.int32, (stacked, 1), 0) % tile_rows
     row_limit = jnp.minimum(start + (row ^ flip), length - 1)
-    column = lax.broadcasted_iota(jnp.int32, (1, 2 * tile_rows), 1) ^ flip
+    column = lax.broadcasted_iota(jnp.int32, (1, STEP * tile_rows), 1) ^ flip
     last = jnp.minimum(start, length - 1) // tile_rows
     acc_ref[...] = jnp.zeros_like(acc_ref)
     total_ref[...] = jnp.zeros_like(total_ref)
     queries = [stack_heads(q_ref, h, per_key) for h in range(kv_heads)]
 
     def body(step, carry):
-        block_a, block_b = meta[ids + 2 * step], meta[ids + 2 * step + 1]
-        allowed = step * (2 * tile_rows) + column <= row_limit
+        taken = [meta[ids + STEP * step + n] for n in range(STEP)]
+        allowed = step * (STEP * tile_rows) + column <= row_limit
+
+        def columns_of(at):
+            return jnp.concatenate([key_block(kv_ref, b, blocks, slice(at, at + HD)) for b in taken], axis=0)
+
+        scores = [dot_nt(queries[h], columns_of(h * HD)) for h in range(kv_heads)]
+        weights = [jnp.where(allowed, jnp.exp2(x * (HD ** (-0.5) * LOG2_E)), 0.0) for x in scores]
+        parts = [dot_nn(weights[h].astype(BF), columns_of(kv_width + h * HD)) for h in range(kv_heads)]
         for h in range(kv_heads):
-            k_cols = slice(h * HD, (h + 1) * HD)
-            v_cols = slice(kv_width + h * HD, kv_width + (h + 1) * HD)
-            keys = jnp.concatenate([key_block(kv_ref, b, blocks, k_cols) for b in (block_a, block_b)], axis=0)
-            values = jnp.concatenate([key_block(kv_ref, b, blocks, v_cols) for b in (block_a, block_b)], axis=0)
-            scores = dot_nt(queries[h], keys)
-            weight = jnp.where(allowed, jnp.exp2(scores * (HD ** (-0.5) * LOG2_E)), 0.0)
-            part = weight[:, :HD]
-            for at in range(HD, 2 * tile_rows, HD):
-                part = part + weight[:, at : at + HD]
+            part = weights[h][:, :HD]
+            for at in range(HD, STEP * tile_rows, HD):
+                part = part + weights[h][:, at : at + HD]
             total_ref[h] += part
-            acc_ref[h] += dot_nn(weight.astype(BF), values)
+            acc_ref[h] += parts[h]
         return carry
 
-    lax.fori_loop(0, last // 2 + 1, body, 0)
+    lax.fori_loop(0, last // STEP + 1, body, 0)
     for h in range(kv_heads):
         total = jnp.sum(total_ref[h], axis=1, keepdims=True)
         out = (acc_ref[h] / total).astype(BF)
@@ -127,7 +129,7 @@
     ids = 2 + 2 * blocks
     row = lax.broadcasted_iota(jnp.int32, (1, stacked), 1) % tile_rows
     row_limit = jnp.minimum(start + (row ^ flip), length - 1)
-    column = lax.broadcasted_iota(jnp.int32, (2 * tile_rows, 1), 0) ^ flip
+    column = lax.broadcasted_iota(jnp.int32, (STEP * tile_rows, 1), 0) ^ flip
     score_scale = HD ** (-0.5)
 
     @pl.when(tile == 0)
@@ -144,26 +146,32 @@
     logs = [lse_ref[0, h] for h in range(kv_heads)]
 
     def body(step, carry):
-        pair = (meta[ids + 2 * step], meta[ids + 2 * step + 1])
-        allowed = step * (2 * tile_rows) + column <= row_limit
-        for h in range(kv_heads):
-            k_cols = slice(h * HD, (h + 1) * HD)
-            v_cols = slice(kv_width + h * HD, kv_width + (h + 1) * HD)
-            keys = jnp.concatenate([key_block(kv_ref, b, blocks, k_cols) for b in pair], axis=0)
-            values = jnp.concatenate([key_block(kv_ref, b, blocks, v_cols) for b in pair], axis=0)
-            scores = dot_nt(keys, queries[h])
-            probs = jnp.where(allowed, jnp.exp2(scores * (score_scale * LOG2_E) - logs[h]), 0.0)
-            dprob = dot_nt(values, grads[h])
-            dscore = (probs * (dprob - deltas[h])).astype(BF)
-            dv = dot_nn(probs.astype(BF), grads[h])
-            dk = dot_nn(dscore, queries[h])
-            for n, block in enumerate(pair):
-                sum_ref[block, :, k_cols] += dk[n * tile_rows : (n + 1) * tile_rows]
-                sum_ref[block, :, v_cols] += dv[n * tile_rows : (n + 1) * tile_rows]
-            dq_sum_ref[h] += dot_tn(dscore, keys)
+        taken = [meta[ids + STEP * step + n] for n in range(STEP)]
+        allowed = step * (STEP * tile_rows) + column <= row_limit
+
+        def columns_of(at):
+            return jnp.concatenate([key_block(kv_ref, b, blocks, slice(at, at + HD)) for b in taken], axis=0)
+
+        each = range(kv_heads)
+        keys = [columns_of(h * HD) for h in each]
+        scores = [dot_nt(keys[h], queries[h]) for h in each]
+        dprobs = [dot_nt(columns_of(kv_width + h * HD), grads[h]) for h in each]
+        probs = [
+            jnp.where(allowed, jnp.exp2(scores[h] * (score_scale * LOG2_E) - logs[h]), 0.0) for h in each
+        ]
+        dscores = [(probs[h] * (dprobs[h] - deltas[h])).astype(BF) for h in each]
+        dvs = [dot_nn(probs[h].astype(BF), grads[h]) for h in each]
+        dks = [dot_nn(dscores[h], queries[h]) for h in each]
+        dqs = [dot_tn(dscores[h], keys[h]) for h in each]
+        for h in each:
+            dq_sum_ref[h] += dqs[h]
+            for n, block in enumerate(taken):
+                part = slice(n * tile_rows, (n + 1) * tile_rows)
+                sum_ref[block, :, h * HD : (h + 1) * HD] += dks[h][part]
+                sum_ref[block, :, kv_width + h * HD : kv_width + (h + 1) * HD] += dvs[h][part]
         return carry
 
-    lax.fori_loop(0, jnp.where(start < length, start // tile_rows // 2 + 1, 0), body, 0)
+    lax.fori_loop(0, jnp.where(start < length, start // tile_rows // STEP + 1, 0), body, 0)
     for h in range(kv_heads):
         for g in range(per_key):
             head = h * per_key + g
@@ -553,12 +561,20 @@
     dy_b = jnp.concatenate([swap(dy_own, k) for k in steps], axis=0)
     grad_down_part, dy_after = together(dot_tn(hidden_act, dy_b).astype(BF), dy_b)
     grad_down = lax.psum_scatter(grad_down_part, "ctx", scatter_dimension=0, tiled=True)
+    out_part = dot_nn(hidden_act, w_down_full).reshape(groups, rows, width)
+    out_sent = [out_part[k].astype(BF) for k in steps[1:]]
+    dy_after, *out_sent = together(dy_after, *out_sent)
+    arrived = [swap(out_sent[k - 1], k) for k in steps[1:]]
     dhid = dot_nt(dy_after, w_down_full)
     _, swiglu_pull = jax.vjp(lambda g, u: jax.nn.silu(g) * u, gate_proj, up_proj)
     dgate_f, dup_f = swiglu_pull(dhid)
-    dgate, dup = dgate_f.astype(BF), dup_f.astype(BF)
+    dgate, dup, arrived[0] = together(dgate_f.astype(BF), dup_f.astype(BF), arrived[0])
     dn_two_part = dot_nt(jnp.concatenate([dgate, dup], axis=1), w_gate_up).reshape(groups, rows, width)
-    dn_two_part, normed_two = together(dn_two_part, normed_two)
+    dn_two_part, normed_two, *arrived = together(dn_two_part, normed_two, *arrived)
+    result = out_part[0] + hidden_res
+    for received in arrived:
+        result = result + received.astype(F32)
+    result = leave_plane(result.astype(BF).reshape(groups, piece, width))
     dn_two = dn_two_part[0]
     for k in steps[1:]:
         dn_two = dn_two + swap(dn_two_part[k].astype(BF), k).astype(F32)
@@ -574,18 +590,12 @@
     dh_rows = dy_own.astype(F32) + dh_norm
     dattn_own = dh_rows.astype(BF)
     dattn_b = jnp.concatenate([swap(dattn_own, k) for k in steps], axis=0)
-    out_part = dot_nn(hidden_act, w_down_full).reshape(groups, rows, width)
-    out_sent = [out_part[k].astype(BF) for k in steps[1:]]
-    dattn_b, grad_gate = together(dattn_b, grad_gate)
+    dattn_b, grad_gate, result = together(dattn_b, grad_gate, result)
+    result = from_plane(result, order_all)
     dmix_b = dot_nt(dattn_b, w_out_full).astype(BF)
-    dmix_b, grad_out_part, *out_sent = together(dmix_b, dot_tn(mix_b, dattn_b).astype(BF), *out_sent)
-    grad_out_w = lax.psum_scatter(grad_out_part, "ctx", scatter_dimension=0, tiled=True)
+    grad_out_w = lax.psum_scatter(dot_tn(mix_b, dattn_b).astype(BF), "ctx", scatter_dimension=0, tiled=True)
 
     dq_rot, dkv_parts = attention_backward(meta, queries, kv_all, dmix_b.reshape(queries.shape), mixture, logs)
-    result, dq_rot = together(out_part[0] + hidden_res, dq_rot)
-    for k in steps[1:]:
-        result = result + swap(out_sent[k - 1], k).astype(F32)
-    result = result.astype(BF)
     dkv_parts = dkv_parts.reshape(lanes, tokens, -1)
     other = swap_lane(dkv_parts[1], 1)
     for k in range(2, lanes):
@@ -595,18 +605,18 @@
     )
 
     dqkv, grad_up, result = together(dqkv, grad_up, result)
+    dn_one_part = dot_nt(dqkv, w_qkv).reshape(groups, rows, width)
+    dn_one_part, normed_one = together(dn_one_part, normed_one)
     grad_qkv_part = dot_tn(normed_one, dqkv).astype(BF).reshape(groups, -1, dqkv.shape[1])
     grad_qkv = lax.psum_scatter(grad_qkv_part, "ctx", scatter_dimension=1, tiled=True)
-    dn_one_part = dot_nt(dqkv, w_qkv).reshape(groups, rows, width)
     dn_one = dn_one_part[0]
     for k in steps[1:]:
         dn_one = dn_one + swap(dn_one_part[k].astype(BF), k).astype(F32)
-    result = leave_plane(result.reshape(groups, piece, width))
-    dn_one, grad_out_w, result = together(dn_one, grad_out_w, result)
-    result = from_plane(result, order_all)
+    dn_one, grad_out_w, grad_up = together(dn_one, grad_out_w, grad_up)
     _, norm_one_pull = jax.vjp(rms_scale, x_own.astype(F32), attn_gain_full)
     dflat_norm, dattn_gain_part = norm_one_pull(dn_one)
-    spread = leave_plane((dh_rows + dflat_norm).astype(BF).reshape(groups, piece, width))
+    grad_rows, dattn_gain_part = together((dh_rows + dflat_norm).astype(BF), dattn_gain_part)
+    spread = leave_plane(grad_rows.reshape(groups, piece, width))
     grad_w_query, grad_w_key, grad_w_value = from_columns(grad_qkv, [q_width, kv_width, kv_width])
     spread, grad_w_query = together(spread, grad_w_query)
     grad_x = from_plane(spread, each)

time: 825 us -> 802 us (0.972)
  starting transfers between devices: 136 us -> 108 us
  waiting for transfers between devices: 342 us -> 366 us
    ppermute x12, waiting for transfers between devices: 52 us -> 69.3 us  [swap_plane(): lax.ppermute(block, 'ctx', [(i, (i // lanes ^ step) * lanes + i % lanes)...]
    ppermute x12, starting transfers between devices: 49.5 us -> 33.1 us  [swap_plane(): lax.ppermute(block, 'ctx', [(i, (i // lanes ^ step) * lanes + i % lanes)...]
    ppermute x5, starting transfers between devices: 13.8 us -> 2.59 us  [scatter_all(): lax.ppermute(sent, axis, [(i, i ^ step) for i in range(count)])]
  transfers between devices with their start and end apart: 84 -> 84, of which waited for: 41 -> 43; matrix products, arithmetic and copies ran while one was open for 29% -> 28% of each run, Pallas kernels for 7% -> 7%
where the time goes in v3:
time: 802 us; the launch traced here: 795 us
  waiting for transfers between devices  366 us (46%)
  matrix products  123 us (15%)
  starting transfers between devices  108 us (13%)
  other arithmetic  76.9 us (10%)
  Pallas kernels  58.8 us (7%)
  local copies, waits for them, and re-layouts  40.1 us (5%)
  between operations  22.3 us (3%)
    ppermute x51, waiting for transfers between devices, swap(): return lax.ppermute(block, 'fsdp', [(i, i ^ step) for i in range(groups)])  281 us
    ppermute x12, waiting for transfers between devices, swap_plane(): lax.ppermute(block, 'ctx', [(i, (i // lanes ^ step) * lanes + i % lanes)...  69.3 us
    ppermute x51, starting transfers between devices, swap(): return lax.ppermute(block, 'fsdp', [(i, i ^ step) for i in range(groups)])  59.8 us
    dot_general x4, matrix products, dot_nt(): lax.dot_general(left, right, (((1,), (1,)), ((), ())), preferred_element_...  44.8 us
    dot_general x5, matrix products, dot_tn(): lax.dot_general(left, right, (((0,), (0,)), ((), ())), preferred_element_...  42.1 us
    dot_general x3, matrix products, dot_nn(): lax.dot_general(left, right, (((1,), (0,)), ((), ())), preferred_element_...  36.5 us
    ppermute x12, starting transfers between devices, swap_plane(): lax.ppermute(block, 'ctx', [(i, (i // lanes ^ step) * lanes + i % lanes)...  33.1 us
    pallas_call x1, Pallas kernels, attention_backward(): pl.pallas_call(functools.partial(attn_bwd_kernel, **sizes), grid_spec=plt...  22.5 us
  transfers between devices with their start and end apart: 84, of which 43 were waited for; matrix products, arithmetic and copies ran while one was open for 28% of the time, Pallas kernels for 7%

profile of v3, /device:TPU:0, one launch (start us, length us, event | category | flops | bytes accessed | tf_op | source)
XLA Modules:
  0.0 795.2 jit_solution(11355750526562735534)
XLA Ops:
  9.3 2.7 concatenate.100
  13.4 3.0 collective-permute-start.7
  17.9 3.1 collective-permute-start.8
  33.1 5.0 collective-permute-done.2
  38.1 2.8 collective-permute-done.1
  45.1 3.7 collective-permute-start.5
  49.8 6.3 collective-permute-done.5
  56.1 12.6 %collective-permute-done.4 = bf16[64,2048]{1,0:T(8,128)(2,1)S(1)} collective-permute-done((bf16[64,2048]{1,0:T(8,128)(2,1)S(1)}, bf16[64,2048]{1,0:T(8,128)(2,1)S(1)}, u32[]{:S(2)}, u32[]{:S(2)}) %collective-permute-start.4) | collective-permute-done | bytes 262176 | tf_op jit(solution)/shard_map/ppermute | solution.py:414
  82.6 16.0 %collective-permute-done.16 = bf16[256,2048]{1,0:T(8,128)(2,1)S(1)} collective-permute-done((bf16[256,2048]{1,0:T(8,128)(2,1)S(1)}, bf16[256,2048]{1,0:T(8,128)(2,1)S(1)}, u32[]{:S(2)}, u32[]{:S(2)}) %collective-permute-start.16) | collective-permute-done | bytes 1048608 | tf_op jit(solution)/shard_map/ppermute | solution.py:409
  98.7 20.6 %collective-permute-done.15 = bf16[256,2048]{1,0:T(8,128)(2,1)S(1)} collective-permute-done((bf16[256,2048]{1,0:T(8,128)(2,1)S(1)}, bf16[256,2048]{1,0:T(8,128)(2,1)S(1)}, u32[]{:S(2)}, u32[]{:S(2)}) %collective-permute-start.15) | collective-permute-done | bytes 1048608 | tf_op jit(solution)/shard_map/ppermute | solution.py:409
  119.3 3.3 pad_maximum_fusion.1.x_ref
  122.7 11.4 %shard_map.255 = (bf16[1024,2048]{1,0:T(8,128)(2,1)}, f32[1024,768]{1,0:T(8,128)}, bf16[1024,512]{1,0:T(8,128)(2,1)}, bf16[1024,512]{1,0:T(8,128)(2,1)}) custom-call(bf16[1024,2048]{1,0:T(8,128)(2,1)} %pad_maximum_fusion.1.x_ref, f32[1,2048]{1,0:T(1,128)} %broadcast_in_dim_reshape.6.gain_ref, bf16[2048,1024]{1,0:T(8,128)(2,1)} %bitcast.307, ...), custom_call_target="tpu_custom_call" | custom-call | flops 4294967296 | bytes 16777216 | tf_op jit(solution)/shard_map/pallas_call | solution.py:293
  138.2 8.1 %collective-permute-done.24 = bf16[64,3072]{1,0:T(8,128)(2,1)S(1)} collective-permute-done((bf16[64,3072]{1,0:T(8,128)(2,1)S(1)}, bf16[64,3072]{1,0:T(8,128)(2,1)S(1)}, u32[]{:S(2)}, u32[]{:S(2)}) %collective-permute-start.24) | collective-permute-done | bytes 393248 | tf_op jit(solution)/shard_map/ppermute | solution.py:409
  146.4 7.7 collective-permute-done.25
  159.0 2.9 pad_maximum_fusion.4.kv_ref
  161.9 17.3 %shard_map.256 = (bf16[2,2,4,64,512]{4,3,2,1,0:T(8,128)(2,1)}, f32[8,2,1,256]{3,2,1,0:T(1,128)}) custom-call(s32[26]{0:T(128)} %pad_add_fusion.2.meta, bf16[2,2,4,64,512]{4,3,2,1,0:T(8,128)(2,1)} %bitcast.310, bf16[2,2,2,4,64,512]{5,4,3,2,1,0:T(8,128)(2,1)} %pad_maximum_fusion.4.kv_ref), custom_call_target="tpu_custom_call" | custom-call | flops 2147483648 | bytes 4194304 | tf_op jit(solution)/shard_map/pallas_call | solution.py:212
  179.2 7.6 fusion.53
  195.6 46.9 %collective-permute-done.29 = bf16[64,2048]{1,0:T(8,128)(2,1)S(1)} collective-permute-done((bf16[64,2048]{1,0:T(8,128)(2,1)S(1)}, bf16[64,2048]{1,0:T(8,128)(2,1)S(1)}, u32[]{:S(2)}, u32[]{:S(2)}) %collective-permute-start.29) | collective-permute-done | bytes 262176 | tf_op jit(solution)/shard_map/ppermute | solution.py:409
  253.5 3.5 multiply_reduce_fusion.2
  263.4 11.7 %collective-permute-done.32 = bf16[64,2048]{1,0:T(8,128)(2,1)S(1)} collective-permute-done((bf16[64,2048]{1,0:T(8,128)(2,1)S(1)}, bf16[64,2048]{1,0:T(8,128)(2,1)S(1)}, u32[]{:S(2)}, u32[]{:S(2)}) %collective-permute-start.32) | collective-permute-done | bytes 262176 | tf_op jit(solution)/shard_map/ppermute | solution.py:414
  275.1 10.7 %collective-permute-start.30 = (bf16[64,2048]{1,0:T(8,128)(2,1)S(1)}, bf16[64,2048]{1,0:T(8,128)(2,1)}, u32[]{:S(2)}, u32[]{:S(2)}) collective-permute-start(bf16[64,2048]{1,0:T(8,128)(2,1)S(1)} %get-tuple-element.179), channel_id=1, source_target_pairs={{0,2},{1,3},{2,0},{3,1},{4,6},{5,7},{6,4},{7,5},{8,10},{9,11},{10,... | collective-permute-start | bytes 786440 | tf_op jit(solution)/shard_map/ppermute | solution.py:414
  286.6 4.4 collective-permute-done.31
  290.9 5.7 collective-permute-done.30
  298.1 7.3 collective-permute-done.22
  305.4 17.1 %fusion.35 = f32[1024,3072]{1,0:T(8,128)S(1)} fusion(bf16[2048,3072]{1,0:T(8,128)(2,1)} %bitcast.305, bf16[256,2048]{1,0:T(8,128)(2,1)} %collective-permute-done.23, bf16[256,2048]{1,0:T(8,128)(2,1)} %collective-permute-done.22, bf16[256,2048]{1,0:T(8,128)(2,1)} %collective-permute-done.21, bf16[256,2048]{1,0:T(8,128)(2,1)} %multiply_convert_fusion.2), kind=kOutput, calls=%fused_computation.247 | convolution fusion | flops 12901679104 | bytes 29360128 | tf_op jit(solution)/shard_map/dot_general | solution.py:36
  328.1 41.9 %collective-permute-done.33 = bf16[256,2048]{1,0:T(8,128)(2,1)S(1)} collective-permute-done((bf16[256,2048]{1,0:T(8,128)(2,1)S(1)}, bf16[256,2048]{1,0:T(8,128)(2,1)S(1)}, u32[]{:S(2)}, u32[]{:S(2)}) %collective-permute-start.33) | collective-permute-done | bytes 1048608 | tf_op jit(solution)/shard_map/ppermute | solution.py:409
  373.3 9.2 %convolution_convert_fusion.2 = bf16[1536,2048]{1,0:T(8,128)(2,1)} fusion(bf16[1024,1536]{1,0:T(8,128)(2,1)S(1)} %multiply_convert_fusion.1, bf16[1024,2048]{1,0:T(8,128)(2,1)S(1)} %constant_dynamic-update-slice_fusion), kind=kOutput, calls=%fused_computation.3 | convolution fusion | flops 6445596672 | bytes 13631488 | tf_op jit(solution)/shard_map/dot_general | solution.py:44
  382.6 3.8 pad_maximum_fusion.2
  386.4 11.9 %fusion.54 = (bf16[1024,2048]{1,0:T(8,128)(2,1)S(1)}, f32[1024,2048]{1,0:T(8,128)}) fusion(bf16[1024,1536]{1,0:T(8,128)(2,1)} %copy-done.12, bf16[1536,2048]{1,0:T(8,128)(2,1)} %all-gather.11.cloned.1.call-done), kind=kOutput, calls=%fused_computation.265 | convolution fusion | flops 6444548096 | bytes 22020096 | tf_op jit(solution)/shard_map/dot_general | solution.py:36
  403.3 14.9 %multiply_convert_fusion = (bf16[1024,1536]{1,0:T(8,128)(2,1)S(1)}, bf16[1024,1536]{1,0:T(8,128)(2,1)}) fusion(f32[1024,3072]{1,0:T(8,128)} %copy-done.7, bf16[1024,2048]{1,0:T(8,128)(2,1)S(1)} %copy-done.32, bf16[1536,2048]{1,0:T(8,128)(2,1)} %all-gather.11.cloned.1.call-done), kind=kOutput, calls=%fused_computation.8 | convolution fusion | flops 6464471040 | bytes 29360128 | tf_op jit(solution)/shard_map/dot_general | solution.py:40
  418.2 7.7 collective-permute-done.36
  426.8 2.9 pad_maximum_fusion
  429.8 17.3 %fusion.55 = f32[4,256,2048]{2,1,0:T(8,128)} fusion(bf16[4,256,3072]{2,1,0:T(8,128)(2,1)S(1)} %bitcast.273, bf16[2048,3072,1]{1,0,2:T(8,128)(2,1)} %bitcast.306), kind=kOutput, calls=%fused_computation.266 | convolution fusion | flops 12884901888 | bytes 27262976 | tf_op jit(solution)/shard_map/dot_general | solution.py:40
  448.4 8.9 %convolution_convert_fusion.1 = bf16[2048,1536]{1,0:T(8,128)(2,1)} fusion(bf16[1024,2048]{1,0:T(8,128)(2,1)S(1)} %copy-done.9, bf16[1024,1536]{1,0:T(8,128)(2,1)S(1)} %copy-done.11), kind=kOutput, calls=%fused_computation.2 | convolution fusion | flops 6445596672 | bytes 13631488 | tf_op jit(solution)/shard_map/dot_general | solution.py:44
  457.4 11.5 %convolution_convert_fusion = bf16[2048,1536]{1,0:T(8,128)(2,1)} fusion(bf16[1024,2048]{1,0:T(8,128)(2,1)} %pad_maximum_fusion.2, bf16[1024,1536]{1,0:T(8,128)(2,1)} %copy-done.10), kind=kOutput, calls=%fused_computation.1 | convolution fusion | flops 6445596672 | bytes 13631488 | tf_op jit(solution)/shard_map/dot_general | solution.py:44
  469.0 4.1 convert.25
  477.1 22.5 %collective-permute-done.39 = bf16[256,2048]{1,0:T(8,128)(2,1)S(1)} collective-permute-done((bf16[256,2048]{1,0:T(8,128)(2,1)S(1)}, bf16[256,2048]{1,0:T(8,128)(2,1)S(1)}, u32[]{:S(2)}, u32[]{:S(2)}) %collective-permute-start.39) | collective-permute-done | bytes 1048608 | tf_op jit(solution)/shard_map/ppermute | solution.py:409
  499.6 21.1 %collective-permute-done.41 = bf16[256,2048]{1,0:T(8,128)(2,1)S(1)} collective-permute-done((bf16[256,2048]{1,0:T(8,128)(2,1)S(1)}, bf16[256,2048]{1,0:T(8,128)(2,1)S(1)}, u32[]{:S(2)}, u32[]{:S(2)}) %collective-permute-start.41) | collective-permute-done | bytes 1048608 | tf_op jit(solution)/shard_map/ppermute | solution.py:409
  522.1 3.7 fusion.21
  528.2 4.7 fusion.17
  537.6 15.5 %collective-permute-done.47 = bf16[64,2048]{1,0:T(8,128)(2,1)S(1)} collective-permute-done((bf16[64,2048]{1,0:T(8,128)(2,1)S(1)}, bf16[64,2048]{1,0:T(8,128)(2,1)S(1)}, u32[]{:S(2)}, u32[]{:S(2)}) %collective-permute-start.47) | collective-permute-done | bytes 262176 | tf_op jit(solution)/shard_map/ppermute | solution.py:414
  553.1 10.5 %collective-permute-start.45 = (bf16[64,2048]{1,0:T(8,128)(2,1)S(1)}, bf16[64,2048]{1,0:T(8,128)(2,1)}, u32[]{:S(2)}, u32[]{:S(2)}) collective-permute-start(bf16[64,2048]{1,0:T(8,128)(2,1)S(1)} %get-tuple-element.175), channel_id=1, source_target_pairs={{0,2},{1,3},{2,0},{3,1},{4,6},{5,7},{6,4},{7,5},{8,10},{9,11},{10,... | collective-permute-start | bytes 786440 | tf_op jit(solution)/shard_map/ppermute | solution.py:414
  571.7 5.9 collective-permute-done.45
  578.8 4.0 pad_maximum_fusion.3
  590.8 5.6 convolution_convert_fusion.5
  596.3 22.5 %shard_map.257 = (f32[2,2,4,64,512]{4,3,2,1,0:T(8,128)}, bf16[2,2,2,4,64,512]{5,4,3,2,1,0:T(8,128)(2,1)}) custom-call(s32[26]{0:T(128)} %pad_add_fusion.2.meta, bf16[2,2,4,64,512]{4,3,2,1,0:T(8,128)(2,1)} %bitcast.311, bf16[2,2,2,4,64,512]{5,4,3,2,1,0:T(8,128)(2,1)} %pad_maximum_fusion.4.kv_ref, bf16[2,2,4,64,512]{4,3,2,1,0:T(8,128)(2,1)} %bitcast.312, ...), custom_call_target="tpu_custom_call" | custom-call | flops 5368709120 | bytes 10485760 | tf_op jit(solution)/shard_map/pallas_call | solution.py:238
  618.8 5.9 convolution_convert_fusion.4
  624.7 3.1 fusion.40
  634.3 7.7 shard_map.258
  642.0 7.1 fusion.56
  649.7 2.7 copy-done.6
  657.7 6.5 convolution_convert_fusion.3
  668.8 11.7 %collective-permute-done.52 = bf16[256,2048]{1,0:T(8,128)(2,1)} collective-permute-done((bf16[256,2048]{1,0:T(8,128)(2,1)}, bf16[256,2048]{1,0:T(8,128)(2,1)}, u32[]{:S(2)}, u32[]{:S(2)}) %collective-permute-start.52) | collective-permute-done | bytes 1048608 | tf_op jit(solution)/shard_map/ppermute | solution.py:409
  680.5 23.6 %collective-permute-done.54 = bf16[256,2048]{1,0:T(8,128)(2,1)} collective-permute-done((bf16[256,2048]{1,0:T(8,128)(2,1)}, bf16[256,2048]{1,0:T(8,128)(2,1)}, u32[]{:S(2)}, u32[]{:S(2)}) %collective-permute-start.54) | collective-permute-done | bytes 1048608 | tf_op jit(solution)/shard_map/ppermute | solution.py:409
  706.3 4.6 fusion.19
  713.4 3.8 fusion.6
  726.3 3.2 collective-permute-done.66
  734.3 4.1 collective-permute-start.57
  742.3 7.7 collective-permute-done.72
  751.4 4.6 collective-permute-done.73
  756.0 4.9 collective-permute-done.56
  766.0 4.5 collective-permute-done.58
  775.1 6.5 collective-permute-done.63
  781.7 4.5 collective-permute-done.62
  (415 shorter events, 164.8 us)
Async XLA Ops:
  7.2 115.4 %all-gather.5.cloned.1.call-start = ((), (), s32[]{:S(2)}) async-start(), calls=%async_computation.5 | async-start | bytes 4718592 | tf_op jit(solution)/shard_map/all_gather | solution.py:532
  29.6 8.6 %collective-permute-start.2 = (bf16[64,2048]{1,0:T(8,128)(2,1)S(1)}, bf16[64,2048]{1,0:T(8,128)(2,1)S(1)}, u32[]{:S(2)}, u32[]{:S(2)}) collective-permute-start(bf16[64,2048]{1,0:T(8,128)(2,1)S(1)} %get-tuple-element.189), channel_id=1, source_target_pairs={{0,24},{8,16},{16,8},{24,0},{1,25},{9,17},{17,9},{25,1},{2,26},{10... | collective-permute-start | bytes 786440 | tf_op jit(solution)/shard_map/ppermute | solution.py:409
  31.1 9.9 %collective-permute-start.1 = (bf16[64,2048]{1,0:T(8,128)(2,1)S(1)}, bf16[64,2048]{1,0:T(8,128)(2,1)S(1)}, u32[]{:S(2)}, u32[]{:S(2)}) collective-permute-start(bf16[64,2048]{1,0:T(8,128)(2,1)S(1)} %get-tuple-element.190), channel_id=1, source_target_pairs={{0,16},{8,24},{16,0},{24,8},{1,17},{9,25},{17,1},{25,9},{2,18},{10... | collective-permute-start | bytes 786440 | tf_op jit(solution)/shard_map/ppermute | solution.py:409
  45.1 11.0 %collective-permute-start.5 = (bf16[64,2048]{1,0:T(8,128)(2,1)S(1)}, bf16[64,2048]{1,0:T(8,128)(2,1)S(1)}, u32[]{:S(2)}, u32[]{:S(2)}) collective-permute-start(bf16[64,2048]{1,0:T(8,128)(2,1)S(1)} %get-tuple-element.185), channel_id=1, source_target_pairs={{0,6},{1,7},{2,4},{3,5},{4,2},{5,3},{6,0},{7,1},{8,14},{9,15},{10,... | collective-permute-start | bytes 786440 | tf_op jit(solution)/shard_map/ppermute | solution.py:414
  48.7 19.9 %collective-permute-start.4 = (bf16[64,2048]{1,0:T(8,128)(2,1)S(1)}, bf16[64,2048]{1,0:T(8,128)(2,1)S(1)}, u32[]{:S(2)}, u32[]{:S(2)}) collective-permute-start(bf16[64,2048]{1,0:T(8,128)(2,1)S(1)} %get-tuple-element.186), channel_id=1, source_target_pairs={{0,4},{1,5},{2,6},{3,7},{4,0},{5,1},{6,2},{7,3},{8,12},{9,13},{10,... | collective-permute-start | bytes 786440 | tf_op jit(solution)/shard_map/ppermute | solution.py:414
  48.8 19.8 %collective-permute-start.3 = (bf16[64,2048]{1,0:T(8,128)(2,1)S(1)}, bf16[64,2048]{1,0:T(8,128)(2,1)S(1)}, u32[]{:S(2)}, u32[]{:S(2)}) collective-permute-start(bf16[64,2048]{1,0:T(8,128)(2,1)S(1)} %get-tuple-element.187), channel_id=1, source_target_pairs={{0,2},{1,3},{2,0},{3,1},{4,6},{5,7},{6,4},{7,5},{8,10},{9,11},{10,... | collective-permute-start | bytes 786440 | tf_op jit(solution)/shard_map/ppermute | solution.py:414
  70.5 108.7 %all-gather.7.cloned.1.call-start = ((), (), s32[]{:S(2)}) async-start(), calls=%async_computation.6 | async-start | bytes 2359296 | tf_op jit(solution)/shard_map/all_gather | solution.py:533
  71.2 234.2 %all-gather.9.cloned.1.call-start = ((), (), s32[]{:S(2)}) async-start(), calls=%async_computation.7 | async-start | bytes 14155776 | tf_op jit(solution)/shard_map/all_gather | solution.py:541
  71.6 27.0 %collective-permute-start.16 = (bf16[256,2048]{1,0:T(8,128)(2,1)S(1)}, bf16[256,2048]{1,0:T(8,128)(2,1)S(1)}, u32[]{:S(2)}, u32[]{:S(2)}) collective-permute-start(bf16[256,2048]{1,0:T(8,128)(2,1)S(1)} %pad_maximum_fusion.6), channel_id=1, source_target_pairs={{0,24},{8,16},{16,8},{24,0},{1,25},{9,17},{17,9},{25,1},{2,26},{10... | collective-permute-start | bytes 3145736 | tf_op jit(solution)/shard_map/ppermute | solution.py:409
  73.1 46.2 %collective-permute-start.15 = (bf16[256,2048]{1,0:T(8,128)(2,1)S(1)}, bf16[256,2048]{1,0:T(8,128)(2,1)S(1)}, u32[]{:S(2)}, u32[]{:S(2)}) collective-permute-start(bf16[256,2048]{1,0:T(8,128)(2,1)S(1)} %pad_maximum_fusion.6), channel_id=1, source_target_pairs={{0,16},{8,24},{16,0},{24,8},{1,17},{9,25},{17,1},{25,9},{2,18},{10... | collective-permute-start | bytes 3145736 | tf_op jit(solution)/shard_map/ppermute | solution.py:409
  73.9 45.4 %collective-permute-start.14 = (bf16[256,2048]{1,0:T(8,128)(2,1)S(1)}, bf16[256,2048]{1,0:T(8,128)(2,1)}, u32[]{:S(2)}, u32[]{:S(2)}) collective-permute-start(bf16[256,2048]{1,0:T(8,128)(2,1)S(1)} %pad_maximum_fusion.6), channel_id=1, source_target_pairs={{0,8},{8,0},{16,24},{24,16},{1,9},{9,1},{17,25},{25,17},{2,10},{10... | collective-permute-start | bytes 3145736 | tf_op jit(solution)/shard_map/ppermute | solution.py:409
  134.3 12.1 %collective-permute-start.24 = (bf16[64,3072]{1,0:T(8,128)(2,1)S(1)}, bf16[64,3072]{1,0:T(8,128)(2,1)S(1)}, u32[]{:S(2)}, u32[]{:S(2)}) collective-permute-start(bf16[64,3072]{1,0:T(8,128)(2,1)S(1)} %pad_maximum_fusion.18), channel_id=1, source_target_pairs={{0,8},{8,0},{16,24},{24,16},{1,9},{9,1},{17,25},{25,17},{2,10},{10... | collective-permute-start | bytes 1179656 | tf_op jit(solution)/shard_map/ppermute | solution.py:409
  134.8 19.2 %collective-permute-start.25 = (bf16[64,3072]{1,0:T(8,128)(2,1)S(1)}, bf16[64,3072]{1,0:T(8,128)(2,1)S(1)}, u32[]{:S(2)}, u32[]{:S(2)}) collective-permute-start(bf16[64,3072]{1,0:T(8,128)(2,1)S(1)} %pad_maximum_fusion.19), channel_id=1, source_target_pairs={{0,16},{8,24},{16,0},{24,8},{1,17},{9,25},{17,1},{25,9},{2,18},{10... | collective-permute-start | bytes 1179656 | tf_op jit(solution)/shard_map/ppermute | solution.py:409
  136.2 17.9 %collective-permute-start.26 = (bf16[64,3072]{1,0:T(8,128)(2,1)S(1)}, bf16[64,3072]{1,0:T(8,128)(2,1)S(1)}, u32[]{:S(2)}, u32[]{:S(2)}) collective-permute-start(bf16[64,3072]{1,0:T(8,128)(2,1)S(1)} %pad_maximum_fusion.20), channel_id=1, source_target_pairs={{0,24},{8,16},{16,8},{24,0},{1,25},{9,17},{17,9},{25,1},{2,26},{10... | collective-permute-start | bytes 1179656 | tf_op jit(solution)/shard_map/ppermute | solution.py:409
  155.3 231.1 %all-gather.11.cloned.1.call-start = ((), (), s32[]{:S(2)}) async-start(), calls=%async_computation.8 | async-start | bytes 7077888 | tf_op jit(solution)/shard_map/all_gather | solution.py:542
  155.9 369.8 %reduce-scatter.6.cloned.1.call-start = ((), (), s32[]{:S(2)}) async-start(), calls=%async_computation.9 | async-start | bytes 7077888 | tf_op jit(solution)/shard_map/reduce_scatter | solution.py:563
  188.4 63.8 %collective-permute-start.18 = (bf16[256,2048]{1,0:T(8,128)(2,1)}, bf16[256,2048]{1,0:T(8,128)(2,1)S(1)}, u32[]{:S(2)}, u32[]{:S(2)}) collective-permute-start(bf16[256,2048]{1,0:T(8,128)(2,1)} %get-tuple-element.144), channel_id=1, source_target_pairs={{0,8},{8,0},{16,24},{24,16},{1,9},{9,1},{17,25},{25,17},{2,10},{10... | collective-permute-start | bytes 3145736 | tf_op jit(solution)/shard_map/ppermute | solution.py:409
  189.7 62.5 %collective-permute-start.20 = (bf16[256,2048]{1,0:T(8,128)(2,1)}, bf16[256,2048]{1,0:T(8,128)(2,1)S(1)}, u32[]{:S(2)}, u32[]{:S(2)}) collective-permute-start(bf16[256,2048]{1,0:T(8,128)(2,1)} %get-tuple-element.145), channel_id=1, source_target_pairs={{0,24},{8,16},{16,8},{24,0},{1,25},{9,17},{17,9},{25,1},{2,26},{10... | collective-permute-start | bytes 3145736 | tf_op jit(solution)/shard_map/ppermute | solution.py:409
  191.0 61.3 %collective-permute-start.19 = (bf16[256,2048]{1,0:T(8,128)(2,1)}, bf16[256,2048]{1,0:T(8,128)(2,1)}, u32[]{:S(2)}, u32[]{:S(2)}) collective-permute-start(bf16[256,2048]{1,0:T(8,128)(2,1)} %get-tuple-element.146), channel_id=1, source_target_pairs={{0,16},{8,24},{16,0},{24,8},{1,17},{9,25},{17,1},{25,9},{2,18},{10... | collective-permute-start | bytes 3145736 | tf_op jit(solution)/shard_map/ppermute | solution.py:409
  192.8 49.6 %collective-permute-start.29 = (bf16[64,2048]{1,0:T(8,128)(2,1)S(1)}, bf16[64,2048]{1,0:T(8,128)(2,1)S(1)}, u32[]{:S(2)}, u32[]{:S(2)}) collective-permute-start(bf16[64,2048]{1,0:T(8,128)(2,1)S(1)} %get-tuple-element.181), channel_id=1, source_target_pairs={{0,24},{8,16},{16,8},{24,0},{1,25},{9,17},{17,9},{25,1},{2,26},{10... | collective-permute-start | bytes 786440 | tf_op jit(solution)/shard_map/ppermute | solution.py:409
  194.0 55.6 %collective-permute-start.28 = (bf16[64,2048]{1,0:T(8,128)(2,1)}, bf16[64,2048]{1,0:T(8,128)(2,1)}, u32[]{:S(2)}, u32[]{:S(2)}) collective-permute-start(bf16[64,2048]{1,0:T(8,128)(2,1)} %get-tuple-element.182), channel_id=1, source_target_pairs={{0,16},{8,24},{16,0},{24,8},{1,17},{9,25},{17,1},{25,9},{2,18},{10... | collective-permute-start | bytes 786440 | tf_op jit(solution)/shard_map/ppermute | solution.py:409
  258.3 39.8 %collective-permute-start.23 = (bf16[256,2048]{1,0:T(8,128)(2,1)}, bf16[256,2048]{1,0:T(8,128)(2,1)}, u32[]{:S(2)}, u32[]{:S(2)}) collective-permute-start(bf16[256,2048]{1,0:T(8,128)(2,1)} %multiply_convert_fusion.2), channel_id=1, source_target_pairs={{0,24},{8,16},{16,8},{24,0},{1,25},{9,17},{17,9},{25,1},{2,26},{10... | collective-permute-start | bytes 3145736 | tf_op jit(solution)/shard_map/ppermute | solution.py:409
  259.8 45.6 %collective-permute-start.22 = (bf16[256,2048]{1,0:T(8,128)(2,1)}, bf16[256,2048]{1,0:T(8,128)(2,1)}, u32[]{:S(2)}, u32[]{:S(2)}) collective-permute-start(bf16[256,2048]{1,0:T(8,128)(2,1)} %multiply_convert_fusion.2), channel_id=1, source_target_pairs={{0,16},{8,24},{16,0},{24,8},{1,17},{9,25},{17,1},{25,9},{2,18},{10... | collective-permute-start | bytes 3145736 | tf_op jit(solution)/shard_map/ppermute | solution.py:409
  260.3 45.1 %collective-permute-start.21 = (bf16[256,2048]{1,0:T(8,128)(2,1)}, bf16[256,2048]{1,0:T(8,128)(2,1)}, u32[]{:S(2)}, u32[]{:S(2)}) collective-permute-start(bf16[256,2048]{1,0:T(8,128)(2,1)} %multiply_convert_fusion.2), channel_id=1, source_target_pairs={{0,8},{8,0},{16,24},{24,16},{1,9},{9,1},{17,25},{25,17},{2,10},{10... | collective-permute-start | bytes 3145736 | tf_op jit(solution)/shard_map/ppermute | solution.py:409
  261.8 13.3 %collective-permute-start.32 = (bf16[64,2048]{1,0:T(8,128)(2,1)S(1)}, bf16[64,2048]{1,0:T(8,128)(2,1)S(1)}, u32[]{:S(2)}, u32[]{:S(2)}) collective-permute-start(bf16[64,2048]{1,0:T(8,128)(2,1)S(1)} %get-tuple-element.177), channel_id=1, source_target_pairs={{0,6},{1,7},{2,4},{3,5},{4,2},{5,3},{6,0},{7,1},{8,14},{9,15},{10,... | collective-permute-start | bytes 786440 | tf_op jit(solution)/shard_map/ppermute | solution.py:414
  263.4 27.5 %collective-permute-start.31 = (bf16[64,2048]{1,0:T(8,128)(2,1)S(1)}, bf16[64,2048]{1,0:T(8,128)(2,1)S(1)}, u32[]{:S(2)}, u32[]{:S(2)}) collective-permute-start(bf16[64,2048]{1,0:T(8,128)(2,1)S(1)} %get-tuple-element.178), channel_id=1, source_target_pairs={{0,4},{1,5},{2,6},{3,7},{4,0},{5,1},{6,2},{7,3},{8,12},{9,13},{10,... | collective-permute-start | bytes 786440 | tf_op jit(solution)/shard_map/ppermute | solution.py:414
  275.1 21.5 %collective-permute-start.30 = (bf16[64,2048]{1,0:T(8,128)(2,1)S(1)}, bf16[64,2048]{1,0:T(8,128)(2,1)}, u32[]{:S(2)}, u32[]{:S(2)}) collective-permute-start(bf16[64,2048]{1,0:T(8,128)(2,1)S(1)} %get-tuple-element.179), channel_id=1, source_target_pairs={{0,2},{1,3},{2,0},{3,1},{4,6},{5,7},{6,4},{7,5},{8,10},{9,11},{10,... | collective-permute-start | bytes 786440 | tf_op jit(solution)/shard_map/ppermute | solution.py:414
  322.5 48.6 %collective-permute-start.35 = (bf16[256,2048]{1,0:T(8,128)(2,1)S(1)}, bf16[256,2048]{1,0:T(8,128)(2,1)S(1)}, u32[]{:S(2)}, u32[]{:S(2)}) collective-permute-start(bf16[256,2048]{1,0:T(8,128)(2,1)S(1)} %maximum_select_fusion), channel_id=1, source_target_pairs={{0,24},{8,16},{16,8},{24,0},{1,25},{9,17},{17,9},{25,1},{2,26},{10... | collective-permute-start | bytes 3145736 | tf_op jit(solution)/shard_map/ppermute | solution.py:409
  324.1 47.0 %collective-permute-start.34 = (bf16[256,2048]{1,0:T(8,128)(2,1)S(1)}, bf16[256,2048]{1,0:T(8,128)(2,1)S(1)}, u32[]{:S(2)}, u32[]{:S(2)}) collective-permute-start(bf16[256,2048]{1,0:T(8,128)(2,1)S(1)} %maximum_select_fusion), channel_id=1, source_target_pairs={{0,16},{8,24},{16,0},{24,8},{1,17},{9,25},{17,1},{25,9},{2,18},{10... | collective-permute-start | bytes 3145736 | tf_op jit(solution)/shard_map/ppermute | solution.py:409
  324.7 45.4 %collective-permute-start.33 = (bf16[256,2048]{1,0:T(8,128)(2,1)S(1)}, bf16[256,2048]{1,0:T(8,128)(2,1)S(1)}, u32[]{:S(2)}, u32[]{:S(2)}) collective-permute-start(bf16[256,2048]{1,0:T(8,128)(2,1)S(1)} %maximum_select_fusion), channel_id=1, source_target_pairs={{0,8},{8,0},{16,24},{24,16},{1,9},{9,1},{17,25},{25,17},{2,10},{10... | collective-permute-start | bytes 3145736 | tf_op jit(solution)/shard_map/ppermute | solution.py:409
  382.5 200.2 %reduce-scatter.8.cloned.1.call-start = ((), (), s32[]{:S(2)}) async-start(), calls=%async_computation.10 | async-start | bytes 7077888 | tf_op jit(solution)/shard_map/reduce_scatter | solution.py:581
  399.8 26.0 %collective-permute-start.36 = (bf16[256,2048]{1,0:T(8,128)(2,1)S(1)}, bf16[256,2048]{1,0:T(8,128)(2,1)S(1)}, u32[]{:S(2)}, u32[]{:S(2)}) collective-permute-start(bf16[256,2048]{1,0:T(8,128)(2,1)S(1)} %get-tuple-element.87), channel_id=1, source_target_pairs={{0,8},{8,0},{16,24},{24,16},{1,9},{9,1},{17,25},{25,17},{2,10},{10... | collective-permute-start | bytes 3145736 | tf_op jit(solution)/shard_map/ppermute | solution.py:409
  400.9 47.4 %collective-permute-start.37 = (bf16[256,2048]{1,0:T(8,128)(2,1)}, bf16[256,2048]{1,0:T(8,128)(2,1)}, u32[]{:S(2)}, u32[]{:S(2)}) collective-permute-start(bf16[256,2048]{1,0:T(8,128)(2,1)} %get-tuple-element.91), channel_id=1, source_target_pairs={{0,16},{8,24},{16,0},{24,8},{1,17},{9,25},{17,1},{25,9},{2,18},{10... | collective-permute-start | bytes 3145736 | tf_op jit(solution)/shard_map/ppermute | solution.py:409
  402.2 46.2 %collective-permute-start.38 = (bf16[256,2048]{1,0:T(8,128)(2,1)}, bf16[256,2048]{1,0:T(8,128)(2,1)}, u32[]{:S(2)}, u32[]{:S(2)}) collective-permute-start(bf16[256,2048]{1,0:T(8,128)(2,1)} %get-tuple-element.92), channel_id=1, source_target_pairs={{0,24},{8,16},{16,8},{24,0},{1,25},{9,17},{17,9},{25,1},{2,26},{10... | collective-permute-start | bytes 3145736 | tf_op jit(solution)/shard_map/ppermute | solution.py:409
  457.3 184.6 %reduce-scatter.10.cloned.1.call-start = ((), (), s32[]{:S(2)}) async-start(), calls=%async_computation.11 | async-start | bytes 7077888 | tf_op jit(solution)/shard_map/reduce_scatter | solution.py:584
  468.9 242.0 %reduce-scatter.12.cloned.1.call-start = ((), (), s32[]{:S(2)}) async-start(), calls=%async_computation.12 | async-start | bytes 2359296 | tf_op jit(solution)/shard_map/reduce_scatter | solution.py:596
  473.5 26.1 %collective-permute-start.39 = (bf16[256,2048]{1,0:T(8,128)(2,1)S(1)}, bf16[256,2048]{1,0:T(8,128)(2,1)S(1)}, u32[]{:S(2)}, u32[]{:S(2)}) collective-permute-start(bf16[256,2048]{1,0:T(8,128)(2,1)S(1)} %get-tuple-element.138), channel_id=1, source_target_pairs={{0,8},{8,0},{16,24},{24,16},{1,9},{9,1},{17,25},{25,17},{2,10},{10... | collective-permute-start | bytes 3145736 | tf_op jit(solution)/shard_map/ppermute | solution.py:409
  474.8 45.9 %collective-permute-start.41 = (bf16[256,2048]{1,0:T(8,128)(2,1)S(1)}, bf16[256,2048]{1,0:T(8,128)(2,1)S(1)}, u32[]{:S(2)}, u32[]{:S(2)}) collective-permute-start(bf16[256,2048]{1,0:T(8,128)(2,1)S(1)} %get-tuple-element.139), channel_id=1, source_target_pairs={{0,24},{8,16},{16,8},{24,0},{1,25},{9,17},{17,9},{25,1},{2,26},{10... | collective-permute-start | bytes 3145736 | tf_op jit(solution)/shard_map/ppermute | solution.py:409
  476.5 45.6 %collective-permute-start.40 = (bf16[256,2048]{1,0:T(8,128)(2,1)S(1)}, bf16[256,2048]{1,0:T(8,128)(2,1)S(1)}, u32[]{:S(2)}, u32[]{:S(2)}) collective-permute-start(bf16[256,2048]{1,0:T(8,128)(2,1)S(1)} %get-tuple-element.140), channel_id=1, source_target_pairs={{0,16},{8,24},{16,0},{24,8},{1,17},{9,25},{17,1},{25,9},{2,18},{10... | collective-permute-start | bytes 3145736 | tf_op jit(solution)/shard_map/ppermute | solution.py:409
  532.9 45.9 %collective-permute-start.44 = (bf16[256,2048]{1,0:T(8,128)(2,1)}, bf16[256,2048]{1,0:T(8,128)(2,1)}, u32[]{:S(2)}, u32[]{:S(2)}) collective-permute-start(bf16[256,2048]{1,0:T(8,128)(2,1)} %get-tuple-element.150), channel_id=1, source_target_pairs={{0,24},{8,16},{16,8},{24,0},{1,25},{9,17},{17,9},{25,1},{2,26},{10... | collective-permute-start | bytes 3145736 | tf_op jit(solution)/shard_map/ppermute | solution.py:409
  534.4 44.4 %collective-permute-start.43 = (bf16[256,2048]{1,0:T(8,128)(2,1)}, bf16[256,2048]{1,0:T(8,128)(2,1)}, u32[]{:S(2)}, u32[]{:S(2)}) collective-permute-start(bf16[256,2048]{1,0:T(8,128)(2,1)} %get-tuple-element.150), channel_id=1, source_target_pairs={{0,16},{8,24},{16,0},{24,8},{1,17},{9,25},{17,1},{25,9},{2,18},{10... | collective-permute-start | bytes 3145736 | tf_op jit(solution)/shard_map/ppermute | solution.py:409
  534.8 44.0 %collective-permute-start.42 = (bf16[256,2048]{1,0:T(8,128)(2,1)}, bf16[256,2048]{1,0:T(8,128)(2,1)}, u32[]{:S(2)}, u32[]{:S(2)}) collective-permute-start(bf16[256,2048]{1,0:T(8,128)(2,1)} %get-tuple-element.150), channel_id=1, source_target_pairs={{0,8},{8,0},{16,24},{24,16},{1,9},{9,1},{17,25},{25,17},{2,10},{10... | collective-permute-start | bytes 3145736 | tf_op jit(solution)/shard_map/ppermute | solution.py:409
  536.5 16.7 %collective-permute-start.47 = (bf16[64,2048]{1,0:T(8,128)(2,1)S(1)}, bf16[64,2048]{1,0:T(8,128)(2,1)S(1)}, u32[]{:S(2)}, u32[]{:S(2)}) collective-permute-start(bf16[64,2048]{1,0:T(8,128)(2,1)S(1)} %get-tuple-element.173), channel_id=1, source_target_pairs={{0,6},{1,7},{2,4},{3,5},{4,2},{5,3},{6,0},{7,1},{8,14},{9,15},{10,... | collective-permute-start | bytes 786440 | tf_op jit(solution)/shard_map/ppermute | solution.py:414
  537.6 34.0 %collective-permute-start.46 = (bf16[64,2048]{1,0:T(8,128)(2,1)S(1)}, bf16[64,2048]{1,0:T(8,128)(2,1)S(1)}, u32[]{:S(2)}, u32[]{:S(2)}) collective-permute-start(bf16[64,2048]{1,0:T(8,128)(2,1)S(1)} %get-tuple-element.174), channel_id=1, source_target_pairs={{0,4},{1,5},{2,6},{3,7},{4,0},{5,1},{6,2},{7,3},{8,12},{9,13},{10,... | collective-permute-start | bytes 786440 | tf_op jit(solution)/shard_map/ppermute | solution.py:414
  553.1 24.4 %collective-permute-start.45 = (bf16[64,2048]{1,0:T(8,128)(2,1)S(1)}, bf16[64,2048]{1,0:T(8,128)(2,1)}, u32[]{:S(2)}, u32[]{:S(2)}) collective-permute-start(bf16[64,2048]{1,0:T(8,128)(2,1)S(1)} %get-tuple-element.175), channel_id=1, source_target_pairs={{0,2},{1,3},{2,0},{3,1},{4,6},{5,7},{6,4},{7,5},{8,10},{9,11},{10,... | collective-permute-start | bytes 786440 | tf_op jit(solution)/shard_map/ppermute | solution.py:414
  584.9 136.8 %collective-permute-start.71 = (bf16[64,1536]{1,0:T(8,128)(2,1)}, bf16[64,1536]{1,0:T(8,128)(2,1)}, u32[]{:S(2)}, u32[]{:S(2)}) collective-permute-start(bf16[64,1536]{1,0:T(8,128)(2,1)} %get-tuple-element.195), channel_id=1, source_target_pairs={{0,24},{8,16},{16,8},{24,0},{1,25},{9,17},{17,9},{25,1},{2,26},{10... | collective-permute-start | bytes 589832 | tf_op jit(solution)/shard_map/ppermute | solution.py:409
  586.0 78.2 %collective-permute-start.69 = (bf16[64,1536]{1,0:T(8,128)(2,1)}, bf16[64,1536]{1,0:T(8,128)(2,1)}, u32[]{:S(2)}, u32[]{:S(2)}) collective-permute-start(bf16[64,1536]{1,0:T(8,128)(2,1)} %get-tuple-element.197), channel_id=1, source_target_pairs={{0,8},{8,0},{16,24},{24,16},{1,9},{9,1},{17,25},{25,17},{2,10},{10... | collective-permute-start | bytes 589832 | tf_op jit(solution)/shard_map/ppermute | solution.py:409
  587.3 41.7 %collective-permute-start.51 = (bf16[64,2048]{1,0:T(8,128)(2,1)}, bf16[64,2048]{1,0:T(8,128)(2,1)}, u32[]{:S(2)}, u32[]{:S(2)}) collective-permute-start(bf16[64,2048]{1,0:T(8,128)(2,1)} %get-tuple-element.169), channel_id=1, source_target_pairs={{0,24},{8,16},{16,8},{24,0},{1,25},{9,17},{17,9},{25,1},{2,26},{10... | collective-permute-start | bytes 786440 | tf_op jit(solution)/shard_map/ppermute | solution.py:409
  589.1 41.2 %collective-permute-start.50 = (bf16[64,2048]{1,0:T(8,128)(2,1)}, bf16[64,2048]{1,0:T(8,128)(2,1)}, u32[]{:S(2)}, u32[]{:S(2)}) collective-permute-start(bf16[64,2048]{1,0:T(8,128)(2,1)} %get-tuple-element.170), channel_id=1, source_target_pairs={{0,16},{8,24},{16,0},{24,8},{1,17},{9,25},{17,1},{25,9},{2,18},{10... | collective-permute-start | bytes 786440 | tf_op jit(solution)/shard_map/ppermute | solution.py:409
  590.4 39.9 %collective-permute-start.49 = (bf16[64,2048]{1,0:T(8,128)(2,1)}, bf16[64,2048]{1,0:T(8,128)(2,1)}, u32[]{:S(2)}, u32[]{:S(2)}) collective-permute-start(bf16[64,2048]{1,0:T(8,128)(2,1)} %get-tuple-element.171), channel_id=1, source_target_pairs={{0,8},{8,0},{16,24},{24,16},{1,9},{9,1},{17,25},{25,17},{2,10},{10... | collective-permute-start | bytes 786440 | tf_op jit(solution)/shard_map/ppermute | solution.py:409
  627.8 133.3 %reduce-scatter.14.cloned.1.call-start = ((), (), s32[]{:S(2)}) async-start(), calls=%async_computation.13 | async-start | bytes 4718592 | tf_op jit(solution)/shard_map/reduce_scatter | solution.py:611
  654.2 26.3 %collective-permute-start.52 = (bf16[256,2048]{1,0:T(8,128)(2,1)}, bf16[256,2048]{1,0:T(8,128)(2,1)}, u32[]{:S(2)}, u32[]{:S(2)}) collective-permute-start(bf16[256,2048]{1,0:T(8,128)(2,1)} %get-tuple-element.135), channel_id=1, source_target_pairs={{0,8},{8,0},{16,24},{24,16},{1,9},{9,1},{17,25},{25,17},{2,10},{10... | collective-permute-start | bytes 3145736 | tf_op jit(solution)/shard_map/ppermute | solution.py:409
  656.0 48.2 %collective-permute-start.54 = (bf16[256,2048]{1,0:T(8,128)(2,1)}, bf16[256,2048]{1,0:T(8,128)(2,1)}, u32[]{:S(2)}, u32[]{:S(2)}) collective-permute-start(bf16[256,2048]{1,0:T(8,128)(2,1)} %get-tuple-element.136), channel_id=1, source_target_pairs={{0,24},{8,16},{16,8},{24,0},{1,25},{9,17},{17,9},{25,1},{2,26},{10... | collective-permute-start | bytes 3145736 | tf_op jit(solution)/shard_map/ppermute | solution.py:409
  657.5 48.8 %collective-permute-start.53 = (bf16[256,2048]{1,0:T(8,128)(2,1)}, bf16[256,2048]{1,0:T(8,128)(2,1)}, u32[]{:S(2)}, u32[]{:S(2)}) collective-permute-start(bf16[256,2048]{1,0:T(8,128)(2,1)} %get-tuple-element.137), channel_id=1, source_target_pairs={{0,16},{8,24},{16,0},{24,8},{1,17},{9,25},{17,1},{25,9},{2,18},{10... | collective-permute-start | bytes 3145736 | tf_op jit(solution)/shard_map/ppermute | solution.py:409
  665.1 52.6 %collective-permute-start.70 = (bf16[64,1536]{1,0:T(8,128)(2,1)S(1)}, bf16[64,1536]{1,0:T(8,128)(2,1)}, u32[]{:S(2)}, u32[]{:S(2)}) collective-permute-start(bf16[64,1536]{1,0:T(8,128)(2,1)S(1)} %copy-done.40), channel_id=1, source_target_pairs={{0,16},{8,24},{16,0},{24,8},{1,17},{9,25},{17,1},{25,9},{2,18},{10... | collective-permute-start | bytes 589832 | tf_op jit(solution)/shard_map/ppermute | solution.py:409
  734.3 21.8 %collective-permute-start.57 = (bf16[64,2048]{1,0:T(8,128)(2,1)S(1)}, bf16[64,2048]{1,0:T(8,128)(2,1)S(1)}, u32[]{:S(2)}, u32[]{:S(2)}) collective-permute-start(bf16[64,2048]{1,0:T(8,128)(2,1)S(1)} %get-tuple-element.160), channel_id=1, source_target_pairs={{0,6},{1,7},{2,4},{3,5},{4,2},{5,3},{6,0},{7,1},{8,14},{9,15},{10,... | collective-permute-start | bytes 786440 | tf_op jit(solution)/shard_map/ppermute | solution.py:414
  738.4 22.6 %collective-permute-start.56 = (bf16[64,2048]{1,0:T(8,128)(2,1)S(1)}, bf16[64,2048]{1,0:T(8,128)(2,1)S(1)}, u32[]{:S(2)}, u32[]{:S(2)}) collective-permute-start(bf16[64,2048]{1,0:T(8,128)(2,1)S(1)} %get-tuple-element.161), channel_id=1, source_target_pairs={{0,4},{1,5},{2,6},{3,7},{4,0},{5,1},{6,2},{7,3},{8,12},{9,13},{10,... | collective-permute-start | bytes 786440 | tf_op jit(solution)/shard_map/ppermute | solution.py:414
  738.4 22.6 %collective-permute-start.55 = (bf16[64,2048]{1,0:T(8,128)(2,1)S(1)}, bf16[64,2048]{1,0:T(8,128)(2,1)S(1)}, u32[]{:S(2)}, u32[]{:S(2)}) collective-permute-start(bf16[64,2048]{1,0:T(8,128)(2,1)S(1)} %get-tuple-element.162), channel_id=1, source_target_pairs={{0,2},{1,3},{2,0},{3,1},{4,6},{5,7},{6,4},{7,5},{8,10},{9,11},{10,... | collective-permute-start | bytes 786440 | tf_op jit(solution)/shard_map/ppermute | solution.py:414
  738.9 17.1 %collective-permute-start.74 = (bf16[64,1536]{1,0:T(8,128)(2,1)S(1)}, bf16[64,1536]{1,0:T(8,128)(2,1)S(1)}, u32[]{:S(2)}, u32[]{:S(2)}) collective-permute-start(bf16[64,1536]{1,0:T(8,128)(2,1)S(1)} %get-tuple-element.192), channel_id=1, source_target_pairs={{0,24},{8,16},{16,8},{24,0},{1,25},{9,17},{17,9},{25,1},{2,26},{10... | collective-permute-start | bytes 589832 | tf_op jit(solution)/shard_map/ppermute | solution.py:409
  740.3 9.7 %collective-permute-start.72 = (bf16[64,1536]{1,0:T(8,128)(2,1)S(1)}, bf16[64,1536]{1,0:T(8,128)(2,1)S(1)}, u32[]{:S(2)}, u32[]{:S(2)}) collective-permute-start(bf16[64,1536]{1,0:T(8,128)(2,1)S(1)} %get-tuple-element.194), channel_id=1, source_target_pairs={{0,8},{8,0},{16,24},{24,16},{1,9},{9,1},{17,25},{25,17},{2,10},{10... | collective-permute-start | bytes 589832 | tf_op jit(solution)/shard_map/ppermute | solution.py:409
  762.4 8.9 %collective-permute-start.60 = (bf16[64,1024]{1,0:T(8,128)(2,1)S(1)}, bf16[64,1024]{1,0:T(8,128)(2,1)S(1)}, u32[]{:S(2)}, u32[]{:S(2)}) collective-permute-start(bf16[64,1024]{1,0:T(8,128)(2,1)S(1)} %get-tuple-element.206), channel_id=1, source_target_pairs={{0,24},{8,16},{16,8},{24,0},{1,25},{9,17},{17,9},{25,1},{2,26},{10... | collective-permute-start | bytes 393224 | tf_op jit(solution)/shard_map/ppermute | solution.py:409
  771.5 10.2 %collective-permute-start.63 = (bf16[64,2048]{1,0:T(8,128)(2,1)S(1)}, bf16[64,2048]{1,0:T(8,128)(2,1)S(1)}, u32[]{:S(2)}, u32[]{:S(2)}) collective-permute-start(bf16[64,2048]{1,0:T(8,128)(2,1)S(1)} %get-tuple-element.156), channel_id=1, source_target_pairs={{0,24},{8,16},{16,8},{24,0},{1,25},{9,17},{17,9},{25,1},{2,26},{10... | collective-permute-start | bytes 786440 | tf_op jit(solution)/shard_map/ppermute | solution.py:409
  773.0 13.2 %collective-permute-start.62 = (bf16[64,2048]{1,0:T(8,128)(2,1)S(1)}, bf16[64,2048]{1,0:T(8,128)(2,1)S(1)}, u32[]{:S(2)}, u32[]{:S(2)}) collective-permute-start(bf16[64,2048]{1,0:T(8,128)(2,1)S(1)} %get-tuple-element.157), channel_id=1, source_target_pairs={{0,16},{8,24},{16,0},{24,8},{1,17},{9,25},{17,1},{25,9},{2,18},{10... | collective-permute-start | bytes 786440 | tf_op jit(solution)/shard_map/ppermute | solution.py:409
  773.6 12.6 %collective-permute-start.61 = (bf16[64,2048]{1,0:T(8,128)(2,1)S(1)}, bf16[64,2048]{1,0:T(8,128)(2,1)S(1)}, u32[]{:S(2)}, u32[]{:S(2)}) collective-permute-start(bf16[64,2048]{1,0:T(8,128)(2,1)S(1)} %get-tuple-element.158), channel_id=1, source_target_pairs={{0,8},{8,0},{16,24},{24,16},{1,9},{9,1},{17,25},{25,17},{2,10},{10... | collective-permute-start | bytes 786440 | tf_op jit(solution)/shard_map/ppermute | solution.py:409
  (69 other events, 1148.0 us)
Sparse Core Ops, SparseCore 0:
  70.6 45.9 all-gather.4
  118.2 27.9 all-gather.6
  155.4 130.0 all-gather.8
  287.1 63.2 all-gather.10
  382.7 67.8 reduce-scatter.5
  457.5 67.4 reduce-scatter.7
  527.3 85.0 reduce-scatter.9
  628.0 37.4 reduce-scatter.11
  667.7 48.3 reduce-scatter.13

commit v4 on v3

--- a/solution.py
+++ b/solution.py
@@ -615,10 +615,9 @@
     dn_one, grad_out_w, grad_up = together(dn_one, grad_out_w, grad_up)
     _, norm_one_pull = jax.vjp(rms_scale, x_own.astype(F32), attn_gain_full)
     dflat_norm, dattn_gain_part = norm_one_pull(dn_one)
-    grad_rows, dattn_gain_part = together((dh_rows + dflat_norm).astype(BF), dattn_gain_part)
-    spread = leave_plane(grad_rows.reshape(groups, piece, width))
+    spread = leave_plane((dh_rows + dflat_norm).astype(BF).reshape(groups, piece, width))
     grad_w_query, grad_w_key, grad_w_value = from_columns(grad_qkv, [q_width, kv_width, kv_width])
-    spread, grad_w_query = together(spread, grad_w_query)
+    spread, grad_w_query, dattn_gain_part = together(spread, grad_w_query, dattn_gain_part)
     grad_x = from_plane(spread, each)
 
     devices = groups * ring

time: 802 us -> 811 us (1.011)
  transfers between devices with their start and end apart: 84 -> 84, of which waited for: 43 -> 41; matrix products, arithmetic and copies ran while one was open for 28% -> 29% of each run, Pallas kernels for 7% -> 7%
where the time goes in v4:
time: 811 us; the launch traced here: 802 us
  waiting for transfers between devices  368 us (45%)
  matrix products  128 us (16%)
  starting transfers between devices  106 us (13%)
  other arithmetic  77.8 us (10%)
  Pallas kernels  58.9 us (7%)
  local copies, waits for them, and re-layouts  41.1 us (5%)
  between operations  22.3 us (3%)
    ppermute x51, waiting for transfers between devices, swap(): return lax.ppermute(block, 'fsdp', [(i, i ^ step) for i in range(groups)])  278 us
    ppermute x12, waiting for transfers between devices, swap_plane(): lax.ppermute(block, 'ctx', [(i, (i // lanes ^ step) * lanes + i % lanes)...  74.5 us
    ppermute x51, starting transfers between devices, swap(): return lax.ppermute(block, 'fsdp', [(i, i ^ step) for i in range(groups)])  60 us
    dot_general x4, matrix products, dot_nt(): lax.dot_general(left, right, (((1,), (1,)), ((), ())), preferred_element_...  49.3 us
    dot_general x5, matrix products, dot_tn(): lax.dot_general(left, right, (((0,), (0,)), ((), ())), preferred_element_...  42.1 us
    dot_general x3, matrix products, dot_nn(): lax.dot_general(left, right, (((1,), (0,)), ((), ())), preferred_element_...  36.5 us
    ppermute x12, starting transfers between devices, swap_plane(): lax.ppermute(block, 'ctx', [(i, (i // lanes ^ step) * lanes + i % lanes)...  30.1 us
    pallas_call x1, Pallas kernels, attention_backward(): pl.pallas_call(functools.partial(attn_bwd_kernel, **sizes), grid_spec=plt...  22.5 us
  transfers between devices with their start and end apart: 84, of which 41 were waited for; matrix products, arithmetic and copies ran while one was open for 29% of the time, Pallas kernels for 7%

profile of v4, /device:TPU:0, one launch (start us, length us, event | category | flops | bytes accessed | tf_op | source)
XLA Modules:
  0.0 802.4 jit_solution(5627977208402460257)
XLA Ops:
  13.4 3.0 collective-permute-start.7
  17.9 3.1 collective-permute-start.8
  33.1 5.0 collective-permute-done.2
  38.1 2.8 collective-permute-done.1
  45.1 3.7 collective-permute-start.5
  49.8 6.3 collective-permute-done.5
  56.1 12.6 %collective-permute-done.4 = bf16[64,2048]{1,0:T(8,128)(2,1)S(1)} collective-permute-done((bf16[64,2048]{1,0:T(8,128)(2,1)S(1)}, bf16[64,2048]{1,0:T(8,128)(2,1)S(1)}, u32[]{:S(2)}, u32[]{:S(2)}) %collective-permute-start.4) | collective-permute-done | bytes 262176 | tf_op jit(solution)/shard_map/ppermute | solution.py:414
  82.6 16.0 %collective-permute-done.16 = bf16[256,2048]{1,0:T(8,128)(2,1)S(1)} collective-permute-done((bf16[256,2048]{1,0:T(8,128)(2,1)S(1)}, bf16[256,2048]{1,0:T(8,128)(2,1)S(1)}, u32[]{:S(2)}, u32[]{:S(2)}) %collective-permute-start.16) | collective-permute-done | bytes 1048608 | tf_op jit(solution)/shard_map/ppermute | solution.py:409
  98.7 20.6 %collective-permute-done.15 = bf16[256,2048]{1,0:T(8,128)(2,1)S(1)} collective-permute-done((bf16[256,2048]{1,0:T(8,128)(2,1)S(1)}, bf16[256,2048]{1,0:T(8,128)(2,1)S(1)}, u32[]{:S(2)}, u32[]{:S(2)}) %collective-permute-start.15) | collective-permute-done | bytes 1048608 | tf_op jit(solution)/shard_map/ppermute | solution.py:409
  119.3 3.3 pad_maximum_fusion.1.x_ref
  122.6 11.4 %shard_map.255 = (bf16[1024,2048]{1,0:T(8,128)(2,1)}, f32[1024,768]{1,0:T(8,128)}, bf16[1024,512]{1,0:T(8,128)(2,1)}, bf16[1024,512]{1,0:T(8,128)(2,1)}) custom-call(bf16[1024,2048]{1,0:T(8,128)(2,1)} %pad_maximum_fusion.1.x_ref, f32[1,2048]{1,0:T(1,128)} %broadcast_in_dim_reshape.6.gain_ref, bf16[2048,1024]{1,0:T(8,128)(2,1)} %bitcast.306, ...), custom_call_target="tpu_custom_call" | custom-call | flops 4294967296 | bytes 16777216 | tf_op jit(solution)/shard_map/pallas_call | solution.py:293
  138.2 8.1 %collective-permute-done.24 = bf16[64,3072]{1,0:T(8,128)(2,1)S(1)} collective-permute-done((bf16[64,3072]{1,0:T(8,128)(2,1)S(1)}, bf16[64,3072]{1,0:T(8,128)(2,1)S(1)}, u32[]{:S(2)}, u32[]{:S(2)}) %collective-permute-start.24) | collective-permute-done | bytes 393248 | tf_op jit(solution)/shard_map/ppermute | solution.py:409
  146.4 7.7 collective-permute-done.25
  158.9 2.9 pad_maximum_fusion.4.kv_ref
  161.8 17.3 %shard_map.256 = (bf16[2,2,4,64,512]{4,3,2,1,0:T(8,128)(2,1)}, f32[8,2,1,256]{3,2,1,0:T(1,128)}) custom-call(s32[26]{0:T(128)} %pad_add_fusion.2.meta, bf16[2,2,4,64,512]{4,3,2,1,0:T(8,128)(2,1)} %bitcast.309, bf16[2,2,2,4,64,512]{5,4,3,2,1,0:T(8,128)(2,1)} %pad_maximum_fusion.4.kv_ref), custom_call_target="tpu_custom_call" | custom-call | flops 2147483648 | bytes 4194304 | tf_op jit(solution)/shard_map/pallas_call | solution.py:212
  179.1 7.6 fusion.53
  195.5 47.0 %collective-permute-done.29 = bf16[64,2048]{1,0:T(8,128)(2,1)S(1)} collective-permute-done((bf16[64,2048]{1,0:T(8,128)(2,1)S(1)}, bf16[64,2048]{1,0:T(8,128)(2,1)S(1)}, u32[]{:S(2)}, u32[]{:S(2)}) %collective-permute-start.29) | collective-permute-done | bytes 262176 | tf_op jit(solution)/shard_map/ppermute | solution.py:409
  253.6 4.1 multiply_reduce_fusion.2
  262.7 12.4 %collective-permute-done.32 = bf16[64,2048]{1,0:T(8,128)(2,1)S(1)} collective-permute-done((bf16[64,2048]{1,0:T(8,128)(2,1)S(1)}, bf16[64,2048]{1,0:T(8,128)(2,1)S(1)}, u32[]{:S(2)}, u32[]{:S(2)}) %collective-permute-start.32) | collective-permute-done | bytes 262176 | tf_op jit(solution)/shard_map/ppermute | solution.py:414
  275.1 10.7 %collective-permute-start.30 = (bf16[64,2048]{1,0:T(8,128)(2,1)S(1)}, bf16[64,2048]{1,0:T(8,128)(2,1)}, u32[]{:S(2)}, u32[]{:S(2)}) collective-permute-start(bf16[64,2048]{1,0:T(8,128)(2,1)S(1)} %get-tuple-element.177), channel_id=1, source_target_pairs={{0,2},{1,3},{2,0},{3,1},{4,6},{5,7},{6,4},{7,5},{8,10},{9,11},{10,... | collective-permute-start | bytes 786440 | tf_op jit(solution)/shard_map/ppermute | solution.py:414
  286.5 4.4 collective-permute-done.31
  290.9 6.1 collective-permute-done.30
  298.4 7.7 collective-permute-done.22
  306.1 17.1 %fusion.35 = f32[1024,3072]{1,0:T(8,128)S(1)} fusion(bf16[2048,3072]{1,0:T(8,128)(2,1)} %bitcast.304, bf16[256,2048]{1,0:T(8,128)(2,1)} %collective-permute-done.23, bf16[256,2048]{1,0:T(8,128)(2,1)} %collective-permute-done.22, bf16[256,2048]{1,0:T(8,128)(2,1)} %collective-permute-done.21, bf16[256,2048]{1,0:T(8,128)(2,1)} %multiply_convert_fusion.2), kind=kOutput, calls=%fused_computation.247 | convolution fusion | flops 12901679104 | bytes 29360128 | tf_op jit(solution)/shard_map/dot_general | solution.py:36
  328.8 41.9 %collective-permute-done.33 = bf16[256,2048]{1,0:T(8,128)(2,1)S(1)} collective-permute-done((bf16[256,2048]{1,0:T(8,128)(2,1)S(1)}, bf16[256,2048]{1,0:T(8,128)(2,1)S(1)}, u32[]{:S(2)}, u32[]{:S(2)}) %collective-permute-start.33) | collective-permute-done | bytes 1048608 | tf_op jit(solution)/shard_map/ppermute | solution.py:409
  374.0 9.2 %convolution_convert_fusion.2 = bf16[1536,2048]{1,0:T(8,128)(2,1)} fusion(bf16[1024,1536]{1,0:T(8,128)(2,1)S(1)} %multiply_convert_fusion.1, bf16[1024,2048]{1,0:T(8,128)(2,1)S(1)} %constant_dynamic-update-slice_fusion), kind=kOutput, calls=%fused_computation.3 | convolution fusion | flops 6445596672 | bytes 13631488 | tf_op jit(solution)/shard_map/dot_general | solution.py:44
  383.3 3.8 pad_maximum_fusion.2
  387.1 11.8 %fusion.54 = (bf16[1024,2048]{1,0:T(8,128)(2,1)S(1)}, f32[1024,2048]{1,0:T(8,128)}) fusion(bf16[1024,1536]{1,0:T(8,128)(2,1)} %copy-done.11, bf16[1536,2048]{1,0:T(8,128)(2,1)} %all-gather.11.cloned.1.call-done), kind=kOutput, calls=%fused_computation.265 | convolution fusion | flops 6444548096 | bytes 22020096 | tf_op jit(solution)/shard_map/dot_general | solution.py:36
  404.0 14.8 %multiply_convert_fusion = (bf16[1024,1536]{1,0:T(8,128)(2,1)S(1)}, bf16[1024,1536]{1,0:T(8,128)(2,1)}) fusion(f32[1024,3072]{1,0:T(8,128)} %copy-done.6, bf16[1024,2048]{1,0:T(8,128)(2,1)S(1)} %copy-done.29, bf16[1536,2048]{1,0:T(8,128)(2,1)} %all-gather.11.cloned.1.call-done), kind=kOutput, calls=%fused_computation.8 | convolution fusion | flops 6464471040 | bytes 29360128 | tf_op jit(solution)/shard_map/dot_general | solution.py:40
  418.8 7.7 collective-permute-done.36
  427.5 2.8 pad_maximum_fusion
  430.4 17.3 %fusion.55 = f32[4,256,2048]{2,1,0:T(8,128)} fusion(bf16[4,256,3072]{2,1,0:T(8,128)(2,1)S(1)} %bitcast.273, bf16[2048,3072,1]{1,0,2:T(8,128)(2,1)} %bitcast.305), kind=kOutput, calls=%fused_computation.266 | convolution fusion | flops 12884901888 | bytes 27262976 | tf_op jit(solution)/shard_map/dot_general | solution.py:40
  449.2 8.9 %convolution_convert_fusion.1 = bf16[2048,1536]{1,0:T(8,128)(2,1)} fusion(bf16[1024,2048]{1,0:T(8,128)(2,1)S(1)} %copy-done.8, bf16[1024,1536]{1,0:T(8,128)(2,1)S(1)} %copy-done.10), kind=kOutput, calls=%fused_computation.2 | convolution fusion | flops 6445596672 | bytes 13631488 | tf_op jit(solution)/shard_map/dot_general | solution.py:44
  458.2 11.5 %convolution_convert_fusion = bf16[2048,1536]{1,0:T(8,128)(2,1)} fusion(bf16[1024,2048]{1,0:T(8,128)(2,1)} %pad_maximum_fusion.2, bf16[1024,1536]{1,0:T(8,128)(2,1)} %copy-done.9), kind=kOutput, calls=%fused_computation.1 | convolution fusion | flops 6445596672 | bytes 13631488 | tf_op jit(solution)/shard_map/dot_general | solution.py:44
  469.8 4.1 convert.25
  477.9 22.5 %collective-permute-done.39 = bf16[256,2048]{1,0:T(8,128)(2,1)S(1)} collective-permute-done((bf16[256,2048]{1,0:T(8,128)(2,1)S(1)}, bf16[256,2048]{1,0:T(8,128)(2,1)S(1)}, u32[]{:S(2)}, u32[]{:S(2)}) %collective-permute-start.39) | collective-permute-done | bytes 1048608 | tf_op jit(solution)/shard_map/ppermute | solution.py:409
  500.5 20.8 %collective-permute-done.41 = bf16[256,2048]{1,0:T(8,128)(2,1)S(1)} collective-permute-done((bf16[256,2048]{1,0:T(8,128)(2,1)S(1)}, bf16[256,2048]{1,0:T(8,128)(2,1)S(1)}, u32[]{:S(2)}, u32[]{:S(2)}) %collective-permute-start.41) | collective-permute-done | bytes 1048608 | tf_op jit(solution)/shard_map/ppermute | solution.py:409
  522.6 3.6 fusion.21
  528.7 4.6 fusion.17
  537.1 16.5 %collective-permute-done.47 = bf16[64,2048]{1,0:T(8,128)(2,1)S(1)} collective-permute-done((bf16[64,2048]{1,0:T(8,128)(2,1)S(1)}, bf16[64,2048]{1,0:T(8,128)(2,1)S(1)}, u32[]{:S(2)}, u32[]{:S(2)}) %collective-permute-start.47) | collective-permute-done | bytes 262176 | tf_op jit(solution)/shard_map/ppermute | solution.py:414
  553.6 10.1 %collective-permute-start.45 = (bf16[64,2048]{1,0:T(8,128)(2,1)S(1)}, bf16[64,2048]{1,0:T(8,128)(2,1)}, u32[]{:S(2)}, u32[]{:S(2)}) collective-permute-start(bf16[64,2048]{1,0:T(8,128)(2,1)S(1)} %get-tuple-element.173), channel_id=1, source_target_pairs={{0,2},{1,3},{2,0},{3,1},{4,6},{5,7},{6,4},{7,5},{8,10},{9,11},{10,... | collective-permute-start | bytes 786440 | tf_op jit(solution)/shard_map/ppermute | solution.py:414
  566.9 5.1 collective-permute-done.46
  572.0 5.3 collective-permute-done.45
  578.6 4.0 pad_maximum_fusion.3
  586.9 6.2 convolution_convert_fusion.5
  593.1 22.5 %shard_map.257 = (f32[2,2,4,64,512]{4,3,2,1,0:T(8,128)}, bf16[2,2,2,4,64,512]{5,4,3,2,1,0:T(8,128)(2,1)}) custom-call(s32[26]{0:T(128)} %pad_add_fusion.2.meta, bf16[2,2,4,64,512]{4,3,2,1,0:T(8,128)(2,1)} %bitcast.310, bf16[2,2,2,4,64,512]{5,4,3,2,1,0:T(8,128)(2,1)} %pad_maximum_fusion.4.kv_ref, bf16[2,2,4,64,512]{4,3,2,1,0:T(8,128)(2,1)} %bitcast.311, ...), custom_call_target="tpu_custom_call" | custom-call | flops 5368709120 | bytes 10485760 | tf_op jit(solution)/shard_map/pallas_call | solution.py:238
  615.6 5.9 convolution_convert_fusion.4
  621.6 3.1 fusion.40
  630.9 7.8 shard_map.258
  638.7 11.0 %fusion.56 = f32[4,256,2048]{2,1,0:T(8,128)} fusion(bf16[4,256,1024]{2,1,0:T(8,128)(2,1)} %bitcast.308, bf16[2048,1024,1]{1,0,2:T(8,128)(2,1)} %bitcast.307), kind=kOutput, calls=%fused_computation.267 | convolution fusion | flops 4294967296 | bytes 14680064 | tf_op jit(solution)/shard_map/dot_general | solution.py:40
  649.7 6.5 convolution_convert_fusion.3
  665.1 5.6 collective-permute-done.69
  671.5 4.0 convert.26
  682.6 21.1 %collective-permute-done.52 = bf16[256,2048]{1,0:T(8,128)(2,1)} collective-permute-done((bf16[256,2048]{1,0:T(8,128)(2,1)}, bf16[256,2048]{1,0:T(8,128)(2,1)}, u32[]{:S(2)}, u32[]{:S(2)}) %collective-permute-start.52) | collective-permute-done | bytes 1048608 | tf_op jit(solution)/shard_map/ppermute | solution.py:409
  703.6 21.7 %collective-permute-done.54 = bf16[256,2048]{1,0:T(8,128)(2,1)} collective-permute-done((bf16[256,2048]{1,0:T(8,128)(2,1)}, bf16[256,2048]{1,0:T(8,128)(2,1)}, u32[]{:S(2)}, u32[]{:S(2)}) %collective-permute-start.54) | collective-permute-done | bytes 1048608 | tf_op jit(solution)/shard_map/ppermute | solution.py:409
  726.7 4.6 fusion.19
  735.5 2.9 fusion.6
  738.6 3.7 collective-permute-start.56
  745.2 5.6 collective-permute-done.72
  752.3 4.2 collective-permute-done.73
  756.6 5.8 collective-permute-done.56
  768.8 3.1 collective-permute-done.58
  783.4 3.8 collective-permute-done.66
  788.0 2.9 collective-permute-done.67
  (409 shorter events, 161.0 us)
Async XLA Ops:
  7.2 115.4 %all-gather.5.cloned.1.call-start = ((), (), s32[]{:S(2)}) async-start(), calls=%async_computation.5 | async-start | bytes 4718592 | tf_op jit(solution)/shard_map/all_gather | solution.py:532
  29.6 8.6 %collective-permute-start.2 = (bf16[64,2048]{1,0:T(8,128)(2,1)S(1)}, bf16[64,2048]{1,0:T(8,128)(2,1)S(1)}, u32[]{:S(2)}, u32[]{:S(2)}) collective-permute-start(bf16[64,2048]{1,0:T(8,128)(2,1)S(1)} %get-tuple-element.187), channel_id=1, source_target_pairs={{0,24},{8,16},{16,8},{24,0},{1,25},{9,17},{17,9},{25,1},{2,26},{10... | collective-permute-start | bytes 786440 | tf_op jit(solution)/shard_map/ppermute | solution.py:409
  31.1 9.9 %collective-permute-start.1 = (bf16[64,2048]{1,0:T(8,128)(2,1)S(1)}, bf16[64,2048]{1,0:T(8,128)(2,1)S(1)}, u32[]{:S(2)}, u32[]{:S(2)}) collective-permute-start(bf16[64,2048]{1,0:T(8,128)(2,1)S(1)} %get-tuple-element.188), channel_id=1, source_target_pairs={{0,16},{8,24},{16,0},{24,8},{1,17},{9,25},{17,1},{25,9},{2,18},{10... | collective-permute-start | bytes 786440 | tf_op jit(solution)/shard_map/ppermute | solution.py:409
  45.1 11.0 %collective-permute-start.5 = (bf16[64,2048]{1,0:T(8,128)(2,1)S(1)}, bf16[64,2048]{1,0:T(8,128)(2,1)S(1)}, u32[]{:S(2)}, u32[]{:S(2)}) collective-permute-start(bf16[64,2048]{1,0:T(8,128)(2,1)S(1)} %get-tuple-element.183), channel_id=1, source_target_pairs={{0,6},{1,7},{2,4},{3,5},{4,2},{5,3},{6,0},{7,1},{8,14},{9,15},{10,... | collective-permute-start | bytes 786440 | tf_op jit(solution)/shard_map/ppermute | solution.py:414
  48.7 19.9 %collective-permute-start.4 = (bf16[64,2048]{1,0:T(8,128)(2,1)S(1)}, bf16[64,2048]{1,0:T(8,128)(2,1)S(1)}, u32[]{:S(2)}, u32[]{:S(2)}) collective-permute-start(bf16[64,2048]{1,0:T(8,128)(2,1)S(1)} %get-tuple-element.184), channel_id=1, source_target_pairs={{0,4},{1,5},{2,6},{3,7},{4,0},{5,1},{6,2},{7,3},{8,12},{9,13},{10,... | collective-permute-start | bytes 786440 | tf_op jit(solution)/shard_map/ppermute | solution.py:414
  48.8 19.8 %collective-permute-start.3 = (bf16[64,2048]{1,0:T(8,128)(2,1)S(1)}, bf16[64,2048]{1,0:T(8,128)(2,1)S(1)}, u32[]{:S(2)}, u32[]{:S(2)}) collective-permute-start(bf16[64,2048]{1,0:T(8,128)(2,1)S(1)} %get-tuple-element.185), channel_id=1, source_target_pairs={{0,2},{1,3},{2,0},{3,1},{4,6},{5,7},{6,4},{7,5},{8,10},{9,11},{10,... | collective-permute-start | bytes 786440 | tf_op jit(solution)/shard_map/ppermute | solution.py:414
  70.5 108.7 %all-gather.7.cloned.1.call-start = ((), (), s32[]{:S(2)}) async-start(), calls=%async_computation.6 | async-start | bytes 2359296 | tf_op jit(solution)/shard_map/all_gather | solution.py:533
  71.2 234.9 %all-gather.9.cloned.1.call-start = ((), (), s32[]{:S(2)}) async-start(), calls=%async_computation.7 | async-start | bytes 14155776 | tf_op jit(solution)/shard_map/all_gather | solution.py:541
  71.6 27.0 %collective-permute-start.16 = (bf16[256,2048]{1,0:T(8,128)(2,1)S(1)}, bf16[256,2048]{1,0:T(8,128)(2,1)S(1)}, u32[]{:S(2)}, u32[]{:S(2)}) collective-permute-start(bf16[256,2048]{1,0:T(8,128)(2,1)S(1)} %pad_maximum_fusion.6), channel_id=1, source_target_pairs={{0,24},{8,16},{16,8},{24,0},{1,25},{9,17},{17,9},{25,1},{2,26},{10... | collective-permute-start | bytes 3145736 | tf_op jit(solution)/shard_map/ppermute | solution.py:409
  73.1 46.2 %collective-permute-start.15 = (bf16[256,2048]{1,0:T(8,128)(2,1)S(1)}, bf16[256,2048]{1,0:T(8,128)(2,1)S(1)}, u32[]{:S(2)}, u32[]{:S(2)}) collective-permute-start(bf16[256,2048]{1,0:T(8,128)(2,1)S(1)} %pad_maximum_fusion.6), channel_id=1, source_target_pairs={{0,16},{8,24},{16,0},{24,8},{1,17},{9,25},{17,1},{25,9},{2,18},{10... | collective-permute-start | bytes 3145736 | tf_op jit(solution)/shard_map/ppermute | solution.py:409
  73.9 45.4 %collective-permute-start.14 = (bf16[256,2048]{1,0:T(8,128)(2,1)S(1)}, bf16[256,2048]{1,0:T(8,128)(2,1)}, u32[]{:S(2)}, u32[]{:S(2)}) collective-permute-start(bf16[256,2048]{1,0:T(8,128)(2,1)S(1)} %pad_maximum_fusion.6), channel_id=1, source_target_pairs={{0,8},{8,0},{16,24},{24,16},{1,9},{9,1},{17,25},{25,17},{2,10},{10... | collective-permute-start | bytes 3145736 | tf_op jit(solution)/shard_map/ppermute | solution.py:409
  134.3 12.1 %collective-permute-start.24 = (bf16[64,3072]{1,0:T(8,128)(2,1)S(1)}, bf16[64,3072]{1,0:T(8,128)(2,1)S(1)}, u32[]{:S(2)}, u32[]{:S(2)}) collective-permute-start(bf16[64,3072]{1,0:T(8,128)(2,1)S(1)} %pad_maximum_fusion.18), channel_id=1, source_target_pairs={{0,8},{8,0},{16,24},{24,16},{1,9},{9,1},{17,25},{25,17},{2,10},{10... | collective-permute-start | bytes 1179656 | tf_op jit(solution)/shard_map/ppermute | solution.py:409
  134.8 19.2 %collective-permute-start.25 = (bf16[64,3072]{1,0:T(8,128)(2,1)S(1)}, bf16[64,3072]{1,0:T(8,128)(2,1)S(1)}, u32[]{:S(2)}, u32[]{:S(2)}) collective-permute-start(bf16[64,3072]{1,0:T(8,128)(2,1)S(1)} %pad_maximum_fusion.19), channel_id=1, source_target_pairs={{0,16},{8,24},{16,0},{24,8},{1,17},{9,25},{17,1},{25,9},{2,18},{10... | collective-permute-start | bytes 1179656 | tf_op jit(solution)/shard_map/ppermute | solution.py:409
  136.2 17.9 %collective-permute-start.26 = (bf16[64,3072]{1,0:T(8,128)(2,1)S(1)}, bf16[64,3072]{1,0:T(8,128)(2,1)S(1)}, u32[]{:S(2)}, u32[]{:S(2)}) collective-permute-start(bf16[64,3072]{1,0:T(8,128)(2,1)S(1)} %pad_maximum_fusion.20), channel_id=1, source_target_pairs={{0,24},{8,16},{16,8},{24,0},{1,25},{9,17},{17,9},{25,1},{2,26},{10... | collective-permute-start | bytes 1179656 | tf_op jit(solution)/shard_map/ppermute | solution.py:409
  155.3 231.8 %all-gather.11.cloned.1.call-start = ((), (), s32[]{:S(2)}) async-start(), calls=%async_computation.8 | async-start | bytes 7077888 | tf_op jit(solution)/shard_map/all_gather | solution.py:542
  155.9 370.3 %reduce-scatter.6.cloned.1.call-start = ((), (), s32[]{:S(2)}) async-start(), calls=%async_computation.9 | async-start | bytes 7077888 | tf_op jit(solution)/shard_map/reduce_scatter | solution.py:563
  188.4 63.8 %collective-permute-start.18 = (bf16[256,2048]{1,0:T(8,128)(2,1)}, bf16[256,2048]{1,0:T(8,128)(2,1)S(1)}, u32[]{:S(2)}, u32[]{:S(2)}) collective-permute-start(bf16[256,2048]{1,0:T(8,128)(2,1)} %get-tuple-element.142), channel_id=1, source_target_pairs={{0,8},{8,0},{16,24},{24,16},{1,9},{9,1},{17,25},{25,17},{2,10},{10... | collective-permute-start | bytes 3145736 | tf_op jit(solution)/shard_map/ppermute | solution.py:409
  189.7 62.6 %collective-permute-start.20 = (bf16[256,2048]{1,0:T(8,128)(2,1)}, bf16[256,2048]{1,0:T(8,128)(2,1)S(1)}, u32[]{:S(2)}, u32[]{:S(2)}) collective-permute-start(bf16[256,2048]{1,0:T(8,128)(2,1)} %get-tuple-element.143), channel_id=1, source_target_pairs={{0,24},{8,16},{16,8},{24,0},{1,25},{9,17},{17,9},{25,1},{2,26},{10... | collective-permute-start | bytes 3145736 | tf_op jit(solution)/shard_map/ppermute | solution.py:409
  191.0 61.3 %collective-permute-start.19 = (bf16[256,2048]{1,0:T(8,128)(2,1)}, bf16[256,2048]{1,0:T(8,128)(2,1)}, u32[]{:S(2)}, u32[]{:S(2)}) collective-permute-start(bf16[256,2048]{1,0:T(8,128)(2,1)} %get-tuple-element.144), channel_id=1, source_target_pairs={{0,16},{8,24},{16,0},{24,8},{1,17},{9,25},{17,1},{25,9},{2,18},{10... | collective-permute-start | bytes 3145736 | tf_op jit(solution)/shard_map/ppermute | solution.py:409
  192.8 49.7 %collective-permute-start.29 = (bf16[64,2048]{1,0:T(8,128)(2,1)S(1)}, bf16[64,2048]{1,0:T(8,128)(2,1)S(1)}, u32[]{:S(2)}, u32[]{:S(2)}) collective-permute-start(bf16[64,2048]{1,0:T(8,128)(2,1)S(1)} %get-tuple-element.179), channel_id=1, source_target_pairs={{0,24},{8,16},{16,8},{24,0},{1,25},{9,17},{17,9},{25,1},{2,26},{10... | collective-permute-start | bytes 786440 | tf_op jit(solution)/shard_map/ppermute | solution.py:409
  193.9 55.7 %collective-permute-start.28 = (bf16[64,2048]{1,0:T(8,128)(2,1)}, bf16[64,2048]{1,0:T(8,128)(2,1)}, u32[]{:S(2)}, u32[]{:S(2)}) collective-permute-start(bf16[64,2048]{1,0:T(8,128)(2,1)} %get-tuple-element.180), channel_id=1, source_target_pairs={{0,16},{8,24},{16,0},{24,8},{1,17},{9,25},{17,1},{25,9},{2,18},{10... | collective-permute-start | bytes 786440 | tf_op jit(solution)/shard_map/ppermute | solution.py:409
  258.9 39.5 %collective-permute-start.23 = (bf16[256,2048]{1,0:T(8,128)(2,1)}, bf16[256,2048]{1,0:T(8,128)(2,1)}, u32[]{:S(2)}, u32[]{:S(2)}) collective-permute-start(bf16[256,2048]{1,0:T(8,128)(2,1)} %multiply_convert_fusion.2), channel_id=1, source_target_pairs={{0,24},{8,16},{16,8},{24,0},{1,25},{9,17},{17,9},{25,1},{2,26},{10... | collective-permute-start | bytes 3145736 | tf_op jit(solution)/shard_map/ppermute | solution.py:409
  260.4 45.6 %collective-permute-start.22 = (bf16[256,2048]{1,0:T(8,128)(2,1)}, bf16[256,2048]{1,0:T(8,128)(2,1)}, u32[]{:S(2)}, u32[]{:S(2)}) collective-permute-start(bf16[256,2048]{1,0:T(8,128)(2,1)} %multiply_convert_fusion.2), channel_id=1, source_target_pairs={{0,16},{8,24},{16,0},{24,8},{1,17},{9,25},{17,1},{25,9},{2,18},{10... | collective-permute-start | bytes 3145736 | tf_op jit(solution)/shard_map/ppermute | solution.py:409
  260.9 45.2 %collective-permute-start.21 = (bf16[256,2048]{1,0:T(8,128)(2,1)}, bf16[256,2048]{1,0:T(8,128)(2,1)}, u32[]{:S(2)}, u32[]{:S(2)}) collective-permute-start(bf16[256,2048]{1,0:T(8,128)(2,1)} %multiply_convert_fusion.2), channel_id=1, source_target_pairs={{0,8},{8,0},{16,24},{24,16},{1,9},{9,1},{17,25},{25,17},{2,10},{10... | collective-permute-start | bytes 3145736 | tf_op jit(solution)/shard_map/ppermute | solution.py:409
  262.5 12.6 %collective-permute-start.32 = (bf16[64,2048]{1,0:T(8,128)(2,1)S(1)}, bf16[64,2048]{1,0:T(8,128)(2,1)S(1)}, u32[]{:S(2)}, u32[]{:S(2)}) collective-permute-start(bf16[64,2048]{1,0:T(8,128)(2,1)S(1)} %get-tuple-element.175), channel_id=1, source_target_pairs={{0,6},{1,7},{2,4},{3,5},{4,2},{5,3},{6,0},{7,1},{8,14},{9,15},{10,... | collective-permute-start | bytes 786440 | tf_op jit(solution)/shard_map/ppermute | solution.py:414
  262.7 28.3 %collective-permute-start.31 = (bf16[64,2048]{1,0:T(8,128)(2,1)S(1)}, bf16[64,2048]{1,0:T(8,128)(2,1)S(1)}, u32[]{:S(2)}, u32[]{:S(2)}) collective-permute-start(bf16[64,2048]{1,0:T(8,128)(2,1)S(1)} %get-tuple-element.176), channel_id=1, source_target_pairs={{0,4},{1,5},{2,6},{3,7},{4,0},{5,1},{6,2},{7,3},{8,12},{9,13},{10,... | collective-permute-start | bytes 786440 | tf_op jit(solution)/shard_map/ppermute | solution.py:414
  275.1 21.9 %collective-permute-start.30 = (bf16[64,2048]{1,0:T(8,128)(2,1)S(1)}, bf16[64,2048]{1,0:T(8,128)(2,1)}, u32[]{:S(2)}, u32[]{:S(2)}) collective-permute-start(bf16[64,2048]{1,0:T(8,128)(2,1)S(1)} %get-tuple-element.177), channel_id=1, source_target_pairs={{0,2},{1,3},{2,0},{3,1},{4,6},{5,7},{6,4},{7,5},{8,10},{9,11},{10,... | collective-permute-start | bytes 786440 | tf_op jit(solution)/shard_map/ppermute | solution.py:414
  323.2 48.6 %collective-permute-start.35 = (bf16[256,2048]{1,0:T(8,128)(2,1)S(1)}, bf16[256,2048]{1,0:T(8,128)(2,1)S(1)}, u32[]{:S(2)}, u32[]{:S(2)}) collective-permute-start(bf16[256,2048]{1,0:T(8,128)(2,1)S(1)} %maximum_select_fusion), channel_id=1, source_target_pairs={{0,24},{8,16},{16,8},{24,0},{1,25},{9,17},{17,9},{25,1},{2,26},{10... | collective-permute-start | bytes 3145736 | tf_op jit(solution)/shard_map/ppermute | solution.py:409
  324.8 46.9 %collective-permute-start.34 = (bf16[256,2048]{1,0:T(8,128)(2,1)S(1)}, bf16[256,2048]{1,0:T(8,128)(2,1)S(1)}, u32[]{:S(2)}, u32[]{:S(2)}) collective-permute-start(bf16[256,2048]{1,0:T(8,128)(2,1)S(1)} %maximum_select_fusion), channel_id=1, source_target_pairs={{0,16},{8,24},{16,0},{24,8},{1,17},{9,25},{17,1},{25,9},{2,18},{10... | collective-permute-start | bytes 3145736 | tf_op jit(solution)/shard_map/ppermute | solution.py:409
  325.4 45.3 %collective-permute-start.33 = (bf16[256,2048]{1,0:T(8,128)(2,1)S(1)}, bf16[256,2048]{1,0:T(8,128)(2,1)S(1)}, u32[]{:S(2)}, u32[]{:S(2)}) collective-permute-start(bf16[256,2048]{1,0:T(8,128)(2,1)S(1)} %maximum_select_fusion), channel_id=1, source_target_pairs={{0,8},{8,0},{16,24},{24,16},{1,9},{9,1},{17,25},{25,17},{2,10},{10... | collective-permute-start | bytes 3145736 | tf_op jit(solution)/shard_map/ppermute | solution.py:409
  383.3 199.2 %reduce-scatter.8.cloned.1.call-start = ((), (), s32[]{:S(2)}) async-start(), calls=%async_computation.10 | async-start | bytes 7077888 | tf_op jit(solution)/shard_map/reduce_scatter | solution.py:581
  400.5 26.0 %collective-permute-start.36 = (bf16[256,2048]{1,0:T(8,128)(2,1)S(1)}, bf16[256,2048]{1,0:T(8,128)(2,1)S(1)}, u32[]{:S(2)}, u32[]{:S(2)}) collective-permute-start(bf16[256,2048]{1,0:T(8,128)(2,1)S(1)} %get-tuple-element.86), channel_id=1, source_target_pairs={{0,8},{8,0},{16,24},{24,16},{1,9},{9,1},{17,25},{25,17},{2,10},{10... | collective-permute-start | bytes 3145736 | tf_op jit(solution)/shard_map/ppermute | solution.py:409
  401.6 47.6 %collective-permute-start.37 = (bf16[256,2048]{1,0:T(8,128)(2,1)}, bf16[256,2048]{1,0:T(8,128)(2,1)}, u32[]{:S(2)}, u32[]{:S(2)}) collective-permute-start(bf16[256,2048]{1,0:T(8,128)(2,1)} %get-tuple-element.90), channel_id=1, source_target_pairs={{0,16},{8,24},{16,0},{24,8},{1,17},{9,25},{17,1},{25,9},{2,18},{10... | collective-permute-start | bytes 3145736 | tf_op jit(solution)/shard_map/ppermute | solution.py:409
  403.1 46.1 %collective-permute-start.38 = (bf16[256,2048]{1,0:T(8,128)(2,1)}, bf16[256,2048]{1,0:T(8,128)(2,1)}, u32[]{:S(2)}, u32[]{:S(2)}) collective-permute-start(bf16[256,2048]{1,0:T(8,128)(2,1)} %get-tuple-element.91), channel_id=1, source_target_pairs={{0,24},{8,16},{16,8},{24,0},{1,25},{9,17},{17,9},{25,1},{2,26},{10... | collective-permute-start | bytes 3145736 | tf_op jit(solution)/shard_map/ppermute | solution.py:409
  458.2 180.5 %reduce-scatter.10.cloned.1.call-start = ((), (), s32[]{:S(2)}) async-start(), calls=%async_computation.11 | async-start | bytes 7077888 | tf_op jit(solution)/shard_map/reduce_scatter | solution.py:584
  469.8 261.5 %reduce-scatter.12.cloned.1.call-start = ((), (), s32[]{:S(2)}) async-start(), calls=%async_computation.12 | async-start | bytes 2359296 | tf_op jit(solution)/shard_map/reduce_scatter | solution.py:596
  474.4 26.1 %collective-permute-start.39 = (bf16[256,2048]{1,0:T(8,128)(2,1)S(1)}, bf16[256,2048]{1,0:T(8,128)(2,1)S(1)}, u32[]{:S(2)}, u32[]{:S(2)}) collective-permute-start(bf16[256,2048]{1,0:T(8,128)(2,1)S(1)} %get-tuple-element.136), channel_id=1, source_target_pairs={{0,8},{8,0},{16,24},{24,16},{1,9},{9,1},{17,25},{25,17},{2,10},{10... | collective-permute-start | bytes 3145736 | tf_op jit(solution)/shard_map/ppermute | solution.py:409
  475.4 45.8 %collective-permute-start.41 = (bf16[256,2048]{1,0:T(8,128)(2,1)S(1)}, bf16[256,2048]{1,0:T(8,128)(2,1)S(1)}, u32[]{:S(2)}, u32[]{:S(2)}) collective-permute-start(bf16[256,2048]{1,0:T(8,128)(2,1)S(1)} %get-tuple-element.137), channel_id=1, source_target_pairs={{0,24},{8,16},{16,8},{24,0},{1,25},{9,17},{17,9},{25,1},{2,26},{10... | collective-permute-start | bytes 3145736 | tf_op jit(solution)/shard_map/ppermute | solution.py:409
  477.4 45.1 %collective-permute-start.40 = (bf16[256,2048]{1,0:T(8,128)(2,1)S(1)}, bf16[256,2048]{1,0:T(8,128)(2,1)S(1)}, u32[]{:S(2)}, u32[]{:S(2)}) collective-permute-start(bf16[256,2048]{1,0:T(8,128)(2,1)S(1)} %get-tuple-element.138), channel_id=1, source_target_pairs={{0,16},{8,24},{16,0},{24,8},{1,17},{9,25},{17,1},{25,9},{2,18},{10... | collective-permute-start | bytes 3145736 | tf_op jit(solution)/shard_map/ppermute | solution.py:409
  533.4 45.2 %collective-permute-start.44 = (bf16[256,2048]{1,0:T(8,128)(2,1)}, bf16[256,2048]{1,0:T(8,128)(2,1)}, u32[]{:S(2)}, u32[]{:S(2)}) collective-permute-start(bf16[256,2048]{1,0:T(8,128)(2,1)} %get-tuple-element.148), channel_id=1, source_target_pairs={{0,24},{8,16},{16,8},{24,0},{1,25},{9,17},{17,9},{25,1},{2,26},{10... | collective-permute-start | bytes 3145736 | tf_op jit(solution)/shard_map/ppermute | solution.py:409
  535.3 43.2 %collective-permute-start.43 = (bf16[256,2048]{1,0:T(8,128)(2,1)}, bf16[256,2048]{1,0:T(8,128)(2,1)}, u32[]{:S(2)}, u32[]{:S(2)}) collective-permute-start(bf16[256,2048]{1,0:T(8,128)(2,1)} %get-tuple-element.148), channel_id=1, source_target_pairs={{0,16},{8,24},{16,0},{24,8},{1,17},{9,25},{17,1},{25,9},{2,18},{10... | collective-permute-start | bytes 3145736 | tf_op jit(solution)/shard_map/ppermute | solution.py:409
  535.8 42.8 %collective-permute-start.42 = (bf16[256,2048]{1,0:T(8,128)(2,1)}, bf16[256,2048]{1,0:T(8,128)(2,1)}, u32[]{:S(2)}, u32[]{:S(2)}) collective-permute-start(bf16[256,2048]{1,0:T(8,128)(2,1)} %get-tuple-element.148), channel_id=1, source_target_pairs={{0,8},{8,0},{16,24},{24,16},{1,9},{9,1},{17,25},{25,17},{2,10},{10... | collective-permute-start | bytes 3145736 | tf_op jit(solution)/shard_map/ppermute | solution.py:409
  536.9 16.7 %collective-permute-start.47 = (bf16[64,2048]{1,0:T(8,128)(2,1)S(1)}, bf16[64,2048]{1,0:T(8,128)(2,1)S(1)}, u32[]{:S(2)}, u32[]{:S(2)}) collective-permute-start(bf16[64,2048]{1,0:T(8,128)(2,1)S(1)} %get-tuple-element.171), channel_id=1, source_target_pairs={{0,6},{1,7},{2,4},{3,5},{4,2},{5,3},{6,0},{7,1},{8,14},{9,15},{10,... | collective-permute-start | bytes 786440 | tf_op jit(solution)/shard_map/ppermute | solution.py:414
  537.0 35.0 %collective-permute-start.46 = (bf16[64,2048]{1,0:T(8,128)(2,1)S(1)}, bf16[64,2048]{1,0:T(8,128)(2,1)S(1)}, u32[]{:S(2)}, u32[]{:S(2)}) collective-permute-start(bf16[64,2048]{1,0:T(8,128)(2,1)S(1)} %get-tuple-element.172), channel_id=1, source_target_pairs={{0,4},{1,5},{2,6},{3,7},{4,0},{5,1},{6,2},{7,3},{8,12},{9,13},{10,... | collective-permute-start | bytes 786440 | tf_op jit(solution)/shard_map/ppermute | solution.py:414
  553.6 23.7 %collective-permute-start.45 = (bf16[64,2048]{1,0:T(8,128)(2,1)S(1)}, bf16[64,2048]{1,0:T(8,128)(2,1)}, u32[]{:S(2)}, u32[]{:S(2)}) collective-permute-start(bf16[64,2048]{1,0:T(8,128)(2,1)S(1)} %get-tuple-element.173), channel_id=1, source_target_pairs={{0,2},{1,3},{2,0},{3,1},{4,6},{5,7},{6,4},{7,5},{8,10},{9,11},{10,... | collective-permute-start | bytes 786440 | tf_op jit(solution)/shard_map/ppermute | solution.py:414
  583.4 43.4 %collective-permute-start.51 = (bf16[64,2048]{1,0:T(8,128)(2,1)}, bf16[64,2048]{1,0:T(8,128)(2,1)}, u32[]{:S(2)}, u32[]{:S(2)}) collective-permute-start(bf16[64,2048]{1,0:T(8,128)(2,1)} %get-tuple-element.167), channel_id=1, source_target_pairs={{0,24},{8,16},{16,8},{24,0},{1,25},{9,17},{17,9},{25,1},{2,26},{10... | collective-permute-start | bytes 786440 | tf_op jit(solution)/shard_map/ppermute | solution.py:409
  585.7 41.2 %collective-permute-start.50 = (bf16[64,2048]{1,0:T(8,128)(2,1)}, bf16[64,2048]{1,0:T(8,128)(2,1)}, u32[]{:S(2)}, u32[]{:S(2)}) collective-permute-start(bf16[64,2048]{1,0:T(8,128)(2,1)} %get-tuple-element.168), channel_id=1, source_target_pairs={{0,16},{8,24},{16,0},{24,8},{1,17},{9,25},{17,1},{25,9},{2,18},{10... | collective-permute-start | bytes 786440 | tf_op jit(solution)/shard_map/ppermute | solution.py:409
  586.6 40.3 %collective-permute-start.49 = (bf16[64,2048]{1,0:T(8,128)(2,1)}, bf16[64,2048]{1,0:T(8,128)(2,1)}, u32[]{:S(2)}, u32[]{:S(2)}) collective-permute-start(bf16[64,2048]{1,0:T(8,128)(2,1)} %get-tuple-element.169), channel_id=1, source_target_pairs={{0,8},{8,0},{16,24},{24,16},{1,9},{9,1},{17,25},{25,17},{2,10},{10... | collective-permute-start | bytes 786440 | tf_op jit(solution)/shard_map/ppermute | solution.py:409
  626.8 135.7 %reduce-scatter.14.cloned.1.call-start = ((), (), s32[]{:S(2)}) async-start(), calls=%async_computation.13 | async-start | bytes 4718592 | tf_op jit(solution)/shard_map/reduce_scatter | solution.py:611
  659.5 22.1 %collective-permute-start.71 = (bf16[64,1536]{1,0:T(8,128)(2,1)S(1)}, bf16[64,1536]{1,0:T(8,128)(2,1)S(1)}, u32[]{:S(2)}, u32[]{:S(2)}) collective-permute-start(bf16[64,1536]{1,0:T(8,128)(2,1)S(1)} %get-tuple-element.193), channel_id=1, source_target_pairs={{0,24},{8,16},{16,8},{24,0},{1,25},{9,17},{17,9},{25,1},{2,26},{10... | collective-permute-start | bytes 589832 | tf_op jit(solution)/shard_map/ppermute | solution.py:409
  660.2 20.6 %collective-permute-start.70 = (bf16[64,1536]{1,0:T(8,128)(2,1)S(1)}, bf16[64,1536]{1,0:T(8,128)(2,1)S(1)}, u32[]{:S(2)}, u32[]{:S(2)}) collective-permute-start(bf16[64,1536]{1,0:T(8,128)(2,1)S(1)} %get-tuple-element.194), channel_id=1, source_target_pairs={{0,16},{8,24},{16,0},{24,8},{1,17},{9,25},{17,1},{25,9},{2,18},{10... | collective-permute-start | bytes 589832 | tf_op jit(solution)/shard_map/ppermute | solution.py:409
  661.9 8.8 %collective-permute-start.69 = (bf16[64,1536]{1,0:T(8,128)(2,1)S(1)}, bf16[64,1536]{1,0:T(8,128)(2,1)S(1)}, u32[]{:S(2)}, u32[]{:S(2)}) collective-permute-start(bf16[64,1536]{1,0:T(8,128)(2,1)S(1)} %get-tuple-element.195), channel_id=1, source_target_pairs={{0,8},{8,0},{16,24},{24,16},{1,9},{9,1},{17,25},{25,17},{2,10},{10... | collective-permute-start | bytes 589832 | tf_op jit(solution)/shard_map/ppermute | solution.py:409
  677.3 26.3 %collective-permute-start.52 = (bf16[256,2048]{1,0:T(8,128)(2,1)}, bf16[256,2048]{1,0:T(8,128)(2,1)}, u32[]{:S(2)}, u32[]{:S(2)}) collective-permute-start(bf16[256,2048]{1,0:T(8,128)(2,1)} %get-tuple-element.133), channel_id=1, source_target_pairs={{0,8},{8,0},{16,24},{24,16},{1,9},{9,1},{17,25},{25,17},{2,10},{10... | collective-permute-start | bytes 3145736 | tf_op jit(solution)/shard_map/ppermute | solution.py:409
  677.8 47.5 %collective-permute-start.54 = (bf16[256,2048]{1,0:T(8,128)(2,1)}, bf16[256,2048]{1,0:T(8,128)(2,1)}, u32[]{:S(2)}, u32[]{:S(2)}) collective-permute-start(bf16[256,2048]{1,0:T(8,128)(2,1)} %get-tuple-element.134), channel_id=1, source_target_pairs={{0,24},{8,16},{16,8},{24,0},{1,25},{9,17},{17,9},{25,1},{2,26},{10... | collective-permute-start | bytes 3145736 | tf_op jit(solution)/shard_map/ppermute | solution.py:409
  680.2 46.5 %collective-permute-start.53 = (bf16[256,2048]{1,0:T(8,128)(2,1)}, bf16[256,2048]{1,0:T(8,128)(2,1)}, u32[]{:S(2)}, u32[]{:S(2)}) collective-permute-start(bf16[256,2048]{1,0:T(8,128)(2,1)} %get-tuple-element.135), channel_id=1, source_target_pairs={{0,16},{8,24},{16,0},{24,8},{1,17},{9,25},{17,1},{25,9},{2,18},{10... | collective-permute-start | bytes 3145736 | tf_op jit(solution)/shard_map/ppermute | solution.py:409
  738.5 18.1 %collective-permute-start.57 = (bf16[64,2048]{1,0:T(8,128)(2,1)S(1)}, bf16[64,2048]{1,0:T(8,128)(2,1)S(1)}, u32[]{:S(2)}, u32[]{:S(2)}) collective-permute-start(bf16[64,2048]{1,0:T(8,128)(2,1)S(1)} %get-tuple-element.158), channel_id=1, source_target_pairs={{0,6},{1,7},{2,4},{3,5},{4,2},{5,3},{6,0},{7,1},{8,14},{9,15},{10,... | collective-permute-start | bytes 786440 | tf_op jit(solution)/shard_map/ppermute | solution.py:414
  738.6 23.8 %collective-permute-start.56 = (bf16[64,2048]{1,0:T(8,128)(2,1)S(1)}, bf16[64,2048]{1,0:T(8,128)(2,1)S(1)}, u32[]{:S(2)}, u32[]{:S(2)}) collective-permute-start(bf16[64,2048]{1,0:T(8,128)(2,1)S(1)} %get-tuple-element.159), channel_id=1, source_target_pairs={{0,4},{1,5},{2,6},{3,7},{4,0},{5,1},{6,2},{7,3},{8,12},{9,13},{10,... | collective-permute-start | bytes 786440 | tf_op jit(solution)/shard_map/ppermute | solution.py:414
  742.2 20.1 %collective-permute-start.55 = (bf16[64,2048]{1,0:T(8,128)(2,1)S(1)}, bf16[64,2048]{1,0:T(8,128)(2,1)S(1)}, u32[]{:S(2)}, u32[]{:S(2)}) collective-permute-start(bf16[64,2048]{1,0:T(8,128)(2,1)S(1)} %get-tuple-element.160), channel_id=1, source_target_pairs={{0,2},{1,3},{2,0},{3,1},{4,6},{5,7},{6,4},{7,5},{8,10},{9,11},{10,... | collective-permute-start | bytes 786440 | tf_op jit(solution)/shard_map/ppermute | solution.py:414
  743.0 13.5 %collective-permute-start.74 = (bf16[64,1536]{1,0:T(8,128)(2,1)S(1)}, bf16[64,1536]{1,0:T(8,128)(2,1)S(1)}, u32[]{:S(2)}, u32[]{:S(2)}) collective-permute-start(bf16[64,1536]{1,0:T(8,128)(2,1)S(1)} %get-tuple-element.190), channel_id=1, source_target_pairs={{0,24},{8,16},{16,8},{24,0},{1,25},{9,17},{17,9},{25,1},{2,26},{10... | collective-permute-start | bytes 589832 | tf_op jit(solution)/shard_map/ppermute | solution.py:409
  763.7 9.6 %collective-permute-start.60 = (bf16[64,1024]{1,0:T(8,128)(2,1)S(1)}, bf16[64,1024]{1,0:T(8,128)(2,1)S(1)}, u32[]{:S(2)}, u32[]{:S(2)}) collective-permute-start(bf16[64,1024]{1,0:T(8,128)(2,1)S(1)} %get-tuple-element.204), channel_id=1, source_target_pairs={{0,24},{8,16},{16,8},{24,0},{1,25},{9,17},{17,9},{25,1},{2,26},{10... | collective-permute-start | bytes 393224 | tf_op jit(solution)/shard_map/ppermute | solution.py:409
  764.1 8.5 %collective-permute-start.59 = (bf16[64,1024]{1,0:T(8,128)(2,1)S(1)}, bf16[64,1024]{1,0:T(8,128)(2,1)S(1)}, u32[]{:S(2)}, u32[]{:S(2)}) collective-permute-start(bf16[64,1024]{1,0:T(8,128)(2,1)S(1)} %get-tuple-element.205), channel_id=1, source_target_pairs={{0,16},{8,24},{16,0},{24,8},{1,17},{9,25},{17,1},{25,9},{2,18},{10... | collective-permute-start | bytes 393224 | tf_op jit(solution)/shard_map/ppermute | solution.py:409
  779.1 14.2 %collective-permute-start.63 = (bf16[64,2048]{1,0:T(8,128)(2,1)S(1)}, bf16[64,2048]{1,0:T(8,128)(2,1)S(1)}, u32[]{:S(2)}, u32[]{:S(2)}) collective-permute-start(bf16[64,2048]{1,0:T(8,128)(2,1)S(1)} %get-tuple-element.154), channel_id=1, source_target_pairs={{0,24},{8,16},{16,8},{24,0},{1,25},{9,17},{17,9},{25,1},{2,26},{10... | collective-permute-start | bytes 786440 | tf_op jit(solution)/shard_map/ppermute | solution.py:409
  781.3 12.1 %collective-permute-start.62 = (bf16[64,2048]{1,0:T(8,128)(2,1)S(1)}, bf16[64,2048]{1,0:T(8,128)(2,1)S(1)}, u32[]{:S(2)}, u32[]{:S(2)}) collective-permute-start(bf16[64,2048]{1,0:T(8,128)(2,1)S(1)} %get-tuple-element.155), channel_id=1, source_target_pairs={{0,16},{8,24},{16,0},{24,8},{1,17},{9,25},{17,1},{25,9},{2,18},{10... | collective-permute-start | bytes 786440 | tf_op jit(solution)/shard_map/ppermute | solution.py:409
  781.7 11.6 %collective-permute-start.61 = (bf16[64,2048]{1,0:T(8,128)(2,1)S(1)}, bf16[64,2048]{1,0:T(8,128)(2,1)S(1)}, u32[]{:S(2)}, u32[]{:S(2)}) collective-permute-start(bf16[64,2048]{1,0:T(8,128)(2,1)S(1)} %get-tuple-element.156), channel_id=1, source_target_pairs={{0,8},{8,0},{16,24},{24,16},{1,9},{9,1},{17,25},{25,17},{2,10},{10... | collective-permute-start | bytes 786440 | tf_op jit(solution)/shard_map/ppermute | solution.py:409
  (66 other events, 1084.0 us)
Sparse Core Ops, SparseCore 0:
  70.6 45.9 all-gather.4
  118.2 27.9 all-gather.6
  155.4 129.8 all-gather.8
  286.8 63.1 all-gather.10
  383.4 67.0 reduce-scatter.5
  458.3 67.0 reduce-scatter.7
  527.6 85.0 reduce-scatter.9
  626.9 35.1 reduce-scatter.11
  664.4 48.5 reduce-scatter.13
